TPU v7x, 128 devices: a whole 4x4x4 slice. The times are simulated.
128 devices in a mesh: lat: 8 (over x_hi, z), lon: 16 (over y, x_lo, core).
Axes of the slice: x: 4 (x_hi: 2, x_lo: 2; x = x_hi * 2 + x_lo), y: 4, z: 4, core: 2. Of those that a mesh axis runs over, the one named last changes fastest.
Arguments:
- obs_rows: bfloat16 [131072, 512], P(('lat', 'lon')), may hold values from -6 to 6
- obs_dest: int32 [131072, 1], P(('lat', 'lon')), may hold values from 0 to 127; in each aligned block of 1024 rows (0 to 1023, 1024 to 2047, ...) at most 16 rows name the same one
- obs_token: int32 [131072], P(('lat', 'lon')), may hold values from 0 to 511
- obs_count: int32 [128], P(('lat', 'lon')), may hold values from 640 to 1024, as said below
- background: bfloat16 [128, 512, 512], P('lat', 'lon'), may hold values from -6 to 6
- w_obs_in: bfloat16 [512, 2048], replicated, may hold values from -0.25 to 0.25
- w_obs_out: bfloat16 [2048, 512], replicated, may hold values from -0.125 to 0.125
- w_qkv: bfloat16 [2, 512, 1536], replicated, may hold values from -2 to 2
- w_proj: bfloat16 [2, 512, 512], replicated, may hold values from -0.25 to 0.25
- w_up: bfloat16 [2, 512, 2048], replicated, may hold values from -0.25 to 0.25
- w_down: bfloat16 [2, 2048, 512], replicated, may hold values from -0.125 to 0.125
- norm_gain: float32 [2, 2, 512], replicated, may hold values from 0.1 to 1.9
Outputs:
- tokens_out: bfloat16 [128, 512, 512], P('lat', 'lon')
Inputs may be any that keep to these rules, and one draw needn't show every extreme that they name: `obs_dest`: of the 1024 rows of one swath owner, live or not, at most 16 name one tile owner, and some swath owner has exactly 16 rows naming one tile owner. The live rows of a swath owner are its first obs_count rows; some swath owner has all 1024 rows live and another has exactly the least count.
All inputs are finite; a program needn't handle non-finite values.
Results may differ from a plain program's by a relative error of at most 0.018.
Values may be sent and summed in bfloat16 or wider, within the bound.
No kernel may reach another device: no remote copies, remote signals or barrier semaphores. Data moves between devices by JAX's collectives and lax.ppermute only.
A program may use at most 64 MiB of HBM per device.

v0:
```python
import functools

import jax
import jax.numpy as jnp
from jax import lax
from jax.experimental import pallas as pl
from jax.experimental.pallas import tpu as pltpu
from jax.sharding import PartitionSpec as P

D = 512
FF = 2048
HEADS = 8
WIN = 16
HALF = 8
CLAT = 16
CLON = 32
CELLS = CLAT * CLON
OBS_DEV = 1024
OWNERS = 128
CAP = 16
LANES = 128
SLAB = 4 * CAP + 8
BLK = 256
EPS = 1e-5
BF = jnp.bfloat16
F32 = jnp.float32
VMEM = pl.BlockSpec(memory_space=pltpu.VMEM)
SMEM = pl.BlockSpec(memory_space=pltpu.SMEM)


def gelu(v):
    c = 0.7978845608028654
    inner = v * (c + (c * 0.044715) * (v * v))
    half = 0.5 * v
    return half + half * jnp.tanh(inner)


def dot(a, b):
    return jnp.dot(a, b, preferred_element_type=F32)


def dot_nt(a, b):
    return lax.dot_general(a, b, (((1,), (1,)), ((), ())), preferred_element_type=F32)


def normed(x, gain):
    mean = jnp.mean(x, -1, keepdims=True)
    centred = x - mean
    var = jnp.mean(centred * centred, -1, keepdims=True)
    return (centred * lax.rsqrt(var + EPS) * gain).astype(BF)


def iota(shape, axis):
    return lax.broadcasted_iota(jnp.int32, shape, axis)


def encode_kernel(place, count, dest, token, rows, w_in, w_out, slab, encoded, slots):
    live_count = count[0]
    lane_base = (place[0] % 8) * CAP
    before = iota((BLK, BLK), 0) < iota((BLK, BLK), 1)
    upper = jnp.where(before, 1.0, 0.0).astype(BF)
    owner_col = iota((OWNERS, BLK), 0)
    lane_col = iota((LANES, BLK), 0)
    carry = jnp.zeros((OWNERS, 1), F32)
    high = jnp.zeros((OWNERS, LANES), F32)
    low = jnp.zeros((OWNERS, LANES), F32)
    for b in range(OBS_DEV // BLK):
        cols = slice(b * BLK, (b + 1) * BLK)
        target = dest[:, cols]
        live = (iota((1, BLK), 1) + b * BLK) < live_count
        hits = jnp.where((owner_col == target) & live, 1.0, 0.0)
        hits_bf = hits.astype(BF)
        earlier = dot(hits_bf, upper) + carry
        carry = carry + jnp.sum(hits, 1, keepdims=True)
        rank = jnp.sum(earlier * hits, 0, keepdims=True).astype(jnp.int32)
        slots[:, cols] = jnp.where(live, target * CAP + rank, -1)
        cell = token[:, cols]
        spread = lane_col == (rank + lane_base)
        row_part = jnp.where(spread, (cell // CLON).astype(F32), 0.0).astype(BF)
        col_part = jnp.where(spread, (cell % CLON + 1).astype(F32), 0.0).astype(BF)
        high = high + dot_nt(hits_bf, row_part)
        low = low + dot_nt(hits_bf, col_part)
    sub = iota((OWNERS, 8, LANES), 1)
    marks = jnp.where(sub == 0, high[:, None, :], jnp.where(sub == 1, low[:, None, :], 0.0))
    slab[:, 4 * CAP : SLAB, :] = marks.astype(BF)

    def encode_block(b, _):
        r = pl.ds(pl.multiple_of(b * BLK, BLK), BLK)
        x = rows[r, :]
        total = jnp.zeros((BLK, D), F32)
        for t in range(FF // 512):
            f = slice(t * 512, (t + 1) * 512)
            hidden = gelu(dot(x, w_in[:, f])).astype(BF)
            total = total + dot(hidden, w_out[f, :])
        encoded[r, :] = total.astype(BF)
        return 0

    lax.fori_loop(0, OBS_DEV // BLK, encode_block, 0)

    def place_block(b, _):
        wanted = iota((BLK, OBS_DEV), 0) + b * BLK
        pick = jnp.where(slots[...] == wanted, 1.0, 0.0).astype(BF)
        moved = dot(pick, encoded[...]).astype(BF).reshape(BLK // CAP, CAP, D)
        d = pl.ds(b * (BLK // CAP), BLK // CAP)
        for k in range(4):
            slab[d, k * CAP : (k + 1) * CAP, :] = moved[:, :, k * LANES : (k + 1) * LANES]
        return 0

    lax.fori_loop(0, OWNERS * CAP // BLK, place_block, 0)


def encode(place, count, dest, token, rows, w_in, w_out):
    return pl.pallas_call(
        encode_kernel,
        out_shape=jax.ShapeDtypeStruct((OWNERS, SLAB, LANES), BF),
        in_specs=[SMEM, SMEM] + [VMEM] * 5,
        out_specs=VMEM,
        scratch_shapes=[pltpu.VMEM((OBS_DEV, D), BF), pltpu.VMEM((1, OBS_DEV), jnp.int32)],
        compiler_params=pltpu.CompilerParams(vmem_limit_bytes=24 << 20),
        cost_estimate=pl.CostEstimate(
            flops=7 << 30, transcendentals=OBS_DEV * FF, bytes_accessed=8 << 20
        ),
        name="encode",
    )(place, count, dest, token, rows, w_in, w_out)


def block_body(x, bias, gain_a, gain_b, w_qkv, w_proj, w_up, w_down, qkv, mixed):
    count = x.shape[0]
    area = WIN * WIN
    qkv[...] = dot(normed(x, gain_a), w_qkv[...]).astype(BF)
    first = iota((area, LANES), 1) < 64
    ones = jnp.ones((area, LANES), BF)
    for w in range(count // area):
        r = slice(w * area, (w + 1) * area)
        for pair in range(HEADS // 2):
            c = pair * LANES
            q = qkv[r, c : c + LANES] * BF(0.125)
            k = qkv[r, D + c : D + c + LANES]
            v = jnp.concatenate([qkv[r, 2 * D + c : 2 * D + c + LANES], ones], 1)
            out = []
            for head in range(2):
                mine = first if head == 0 else jnp.logical_not(first)
                scores = dot_nt(jnp.where(mine, q, BF(0)), k)
                if bias is not None:
                    scores = scores + bias
                probs = jnp.exp(scores - jnp.max(scores, -1, keepdims=True)).astype(BF)
                both = dot(probs, v)
                out.append(both[:, :LANES] / both[:, LANES:])
            mixed[r, c : c + LANES] = jnp.where(first, out[0], out[1]).astype(BF)
    attended = x + dot(mixed[...], w_proj[...])
    h = normed(attended, gain_b)
    total = attended
    for t in range(FF // 512):
        f = slice(t * 512, (t + 1) * 512)
        total = total + dot(gelu(dot(h, w_up[:, f])).astype(BF), w_down[f, :])
    return total.astype(BF)


def bin_kernel(arrived, background, gains, w_qkv, w_proj, w_up, w_down, out, lined, pick, qkv, mixed, state):
    for k in range(4):
        lined[:, k * LANES : (k + 1) * LANES] = arrived[:, k * CAP : (k + 1) * CAP, :].reshape(
            OWNERS * CAP, LANES
        )
    sub = iota((OWNERS, 8, LANES), 1)
    weight = jnp.where(sub == 0, float(CLON), 1.0)
    marks = arrived[:, 4 * CAP : SLAB, :].astype(F32) * weight
    marks = jnp.sum(marks.reshape(OWNERS // 8, 64, LANES), 1).astype(jnp.int32)
    row = iota((CELLS, LANES), 0)
    inner = row % BLK
    cell = (inner // WIN) * CLON + (row // BLK) * WIN + inner % WIN + 1
    tally = jnp.zeros((CELLS, LANES), F32)
    for g in range(OWNERS // 8):
        hit = jnp.where(cell == marks[g : g + 1, :], 1.0, 0.0)
        tally = tally + hit
        pick[:, g * LANES : (g + 1) * LANES] = hit.astype(BF)
    tally = jnp.sum(tally, 1, keepdims=True)
    sums = dot(pick[...], lined[...]) / jnp.maximum(tally, 1.0)
    for w in range(2):
        r = slice(w * BLK, (w + 1) * BLK)
        back = background[:, w * WIN : (w + 1) * WIN, :].astype(F32).reshape(BLK, D)
        state[r, :] = (back + sums[r, :]).astype(BF).astype(F32)
    done = block_body(
        state[...], None, gains[0:1, :], gains[1:2, :], w_qkv, w_proj, w_up, w_down, qkv, mixed
    )
    for w in range(2):
        out[:, w * WIN : (w + 1) * WIN, :] = done[w * BLK : (w + 1) * BLK].reshape(WIN, WIN, D)


BLOCK_SCRATCH = [
    pltpu.VMEM((CELLS, 3 * D), BF),
    pltpu.VMEM((CELLS, D), BF),
    pltpu.VMEM((CELLS, D), F32),
]
BLOCK_COST = pl.CostEstimate(flops=4 << 30, transcendentals=2 << 20, bytes_accessed=8 << 20)


def bin_block(arrived, background, gains, w_qkv, w_proj, w_up, w_down):
    return pl.pallas_call(
        bin_kernel,
        out_shape=jax.ShapeDtypeStruct((CLAT, CLON, D), BF),
        in_specs=[VMEM] * 7,
        out_specs=VMEM,
        scratch_shapes=[
            pltpu.VMEM((OWNERS * CAP, D), BF),
            pltpu.VMEM((CELLS, OWNERS * CAP), BF),
        ]
        + BLOCK_SCRATCH,
        compiler_params=pltpu.CompilerParams(vmem_limit_bytes=28 << 20),
        cost_estimate=BLOCK_COST,
        name="bin_block",
    )(arrived, background, gains, w_qkv, w_proj, w_up, w_down)


def shift_kernel(last, grid, below, right, corner, gains, w_qkv, w_proj, w_up, w_down, out, qkv, mixed, state, bias):
    area = WIN * WIN
    split = (iota((area, area), 0) < area // 2) != (iota((area, area), 1) < area // 2)
    bias[...] = jnp.where(split & (last[0] == 1), -1e30, 0.0)
    top = grid[HALF:, HALF:, :].astype(F32)
    bottom = below[...].astype(F32)
    h = area // 2
    state[0:h, :] = top[:, :WIN, :].reshape(h, D)
    state[h : 2 * h, :] = bottom[:, :WIN, :].reshape(h, D)
    top = jnp.concatenate([top[:, WIN:, :], right[...].astype(F32)], 1)
    bottom = jnp.concatenate([bottom[:, WIN:, :], corner[...].astype(F32)], 1)
    state[2 * h : 3 * h, :] = top.reshape(h, D)
    state[3 * h : 4 * h, :] = bottom.reshape(h, D)
    done = block_body(
        state[...], bias[...], gains[0:1, :], gains[1:2, :], w_qkv, w_proj, w_up, w_down, qkv, mixed
    )
    for w in range(2):
        out[:, w * WIN : (w + 1) * WIN, :] = done[w * BLK : (w + 1) * BLK].reshape(WIN, WIN, D)


def shift_block(last, grid, below, right, corner, gains, w_qkv, w_proj, w_up, w_down):
    return pl.pallas_call(
        shift_kernel,
        out_shape=jax.ShapeDtypeStruct((CLAT, CLON, D), BF),
        in_specs=[SMEM] + [VMEM] * 9,
        out_specs=VMEM,
        scratch_shapes=BLOCK_SCRATCH + [pltpu.VMEM((WIN * WIN, WIN * WIN), F32)],
        compiler_params=pltpu.CompilerParams(vmem_limit_bytes=28 << 20),
        cost_estimate=BLOCK_COST,
        name="shift_block",
    )(last, grid, below, right, corner, gains, w_qkv, w_proj, w_up, w_down)


def moved(block, lat_step, lon_step):
    lat_count = lax.axis_size("lat")
    lon_count = lax.axis_size("lon")
    route = [
        (
            i * lon_count + j,
            (i + lat_step) % lat_count * lon_count + (j + lon_step) % lon_count,
        )
        for i in range(lat_count)
        for j in range(lon_count)
    ]
    return lax.ppermute(block, ("lat", "lon"), route)


def on_device(
    obs_rows,
    obs_dest,
    obs_token,
    obs_count,
    background,
    w_obs_in,
    w_obs_out,
    w_qkv,
    w_proj,
    w_up,
    w_down,
    norm_gain,
):
    lat = lax.axis_index("lat")
    place = (lat * lax.axis_size("lon") + lax.axis_index("lon")).astype(jnp.int32).reshape(1)
    slab = encode(
        place,
        obs_count,
        obs_dest.reshape(1, OBS_DEV),
        obs_token.reshape(1, OBS_DEV),
        obs_rows,
        w_obs_in,
        w_obs_out,
    )
    arrived = lax.all_to_all(slab, ("lat", "lon"), split_axis=0, concat_axis=0, tiled=True)
    grid = bin_block(arrived, background, norm_gain[0], w_qkv[0], w_proj[0], w_up[0], w_down[0])
    below = moved(grid[:HALF, HALF:], -1, 0)
    right = moved(grid[HALF:, :HALF], 0, -1)
    corner = moved(grid[:HALF, :HALF], -1, -1)
    last = (lat == lax.axis_size("lat") - 1).astype(jnp.int32).reshape(1)
    done = shift_block(
        last, grid, below, right, corner, norm_gain[1], w_qkv[1], w_proj[1], w_up[1], w_down[1]
    )
    cut = CLON - HALF
    above = moved(done[HALF:, :cut], 1, 0)
    left = moved(done[:HALF, cut:], 0, 1)
    corner = moved(done[HALF:, cut:], 1, 1)
    top = jnp.concatenate([corner, above], 1)
    bottom = jnp.concatenate([left, done[:HALF, :cut]], 1)
    return jnp.concatenate([top, bottom], 0)


def solution(mesh):
    both = P(("lat", "lon"))
    rows = P(("lat", "lon"), None)
    grid = P("lat", "lon", None)
    return jax.shard_map(
        on_device,
        mesh=mesh,
        in_specs=(rows, rows, both, both, grid) + (P(),) * 7,
        out_specs=grid,
        check_vma=False,
    )
```

profile of v0, /device:TPU:0, one launch (start us, length us, event | category | flops | bytes accessed | tf_op | source)
XLA Modules:
  0.0 110.0 jit_solution(17127889562678858905)
XLA Ops:
  0.7 1.6 %copy-done.9 = bf16[512,2048]{1,0:T(8,128)(2,1)S(1)} copy-done((bf16[512,2048]{1,0:T(8,128)(2,1)S(1)}, bf16[512,2048]{1,0:T(8,128)(2,1)}, u32[]{:S(2)}) %copy-start.9) | copy-done | bytes 2097176
  2.2 1.6 %copy-done.10 = bf16[2048,512]{1,0:T(8,128)(2,1)S(1)} copy-done((bf16[2048,512]{1,0:T(8,128)(2,1)S(1)}, bf16[2048,512]{1,0:T(8,128)(2,1)}, u32[]{:S(2)}) %copy-start.10) | copy-done | bytes 2097176
  3.8 1.2 %copy-done.11 = bf16[1024,512]{1,0:T(8,128)(2,1)S(1)} copy-done((bf16[1024,512]{1,0:T(8,128)(2,1)S(1)}, bf16[1024,512]{1,0:T(8,128)(2,1)}, u32[]{:S(2)}) %copy-start.11) | copy-done | bytes 1048600
  6.4 11.5 %encode.1 = bf16[128,72,128]{2,1,0:T(8,128)(2,1)S(1)} custom-call(s32[1]{0:T(128)} %bitcast.1.place, s32[1]{0:T(128)S(6)} %copy.13.count, s32[1,1024]{1,0:T(1,128)S(1)} %bitcast.24, s32[1,1024]{1,0:T(1,128)S(1)} %bitcast.25, bf16[1024,512]{1,0:T(8,128)(2,1)S(1)} %copy-done.11, bf16[512,2048]{1,0:T(8,128)(2,1)S(1)} %copy-done.9, bf16[2048,512]{1,0:T(8,128)(2,1)S(1)} %copy-done.10), custom_call_target="tpu_custom_call" | custom-call | flops 7516192768 | bytes 8388608 | tf_op jit(solution)/shard_map/encode/pallas_call | solution.py:113
  18.0 1.4 %copy-done = bf16[128,72,128]{2,1,0:T(8,128)(2,1)} copy-done((bf16[128,72,128]{2,1,0:T(8,128)(2,1)}, bf16[128,72,128]{2,1,0:T(8,128)(2,1)S(1)}, u32[]{:S(2)}) %copy-start) | copy-done | bytes 2359320
  19.4 11.2 %all-to-all-start = ((bf16[128,72,128]{2,1,0:T(8,128)(2,1)}), bf16[128,72,128]{2,1,0:T(8,128)(2,1)S(1)}, u32[]{:S(2)}, u32[]{:S(2)}) async-start(bf16[128,72,128]{2,1,0:T(8,128)(2,1)} %copy-done), calls=%async_computation | async-start | bytes 4718592 | tf_op jit(solution)/shard_map/all_to_all | solution.py:286
  30.6 1.3 %slice_bitcast_fusion.6 = (bf16[512,512]{1,0:T(8,128)(2,1)S(1)}, bf16[512,512]{1,0:T(8,128)(2,1)S(1)}) fusion(bf16[2,512,512]{2,1,0:T(8,128)(2,1)} %param.20), kind=kLoop, calls=%fused_computation.7 | loop fusion | bytes 2097152 | tf_op jit(solution)/shard_map/squeeze | solution.py:293
  31.9 4.0 %slice_bitcast_fusion.4 = (bf16[512,1536]{1,0:T(8,128)(2,1)}, bf16[512,1536]{1,0:T(8,128)(2,1)}) fusion(bf16[2,512,1536]{2,1,0:T(8,128)(2,1)} %param.19), kind=kLoop, calls=%fused_computation.4 | loop fusion | bytes 6291456 | tf_op jit(solution)/shard_map/squeeze | solution.py:293
  35.9 2.7 %slice_bitcast_fusion.1 = (bf16[512,2048]{1,0:T(8,128)(2,1)}, bf16[512,2048]{1,0:T(8,128)(2,1)}) fusion(bf16[2,512,2048]{2,1,0:T(8,128)(2,1)S(1)} %copy-done.15), kind=kLoop, calls=%fused_computation.1 | loop fusion | bytes 8388608 | tf_op jit(solution)/shard_map/squeeze | solution.py:293
  39.6 2.3 %slice_bitcast_fusion = (bf16[2048,512]{1,0:T(8,128)(2,1)}, bf16[2048,512]{1,0:T(8,128)(2,1)}) fusion(bf16[2,2048,512]{2,1,0:T(8,128)(2,1)S(1)} %copy-done.16), kind=kLoop, calls=%fused_computation | loop fusion | bytes 8388608 | tf_op jit(solution)/shard_map/squeeze | solution.py:293
  41.9 21.9 %all-to-all-done.arrived = bf16[128,72,128]{2,1,0:T(8,128)(2,1)S(1)} async-done(((bf16[128,72,128]{2,1,0:T(8,128)(2,1)}), bf16[128,72,128]{2,1,0:T(8,128)(2,1)S(1)}, u32[]{:S(2)}, u32[]{:S(2)}) %all-to-all-start) | async-done | bytes 2359328 | tf_op jit(solution)/shard_map/all_to_all | solution.py:286
  63.7 1.6 %copy-done.3 = bf16[512,2048]{1,0:T(8,128)(2,1)S(1)} copy-done((bf16[512,2048]{1,0:T(8,128)(2,1)S(1)}, bf16[512,2048]{1,0:T(8,128)(2,1)}, u32[]{:S(2)}) %copy-start.3) | copy-done | bytes 2097176
  65.3 1.6 %copy-done.4 = bf16[2048,512]{1,0:T(8,128)(2,1)S(1)} copy-done((bf16[2048,512]{1,0:T(8,128)(2,1)S(1)}, bf16[2048,512]{1,0:T(8,128)(2,1)}, u32[]{:S(2)}) %copy-start.4) | copy-done | bytes 2097176
  66.9 1.4 %copy-done.6 = bf16[512,1536]{1,0:T(8,128)(2,1)S(1)} copy-done((bf16[512,1536]{1,0:T(8,128)(2,1)S(1)}, bf16[512,1536]{1,0:T(8,128)(2,1)}, u32[]{:S(2)}) %copy-start.6) | copy-done | bytes 1572888
  68.3 1.0 copy-done.12
  69.4 7.6 %bin_block.1.grid = bf16[16,32,512]{2,1,0:T(8,128)(2,1)S(1)} custom-call(bf16[128,72,128]{2,1,0:T(8,128)(2,1)S(1)} %all-to-all-done.arrived, bf16[16,32,512]{2,1,0:T(8,128)(2,1)S(1)} %copy-done.12, f32[2,512]{1,0:T(2,128)S(1)} %get-tuple-element.20.gains, bf16[512,1536]{1,0:T(8,128)(2,1)S(1)} %copy-done.6, bf16[512,512]{1,0:T(8,128)(2,1)S(1)} %get-tuple-element.12.w_proj, ...), custom_call_target="tpu_custom_call" | custom-call | flops 4294967296 | bytes 8388608 | tf_op jit(solution)/shard_map/bin_block/pallas_call | solution.py:198
  77.0 1.5 %collective-permute-start = (bf16[8,24,512]{2,1,0:T(8,128)(2,1)S(1)}, bf16[8,24,512]{2,1,0:T(8,128)(2,1)S(1)}, u32[]{:S(2)}, u32[]{:S(2)}) collective-permute-start(bf16[8,24,512]{2,1,0:T(8,128)(2,1)S(1)} %slice.68), channel_id=1, source_target_pairs={{0,112},{1,113},{2,114},{3,115},{4,116},{5,117},{6,118},{7,119},{8... | collective-permute-start | bytes 589832 | tf_op jit(solution)/shard_map/ppermute | solution.py:258
  79.3 1.5 %collective-permute-start.1 = (bf16[8,8,512]{2,1,0:T(8,128)(2,1)S(1)}, bf16[8,8,512]{2,1,0:T(8,128)(2,1)S(1)}, u32[]{:S(2)}, u32[]{:S(2)}) collective-permute-start(bf16[8,8,512]{2,1,0:T(8,128)(2,1)S(1)} %get-tuple-element.18), channel_id=1, source_target_pairs={{0,15},{1,0},{2,1},{3,2},{4,3},{5,4},{6,5},{7,6},{8,7},{9,8},{10,9... | collective-permute-start | bytes 196616 | tf_op jit(solution)/shard_map/ppermute | solution.py:258
  80.8 3.5 %collective-permute-done.2.corner = bf16[8,8,512]{2,1,0:T(8,128)(2,1)S(1)} collective-permute-done((bf16[8,8,512]{2,1,0:T(8,128)(2,1)S(1)}, bf16[8,8,512]{2,1,0:T(8,128)(2,1)S(1)}, u32[]{:S(2)}, u32[]{:S(2)}) %collective-permute-start.2) | collective-permute-done | bytes 65568 | tf_op jit(solution)/shard_map/ppermute | solution.py:258
  84.5 1.6 %copy-done.1 = bf16[512,2048]{1,0:T(8,128)(2,1)S(1)} copy-done((bf16[512,2048]{1,0:T(8,128)(2,1)S(1)}, bf16[512,2048]{1,0:T(8,128)(2,1)}, u32[]{:S(2)}) %copy-start.1) | copy-done | bytes 2097176
  86.1 1.6 %copy-done.2 = bf16[2048,512]{1,0:T(8,128)(2,1)S(1)} copy-done((bf16[2048,512]{1,0:T(8,128)(2,1)S(1)}, bf16[2048,512]{1,0:T(8,128)(2,1)}, u32[]{:S(2)}) %copy-start.2) | copy-done | bytes 2097176
  87.7 1.4 %copy-done.5 = bf16[512,1536]{1,0:T(8,128)(2,1)S(1)} copy-done((bf16[512,1536]{1,0:T(8,128)(2,1)S(1)}, bf16[512,1536]{1,0:T(8,128)(2,1)}, u32[]{:S(2)}) %copy-start.5) | copy-done | bytes 1572888
  90.1 6.0 %shift_block.1 = bf16[16,32,512]{2,1,0:T(8,128)(2,1)S(1)} custom-call(s32[1]{0:T(128)} %bitcast.last, bf16[16,32,512]{2,1,0:T(8,128)(2,1)S(1)} %copy-done.8, bf16[8,24,512]{2,1,0:T(8,128)(2,1)S(1)} %collective-permute-done.below, bf16[8,8,512]{2,1,0:T(8,128)(2,1)S(1)} %collective-permute-done.1.right, bf16[8,8,512]{2,1,0:T(8,128)(2,1)S(1)} %collective-permute-done.2.corner, ...), custom_call_target="tpu_custom_call" | custom-call | flops 4294967296 | bytes 8388608 | tf_op jit(solution)/shard_map/shift_block/pallas_call | solution.py:235
  97.7 11.5 %collective-permute-done.3 = bf16[8,8,512]{2,1,0:T(8,128)(2,1)S(1)} collective-permute-done((bf16[8,8,512]{2,1,0:T(8,128)(2,1)S(1)}, bf16[8,8,512]{2,1,0:T(8,128)(2,1)S(1)}, u32[]{:S(2)}, u32[]{:S(2)}) %collective-permute-start.3) | collective-permute-done | bytes 65568 | tf_op jit(solution)/shard_map/ppermute | solution.py:258
  (39 shorter events, 6.8 us)
Async XLA Ops:
  0.7 1.6 %copy-start.9 = (bf16[512,2048]{1,0:T(8,128)(2,1)S(1)}, bf16[512,2048]{1,0:T(8,128)(2,1)}, u32[]{:S(2)}) copy-start(bf16[512,2048]{1,0:T(8,128)(2,1)} %w_in.1) | copy-start | bytes 6291460
  2.2 1.6 %copy-start.10 = (bf16[2048,512]{1,0:T(8,128)(2,1)S(1)}, bf16[2048,512]{1,0:T(8,128)(2,1)}, u32[]{:S(2)}) copy-start(bf16[2048,512]{1,0:T(8,128)(2,1)} %w_out.1) | copy-start | bytes 6291460
  3.8 1.2 %copy-start.11 = (bf16[1024,512]{1,0:T(8,128)(2,1)S(1)}, bf16[1024,512]{1,0:T(8,128)(2,1)}, u32[]{:S(2)}) copy-start(bf16[1024,512]{1,0:T(8,128)(2,1)} %rows.1) | copy-start | bytes 3145732
  5.1 0.7 copy-start.13
  18.0 1.4 %copy-start = (bf16[128,72,128]{2,1,0:T(8,128)(2,1)}, bf16[128,72,128]{2,1,0:T(8,128)(2,1)S(1)}, u32[]{:S(2)}) copy-start(bf16[128,72,128]{2,1,0:T(8,128)(2,1)S(1)} %encode.1) | copy-start | bytes 7077892
  19.4 11.2 %copy-start.17 = (f32[2,2,512]{2,1,0:T(2,128)S(1)}, f32[2,2,512]{2,1,0:T(2,128)}, u32[]{:S(2)}) copy-start(f32[2,2,512]{2,1,0:T(2,128)} %param.23) | copy-start | bytes 24580
  19.4 44.3 %all-to-all-start = ((bf16[128,72,128]{2,1,0:T(8,128)(2,1)}), bf16[128,72,128]{2,1,0:T(8,128)(2,1)S(1)}, u32[]{:S(2)}, u32[]{:S(2)}) async-start(bf16[128,72,128]{2,1,0:T(8,128)(2,1)} %copy-done), calls=%async_computation | async-start | bytes 4718592 | tf_op jit(solution)/shard_map/all_to_all | solution.py:286
  31.9 4.0 %copy-start.15 = (bf16[2,512,2048]{2,1,0:T(8,128)(2,1)S(1)}, bf16[2,512,2048]{2,1,0:T(8,128)(2,1)}, u32[]{:S(2)}) copy-start(bf16[2,512,2048]{2,1,0:T(8,128)(2,1)} %param.21) | copy-start | bytes 12582916
  35.9 3.7 %copy-start.16 = (bf16[2,2048,512]{2,1,0:T(8,128)(2,1)S(1)}, bf16[2,2048,512]{2,1,0:T(8,128)(2,1)}, u32[]{:S(2)}) copy-start(bf16[2,2048,512]{2,1,0:T(8,128)(2,1)} %param.22) | copy-start | bytes 12582916
  63.7 1.6 %copy-start.3 = (bf16[512,2048]{1,0:T(8,128)(2,1)S(1)}, bf16[512,2048]{1,0:T(8,128)(2,1)}, u32[]{:S(2)}) copy-start(bf16[512,2048]{1,0:T(8,128)(2,1)} %get-tuple-element.8.w_up) | copy-start | bytes 6291460
  65.3 1.6 %copy-start.4 = (bf16[2048,512]{1,0:T(8,128)(2,1)S(1)}, bf16[2048,512]{1,0:T(8,128)(2,1)}, u32[]{:S(2)}) copy-start(bf16[2048,512]{1,0:T(8,128)(2,1)} %get-tuple-element.6.w_down) | copy-start | bytes 6291460
  66.9 1.4 %copy-start.6 = (bf16[512,1536]{1,0:T(8,128)(2,1)S(1)}, bf16[512,1536]{1,0:T(8,128)(2,1)}, u32[]{:S(2)}) copy-start(bf16[512,1536]{1,0:T(8,128)(2,1)} %get-tuple-element.10.w_qkv) | copy-start | bytes 4718596
  68.3 1.0 copy-start.12
  77.0 7.5 %collective-permute-start = (bf16[8,24,512]{2,1,0:T(8,128)(2,1)S(1)}, bf16[8,24,512]{2,1,0:T(8,128)(2,1)S(1)}, u32[]{:S(2)}, u32[]{:S(2)}) collective-permute-start(bf16[8,24,512]{2,1,0:T(8,128)(2,1)S(1)} %slice.68), channel_id=1, source_target_pairs={{0,112},{1,113},{2,114},{3,115},{4,116},{5,117},{6,118},{7,119},{8... | collective-permute-start | bytes 589832 | tf_op jit(solution)/shard_map/ppermute | solution.py:258
  78.5 0.8 copy-start.7
  79.3 5.1 %collective-permute-start.2 = (bf16[8,8,512]{2,1,0:T(8,128)(2,1)S(1)}, bf16[8,8,512]{2,1,0:T(8,128)(2,1)S(1)}, u32[]{:S(2)}, u32[]{:S(2)}) collective-permute-start(bf16[8,8,512]{2,1,0:T(8,128)(2,1)S(1)} %get-tuple-element.17), channel_id=1, source_target_pairs={{0,127},{1,112},{2,113},{3,114},{4,115},{5,116},{6,117},{7,118},{8... | collective-permute-start | bytes 196616 | tf_op jit(solution)/shard_map/ppermute | solution.py:258
  79.3 5.1 %collective-permute-start.1 = (bf16[8,8,512]{2,1,0:T(8,128)(2,1)S(1)}, bf16[8,8,512]{2,1,0:T(8,128)(2,1)S(1)}, u32[]{:S(2)}, u32[]{:S(2)}) collective-permute-start(bf16[8,8,512]{2,1,0:T(8,128)(2,1)S(1)} %get-tuple-element.18), channel_id=1, source_target_pairs={{0,15},{1,0},{2,1},{3,2},{4,3},{5,4},{6,5},{7,6},{8,7},{9,8},{10,9... | collective-permute-start | bytes 196616 | tf_op jit(solution)/shard_map/ppermute | solution.py:258
  84.5 1.6 %copy-start.1 = (bf16[512,2048]{1,0:T(8,128)(2,1)S(1)}, bf16[512,2048]{1,0:T(8,128)(2,1)}, u32[]{:S(2)}) copy-start(bf16[512,2048]{1,0:T(8,128)(2,1)} %get-tuple-element.7.w_up) | copy-start | bytes 6291460
  86.1 1.6 %copy-start.2 = (bf16[2048,512]{1,0:T(8,128)(2,1)S(1)}, bf16[2048,512]{1,0:T(8,128)(2,1)}, u32[]{:S(2)}) copy-start(bf16[2048,512]{1,0:T(8,128)(2,1)} %get-tuple-element.5.w_down) | copy-start | bytes 6291460
  87.7 1.4 %copy-start.5 = (bf16[512,1536]{1,0:T(8,128)(2,1)S(1)}, bf16[512,1536]{1,0:T(8,128)(2,1)}, u32[]{:S(2)}) copy-start(bf16[512,1536]{1,0:T(8,128)(2,1)} %get-tuple-element.9.w_qkv) | copy-start | bytes 4718596
  89.1 1.0 copy-start.8
  96.2 13.0 %collective-permute-start.4 = (bf16[8,24,512]{2,1,0:T(8,128)(2,1)S(1)}, bf16[8,24,512]{2,1,0:T(8,128)(2,1)S(1)}, u32[]{:S(2)}, u32[]{:S(2)}) collective-permute-start(bf16[8,24,512]{2,1,0:T(8,128)(2,1)S(1)} %get-tuple-element.15), channel_id=1, source_target_pairs={{0,16},{1,17},{2,18},{3,19},{4,20},{5,21},{6,22},{7,23},{8,24},{9,... | collective-permute-start | bytes 589832 | tf_op jit(solution)/shard_map/ppermute | solution.py:258
  96.3 12.9 %collective-permute-start.3 = (bf16[8,8,512]{2,1,0:T(8,128)(2,1)S(1)}, bf16[8,8,512]{2,1,0:T(8,128)(2,1)S(1)}, u32[]{:S(2)}, u32[]{:S(2)}) collective-permute-start(bf16[8,8,512]{2,1,0:T(8,128)(2,1)S(1)} %get-tuple-element.13), channel_id=1, source_target_pairs={{0,17},{1,18},{2,19},{3,20},{4,21},{5,22},{6,23},{7,24},{8,25},{9,... | collective-permute-start | bytes 196616 | tf_op jit(solution)/shard_map/ppermute | solution.py:258
  96.9 12.3 %collective-permute-start.5 = (bf16[8,8,512]{2,1,0:T(8,128)(2,1)S(1)}, bf16[8,8,512]{2,1,0:T(8,128)(2,1)S(1)}, u32[]{:S(2)}, u32[]{:S(2)}) collective-permute-start(bf16[8,8,512]{2,1,0:T(8,128)(2,1)S(1)} %get-tuple-element.14), channel_id=1, source_target_pairs={{0,1},{1,2},{2,3},{3,4},{4,5},{5,6},{6,7},{7,8},{8,9},{9,10},{10,1... | collective-permute-start | bytes 196616 | tf_op jit(solution)/shard_map/ppermute | solution.py:258
  (1 other events, 0.7 us)
where the time goes:
time: 111 us; the launch traced here: 110 us
  waiting for transfers between devices  37 us (33%)
  local copies, waits for them, and re-layouts  30.5 us (27%)
  Pallas kernels  25.1 us (23%)
  starting transfers between devices  15.7 us (14%)
    all_to_all x1, waiting for transfers between devices, on_device(): lax.all_to_all(slab, ('lat', 'lon'), split_axis=0, concat_axis=0, tiled=T...  21.9 us
    unnamed x36, local copies, waits for them, and re-layouts  20.3 us
    ppermute x6, waiting for transfers between devices, moved(): return lax.ppermute(block, ('lat', 'lon'), route)  15.2 us
    pallas_call x1, Pallas kernels, encode(): pl.pallas_call(encode_kernel, out_shape=jax.ShapeDtypeStruct((OWNERS, SLA...  11.5 us
    all_to_all x1, starting transfers between devices, on_device(): lax.all_to_all(slab, ('lat', 'lon'), split_axis=0, concat_axis=0, tiled=T...  11.2 us
    pallas_call x1, Pallas kernels, bin_block(): pl.pallas_call(bin_kernel, out_shape=jax.ShapeDtypeStruct((CLAT, CLON, D)...  7.58 us
    pallas_call x1, Pallas kernels, shift_block(): pl.pallas_call(shift_kernel, out_shape=jax.ShapeDtypeStruct((CLAT, CLON,...  5.98 us
    ppermute x6, starting transfers between devices, moved(): return lax.ppermute(block, ('lat', 'lon'), route)  4.51 us
  transfers between devices with their start and end apart: 7, of which 4 were waited for; matrix products, arithmetic and copies ran while one was open for 9% of the time, Pallas kernels for 0%

commit v1 on v0

--- a/solution.py
+++ b/solution.py
@@ -1,5 +1,3 @@
-import functools
-
 import jax
 import jax.numpy as jnp
 from jax import lax
@@ -21,10 +19,15 @@
 LANES = 128
 SLAB = 4 * CAP + 8
 BLK = 256
+TILE = 512
 EPS = 1e-5
+ENCODE_VMEM = 67043328 - (100 << 10)
+BIN_VMEM = 67043328 - (3000 << 10)
+SHIFT_VMEM = 67043328 - (1100 << 10)
 BF = jnp.bfloat16
 F32 = jnp.float32
 VMEM = pl.BlockSpec(memory_space=pltpu.VMEM)
+HBM = pl.BlockSpec(memory_space=pltpu.HBM)
 SMEM = pl.BlockSpec(memory_space=pltpu.SMEM)
 
 
@@ -54,7 +57,25 @@
     return lax.broadcasted_iota(jnp.int32, shape, axis)
 
 
-def encode_kernel(place, count, dest, token, rows, w_in, w_out, slab, encoded, slots):
+def encode_kernel(
+    place, count, dest, token, rows_hbm, w_in_hbm, w_out_hbm, slab_hbm,
+    rows, w_in, w_out, slab, encoded, slots, in_sems, out_sems,
+):
+    tiles = FF // TILE
+    rows_copy = pltpu.make_async_copy(rows_hbm, rows, in_sems.at[2 * tiles])
+    w_in_copies = []
+    w_out_copies = []
+    for t in range(tiles):
+        f = slice(t * TILE, (t + 1) * TILE)
+        w_in_copies.append(pltpu.make_async_copy(w_in_hbm.at[:, f], w_in.at[:, f], in_sems.at[t]))
+        w_out_copies.append(
+            pltpu.make_async_copy(w_out_hbm.at[f, :], w_out.at[f, :], in_sems.at[tiles + t])
+        )
+    rows_copy.start()
+    for t in range(tiles):
+        w_in_copies[t].start()
+        w_out_copies[t].start()
+
     live_count = count[0]
     lane_base = (place[0] % 8) * CAP
     before = iota((BLK, BLK), 0) < iota((BLK, BLK), 1)
@@ -83,40 +104,64 @@
     sub = iota((OWNERS, 8, LANES), 1)
     marks = jnp.where(sub == 0, high[:, None, :], jnp.where(sub == 1, low[:, None, :], 0.0))
     slab[:, 4 * CAP : SLAB, :] = marks.astype(BF)
+    rows_copy.wait()
 
     def encode_block(b, _):
         r = pl.ds(pl.multiple_of(b * BLK, BLK), BLK)
         x = rows[r, :]
         total = jnp.zeros((BLK, D), F32)
-        for t in range(FF // 512):
-            f = slice(t * 512, (t + 1) * 512)
+        for t in range(tiles):
+
+            @pl.when(b == 0)
+            def _():
+                w_in_copies[t].wait()
+                w_out_copies[t].wait()
+
+            f = slice(t * TILE, (t + 1) * TILE)
             hidden = gelu(dot(x, w_in[:, f])).astype(BF)
             total = total + dot(hidden, w_out[f, :])
         encoded[r, :] = total.astype(BF)
         return 0
 
     lax.fori_loop(0, OBS_DEV // BLK, encode_block, 0)
+    step = BLK // CAP
+
+    def slab_copy(b):
+        d = pl.ds(b * step, step)
+        return pltpu.make_async_copy(slab.at[d], slab_hbm.at[d], out_sems.at[b])
 
     def place_block(b, _):
         wanted = iota((BLK, OBS_DEV), 0) + b * BLK
         pick = jnp.where(slots[...] == wanted, 1.0, 0.0).astype(BF)
-        moved = dot(pick, encoded[...]).astype(BF).reshape(BLK // CAP, CAP, D)
-        d = pl.ds(b * (BLK // CAP), BLK // CAP)
+        moved = dot(pick, encoded[...]).astype(BF).reshape(step, CAP, D)
+        d = pl.ds(b * step, step)
         for k in range(4):
             slab[d, k * CAP : (k + 1) * CAP, :] = moved[:, :, k * LANES : (k + 1) * LANES]
+        slab_copy(b).start()
         return 0
 
-    lax.fori_loop(0, OWNERS * CAP // BLK, place_block, 0)
+    lax.fori_loop(0, OWNERS // step, place_block, 0)
+    for b in range(OWNERS // step):
+        slab_copy(b).wait()
 
 
 def encode(place, count, dest, token, rows, w_in, w_out):
     return pl.pallas_call(
         encode_kernel,
         out_shape=jax.ShapeDtypeStruct((OWNERS, SLAB, LANES), BF),
-        in_specs=[SMEM, SMEM] + [VMEM] * 5,
-        out_specs=VMEM,
-        scratch_shapes=[pltpu.VMEM((OBS_DEV, D), BF), pltpu.VMEM((1, OBS_DEV), jnp.int32)],
-        compiler_params=pltpu.CompilerParams(vmem_limit_bytes=24 << 20),
+        in_specs=[SMEM, SMEM, VMEM, VMEM, HBM, HBM, HBM],
+        out_specs=HBM,
+        scratch_shapes=[
+            pltpu.VMEM((OBS_DEV, D), BF),
+            pltpu.VMEM((D, FF), BF),
+            pltpu.VMEM((FF, D), BF),
+            pltpu.VMEM((OWNERS, SLAB, LANES), BF),
+            pltpu.VMEM((OBS_DEV, D), BF),
+            pltpu.VMEM((1, OBS_DEV), jnp.int32),
+            pltpu.SemaphoreType.DMA((2 * FF // TILE + 1,)),
+            pltpu.SemaphoreType.DMA((OWNERS * CAP // BLK,)),
+        ],
+        compiler_params=pltpu.CompilerParams(vmem_limit_bytes=ENCODE_VMEM),
         cost_estimate=pl.CostEstimate(
             flops=7 << 30, transcendentals=OBS_DEV * FF, bytes_accessed=8 << 20
         ),
@@ -124,10 +169,27 @@
     )(place, count, dest, token, rows, w_in, w_out)
 
 
-def block_body(x, bias, gain_a, gain_b, w_qkv, w_proj, w_up, w_down, qkv, mixed):
+def weight_copies(layer, hbm, vmem, sems):
+    w_qkv, w_proj, w_up, w_down = hbm
+    v_qkv, v_proj, v_up, v_down = vmem
+    pairs = [(w_qkv.at[layer], v_qkv), (w_proj.at[layer], v_proj)]
+    for t in range(FF // TILE):
+        f = slice(t * TILE, (t + 1) * TILE)
+        pairs.append((w_up.at[layer, :, f], v_up.at[:, f]))
+        pairs.append((w_down.at[layer, f, :], v_down.at[f, :]))
+    copies = [pltpu.make_async_copy(a, b, sems.at[i]) for i, (a, b) in enumerate(pairs)]
+    for copy in copies:
+        copy.start()
+    return copies
+
+
+def block_body(x, bias, gain_a, gain_b, weights, copies, qkv, mixed):
+    w_qkv, w_proj, w_up, w_down = weights
     count = x.shape[0]
     area = WIN * WIN
-    qkv[...] = dot(normed(x, gain_a), w_qkv[...]).astype(BF)
+    h = normed(x, gain_a)
+    copies[0].wait()
+    qkv[...] = dot(h, w_qkv[...]).astype(BF)
     first = iota((area, LANES), 1) < 64
     ones = jnp.ones((area, LANES), BF)
     for w in range(count // area):
@@ -147,16 +209,25 @@
                 both = dot(probs, v)
                 out.append(both[:, :LANES] / both[:, LANES:])
             mixed[r, c : c + LANES] = jnp.where(first, out[0], out[1]).astype(BF)
+    copies[1].wait()
     attended = x + dot(mixed[...], w_proj[...])
     h = normed(attended, gain_b)
     total = attended
-    for t in range(FF // 512):
-        f = slice(t * 512, (t + 1) * 512)
+    for t in range(FF // TILE):
+        copies[2 + 2 * t].wait()
+        copies[3 + 2 * t].wait()
+        f = slice(t * TILE, (t + 1) * TILE)
         total = total + dot(gelu(dot(h, w_up[:, f])).astype(BF), w_down[f, :])
     return total.astype(BF)
 
 
-def bin_kernel(arrived, background, gains, w_qkv, w_proj, w_up, w_down, out, lined, pick, qkv, mixed, state):
+def bin_kernel(
+    arrived, background_hbm, gains, wq, wp, wu, wd, keep, below, right, corner,
+    lined, pick, background, vq, vp, vu, vd, qkv, mixed, state, sems, back_sem,
+):
+    back_copy = pltpu.make_async_copy(background_hbm, background, back_sem.at[0])
+    back_copy.start()
+    copies = weight_copies(0, (wq, wp, wu, wd), (vq, vp, vu, vd), sems)
     for k in range(4):
         lined[:, k * LANES : (k + 1) * LANES] = arrived[:, k * CAP : (k + 1) * CAP, :].reshape(
             OWNERS * CAP, LANES
@@ -175,47 +246,74 @@
         pick[:, g * LANES : (g + 1) * LANES] = hit.astype(BF)
     tally = jnp.sum(tally, 1, keepdims=True)
     sums = dot(pick[...], lined[...]) / jnp.maximum(tally, 1.0)
+    back_copy.wait()
     for w in range(2):
         r = slice(w * BLK, (w + 1) * BLK)
         back = background[:, w * WIN : (w + 1) * WIN, :].astype(F32).reshape(BLK, D)
         state[r, :] = (back + sums[r, :]).astype(BF).astype(F32)
     done = block_body(
-        state[...], None, gains[0:1, :], gains[1:2, :], w_qkv, w_proj, w_up, w_down, qkv, mixed
+        state[...], None, gains[0, 0:1, :], gains[0, 1:2, :], (vq, vp, vu, vd), copies, qkv, mixed
     )
-    for w in range(2):
-        out[:, w * WIN : (w + 1) * WIN, :] = done[w * BLK : (w + 1) * BLK].reshape(WIN, WIN, D)
-
-
+    one = done[:BLK].reshape(WIN, WIN, D)
+    two = done[BLK:].reshape(WIN, WIN, D)
+    corner[...] = one[:HALF, :HALF]
+    right[...] = one[HALF:, :HALF]
+    below[:, :HALF, :] = one[:HALF, HALF:]
+    below[:, HALF:, :] = two[:HALF]
+    keep[:, :HALF, :] = one[HALF:, HALF:]
+    keep[:, HALF:, :] = two[HALF:]
+
+
+WEIGHT_SCRATCH = [
+    pltpu.VMEM((D, 3 * D), BF),
+    pltpu.VMEM((D, D), BF),
+    pltpu.VMEM((D, FF), BF),
+    pltpu.VMEM((FF, D), BF),
+]
 BLOCK_SCRATCH = [
     pltpu.VMEM((CELLS, 3 * D), BF),
     pltpu.VMEM((CELLS, D), BF),
     pltpu.VMEM((CELLS, D), F32),
 ]
+WEIGHT_SEMS = pltpu.SemaphoreType.DMA((2 + 2 * FF // TILE,))
 BLOCK_COST = pl.CostEstimate(flops=4 << 30, transcendentals=2 << 20, bytes_accessed=8 << 20)
-
-
-def bin_block(arrived, background, gains, w_qkv, w_proj, w_up, w_down):
+PIECES = (
+    jax.ShapeDtypeStruct((HALF, CLON - HALF, D), BF),
+    jax.ShapeDtypeStruct((HALF, CLON - HALF, D), BF),
+    jax.ShapeDtypeStruct((HALF, HALF, D), BF),
+    jax.ShapeDtypeStruct((HALF, HALF, D), BF),
+)
+
+
+def bin_block(arrived, background, gains, *weights):
     return pl.pallas_call(
         bin_kernel,
-        out_shape=jax.ShapeDtypeStruct((CLAT, CLON, D), BF),
-        in_specs=[VMEM] * 7,
-        out_specs=VMEM,
+        out_shape=PIECES,
+        in_specs=[VMEM, HBM, VMEM] + [HBM] * 4,
+        out_specs=[VMEM] * 4,
         scratch_shapes=[
             pltpu.VMEM((OWNERS * CAP, D), BF),
             pltpu.VMEM((CELLS, OWNERS * CAP), BF),
+            pltpu.VMEM((CLAT, CLON, D), BF),
         ]
-        + BLOCK_SCRATCH,
-        compiler_params=pltpu.CompilerParams(vmem_limit_bytes=28 << 20),
+        + WEIGHT_SCRATCH
+        + BLOCK_SCRATCH
+        + [WEIGHT_SEMS, pltpu.SemaphoreType.DMA((1,))],
+        compiler_params=pltpu.CompilerParams(vmem_limit_bytes=BIN_VMEM),
         cost_estimate=BLOCK_COST,
         name="bin_block",
-    )(arrived, background, gains, w_qkv, w_proj, w_up, w_down)
-
-
-def shift_kernel(last, grid, below, right, corner, gains, w_qkv, w_proj, w_up, w_down, out, qkv, mixed, state, bias):
+    )(arrived, background, gains, *weights)
+
+
+def shift_kernel(
+    last, mine, below, right, corner, gains, wq, wp, wu, wd, keep, above, left, diagonal,
+    vq, vp, vu, vd, qkv, mixed, state, bias, sems,
+):
+    copies = weight_copies(1, (wq, wp, wu, wd), (vq, vp, vu, vd), sems)
     area = WIN * WIN
     split = (iota((area, area), 0) < area // 2) != (iota((area, area), 1) < area // 2)
     bias[...] = jnp.where(split & (last[0] == 1), -1e30, 0.0)
-    top = grid[HALF:, HALF:, :].astype(F32)
+    top = mine[...].astype(F32)
     bottom = below[...].astype(F32)
     h = area // 2
     state[0:h, :] = top[:, :WIN, :].reshape(h, D)
@@ -225,23 +323,31 @@
     state[2 * h : 3 * h, :] = top.reshape(h, D)
     state[3 * h : 4 * h, :] = bottom.reshape(h, D)
     done = block_body(
-        state[...], bias[...], gains[0:1, :], gains[1:2, :], w_qkv, w_proj, w_up, w_down, qkv, mixed
+        state[...], bias[...], gains[1, 0:1, :], gains[1, 1:2, :], (vq, vp, vu, vd), copies, qkv, mixed
     )
-    for w in range(2):
-        out[:, w * WIN : (w + 1) * WIN, :] = done[w * BLK : (w + 1) * BLK].reshape(WIN, WIN, D)
-
-
-def shift_block(last, grid, below, right, corner, gains, w_qkv, w_proj, w_up, w_down):
+    one = done[:BLK].reshape(WIN, WIN, D)
+    two = done[BLK:].reshape(WIN, WIN, D)
+    diagonal[...] = two[HALF:, HALF:]
+    left[...] = two[:HALF, HALF:]
+    above[:, :WIN, :] = one[HALF:]
+    above[:, WIN:, :] = two[HALF:, :HALF]
+    keep[:, :WIN, :] = one[:HALF]
+    keep[:, WIN:, :] = two[:HALF, :HALF]
+
+
+def shift_block(last, mine, below, right, corner, gains, *weights):
     return pl.pallas_call(
         shift_kernel,
-        out_shape=jax.ShapeDtypeStruct((CLAT, CLON, D), BF),
-        in_specs=[SMEM] + [VMEM] * 9,
-        out_specs=VMEM,
-        scratch_shapes=BLOCK_SCRATCH + [pltpu.VMEM((WIN * WIN, WIN * WIN), F32)],
-        compiler_params=pltpu.CompilerParams(vmem_limit_bytes=28 << 20),
+        out_shape=PIECES,
+        in_specs=[SMEM] + [VMEM] * 5 + [HBM] * 4,
+        out_specs=[VMEM] * 4,
+        scratch_shapes=WEIGHT_SCRATCH
+        + BLOCK_SCRATCH
+        + [pltpu.VMEM((WIN * WIN, WIN * WIN), F32), WEIGHT_SEMS],
+        compiler_params=pltpu.CompilerParams(vmem_limit_bytes=SHIFT_VMEM),
         cost_estimate=BLOCK_COST,
         name="shift_block",
-    )(last, grid, below, right, corner, gains, w_qkv, w_proj, w_up, w_down)
+    )(last, mine, below, right, corner, gains, *weights)
 
 
 def moved(block, lat_step, lon_step):
@@ -284,20 +390,20 @@
         w_obs_out,
     )
     arrived = lax.all_to_all(slab, ("lat", "lon"), split_axis=0, concat_axis=0, tiled=True)
-    grid = bin_block(arrived, background, norm_gain[0], w_qkv[0], w_proj[0], w_up[0], w_down[0])
-    below = moved(grid[:HALF, HALF:], -1, 0)
-    right = moved(grid[HALF:, :HALF], 0, -1)
-    corner = moved(grid[:HALF, :HALF], -1, -1)
+    weights = (w_qkv, w_proj, w_up, w_down)
+    mine, below, right, corner = bin_block(arrived, background, norm_gain, *weights)
+    below = moved(below, -1, 0)
+    right = moved(right, 0, -1)
+    corner = moved(corner, -1, -1)
     last = (lat == lax.axis_size("lat") - 1).astype(jnp.int32).reshape(1)
-    done = shift_block(
-        last, grid, below, right, corner, norm_gain[1], w_qkv[1], w_proj[1], w_up[1], w_down[1]
+    mine, above, left, corner = shift_block(
+        last, mine, below, right, corner, norm_gain, *weights
     )
-    cut = CLON - HALF
-    above = moved(done[HALF:, :cut], 1, 0)
-    left = moved(done[:HALF, cut:], 0, 1)
-    corner = moved(done[HALF:, cut:], 1, 1)
+    above = moved(above, 1, 0)
+    left = moved(left, 0, 1)
+    corner = moved(corner, 1, 1)
     top = jnp.concatenate([corner, above], 1)
-    bottom = jnp.concatenate([left, done[:HALF, :cut]], 1)
+    bottom = jnp.concatenate([left, mine], 1)
     return jnp.concatenate([top, bottom], 0)
 
 

time: 111 us -> 106 us (0.955)
  blocking collectives: 0 us -> 44.5 us
  local copies, waits for them, and re-layouts: 30.5 us -> 0.68 us
  waiting for transfers between devices: 37 us -> 17 us
  starting transfers between devices: 15.7 us -> 3.98 us
  Pallas kernels: 25.1 us -> 36.7 us
    all_to_all x0 -> x1, blocking collectives: none -> 44.5 us  [on_device(): lax.all_to_all(slab, ('lat', 'lon'), split_axis=0, concat_axis=0, tiled=T...]
    all_to_all x1 -> x0, waiting for transfers between devices: 21.9 us -> none  [on_device(): lax.all_to_all(slab, ('lat', 'lon'), split_axis=0, concat_axis=0, tiled=T...]
    unnamed x36 -> x6, local copies, waits for them, and re-layouts: 20.3 us -> 0.68 us
    all_to_all x1 -> x0, starting transfers between devices: 11.2 us -> none  [on_device(): lax.all_to_all(slab, ('lat', 'lon'), split_axis=0, concat_axis=0, tiled=T...]
    squeeze x5 -> x0, local copies, waits for them, and re-layouts: 10.2 us -> none  [the longest x1 3.99 us: on_device(): w_qkv[1]]
    pallas_call x2, Pallas kernels: 13.6 us -> 21.6 us  [the longest x1 12.1 us: bin_block(): pl.pallas_call(bin_kernel, out_shape=PIECES, in_specs=[VMEM, HBM, VMEM] +...]
    pallas_call x1, Pallas kernels: 11.5 us -> 15.1 us  [encode(): pl.pallas_call(encode_kernel, out_shape=jax.ShapeDtypeStruct((OWNERS, SLA...]
    ppermute x6, waiting for transfers between devices: 15.2 us -> 17 us  [moved(): return lax.ppermute(block, ('lat', 'lon'), route)]
  transfers between devices with their start and end apart: 7 -> 6, of which waited for: 4 -> 4; matrix products, arithmetic and copies ran while one was open for 9% -> 0% of each run, Pallas kernels for 0% -> 0%
where the time goes in v1:
time: 106 us; the launch traced here: 105 us
  blocking collectives  44.5 us (42%)
  Pallas kernels  36.7 us (35%)
  waiting for transfers between devices  17 us (16%)
  starting transfers between devices  3.98 us (4%)
  other arithmetic  1.78 us (2%)
    all_to_all x1, blocking collectives, on_device(): lax.all_to_all(slab, ('lat', 'lon'), split_axis=0, concat_axis=0, tiled=T...  44.5 us
    ppermute x6, waiting for transfers between devices, moved(): return lax.ppermute(block, ('lat', 'lon'), route)  17 us
    pallas_call x1, Pallas kernels, encode(): pl.pallas_call(encode_kernel, out_shape=jax.ShapeDtypeStruct((OWNERS, SLA...  15.1 us
    pallas_call x1, Pallas kernels, bin_block(): pl.pallas_call(bin_kernel, out_shape=PIECES, in_specs=[VMEM, HBM, VMEM] +...  12.1 us
    pallas_call x1, Pallas kernels, shift_block(): pl.pallas_call(shift_kernel, out_shape=PIECES, in_specs=[SMEM] + [VMEM] *...  9.55 us
    ppermute x6, starting transfers between devices, moved(): return lax.ppermute(block, ('lat', 'lon'), route)  3.98 us
  transfers between devices with their start and end apart: 6, of which 4 were waited for; matrix products, arithmetic and copies ran while one was open for 0% of the time, Pallas kernels for 0%

profile of v1, /device:TPU:0, one launch (start us, length us, event | category | flops | bytes accessed | tf_op | source)
XLA Modules:
  0.0 105.3 jit_solution(48390667284158845)
XLA Ops:
  0.7 15.1 %encode.1 = bf16[128,72,128]{2,1,0:T(8,128)(2,1)} custom-call(s32[1]{0:T(128)} %bitcast.1.place, s32[1]{0:T(128)S(6)} %copy.13.count, s32[1,1024]{1,0:T(1,128)} %bitcast.4, s32[1,1024]{1,0:T(1,128)} %bitcast.5, bf16[1024,512]{1,0:T(8,128)(2,1)} %rows_hbm.1, bf16[512,2048]{1,0:T(8,128)(2,1)} %w_in_hbm.1, bf16[2048,512]{1,0:T(8,128)(2,1)} %w_out_hbm.1), custom_call_target="tpu_custom_call" | custom-call | flops 7516192768 | bytes 8388608 | tf_op jit(solution)/shard_map/encode/pallas_call | solution.py:149
  15.8 44.5 %all_to_all.5.arrived = bf16[128,72,128]{2,1,0:T(8,128)(2,1)} all-to-all(bf16[128,72,128]{2,1,0:T(8,128)(2,1)} %encode.1), channel_id=1, replica_groups=mesh['lat'=8,'lon'=16] {'lat','lon'}, dimensions={0} | all-to-all | bytes 4718592 | tf_op jit(solution)/shard_map/all_to_all | solution.py:392
  60.2 12.1 %bin_block.1 = (bf16[8,24,512]{2,1,0:T(8,128)(2,1)}, bf16[8,24,512]{2,1,0:T(8,128)(2,1)}, bf16[8,8,512]{2,1,0:T(8,128)(2,1)}, bf16[8,8,512]{2,1,0:T(8,128)(2,1)}) custom-call(bf16[128,72,128]{2,1,0:T(8,128)(2,1)} %all_to_all.5.arrived, bf16[16,32,512]{2,1,0:T(8,128)(2,1)} %background_hbm.1, f32[2,2,512]{2,1,0:T(2,128)} %gains.3, bf16[2,512,1536]{2,1,0:T(8,128)(2,1)} %wq.3, ...), custom_call_target="tpu_custom_call" | custom-call | flops 4294967296 | bytes 8388608 | tf_op jit(solution)/shard_map/bin_block/pallas_call | solution.py:289
  72.3 1.5 %collective-permute-start = (bf16[8,24,512]{2,1,0:T(8,128)(2,1)}, bf16[8,24,512]{2,1,0:T(8,128)(2,1)S(1)}, u32[]{:S(2)}, u32[]{:S(2)}) collective-permute-start(bf16[8,24,512]{2,1,0:T(8,128)(2,1)} %get-tuple-element.14), channel_id=1, source_target_pairs={{0,112},{1,113},{2,114},{3,115},{4,116},{5,117},{6,118},{7,119},{8... | collective-permute-start | bytes 589832 | tf_op jit(solution)/shard_map/ppermute | solution.py:364
  73.8 0.6 collective-permute-start.1
  74.3 0.5 collective-permute-start.2
  74.9 4.3 %collective-permute-done.1.right = bf16[8,8,512]{2,1,0:T(8,128)(2,1)S(1)} collective-permute-done((bf16[8,8,512]{2,1,0:T(8,128)(2,1)}, bf16[8,8,512]{2,1,0:T(8,128)(2,1)S(1)}, u32[]{:S(2)}, u32[]{:S(2)}) %collective-permute-start.1) | collective-permute-done | bytes 65568 | tf_op jit(solution)/shard_map/ppermute | solution.py:364
  79.1 0.0 copy-start.1
  79.1 0.5 collective-permute-done.2.corner
  79.6 0.0 copy-start.2
  79.6 0.4 collective-permute-done.below
  80.0 0.0 copy-start
  80.0 0.0 copy-done.1
  80.0 0.2 copy-done.2
  80.3 0.4 copy-done
  80.7 9.5 %shift_block.1 = (bf16[8,24,512]{2,1,0:T(8,128)(2,1)}, bf16[8,24,512]{2,1,0:T(8,128)(2,1)}, bf16[8,8,512]{2,1,0:T(8,128)(2,1)}, bf16[8,8,512]{2,1,0:T(8,128)(2,1)}) custom-call(s32[1]{0:T(128)} %bitcast.last, bf16[8,24,512]{2,1,0:T(8,128)(2,1)} %get-tuple-element.13.mine, bf16[8,24,512]{2,1,0:T(8,128)(2,1)} %copy-done, bf16[8,8,512]{2,1,0:T(8,128)(2,1)} %copy-done.1, ...), custom_call_target="tpu_custom_call" | custom-call | flops 4294967296 | bytes 8388608 | tf_op jit(solution)/shard_map/shift_block/pallas_call | solution.py:339
  90.3 0.1 collective-permute-start.4
  90.3 0.1 collective-permute-start.3
  90.4 1.3 %collective-permute-start.5 = (bf16[8,8,512]{2,1,0:T(8,128)(2,1)}, bf16[8,8,512]{2,1,0:T(8,128)(2,1)S(1)}, u32[]{:S(2)}, u32[]{:S(2)}) collective-permute-start(bf16[8,8,512]{2,1,0:T(8,128)(2,1)} %get-tuple-element.19), channel_id=1, source_target_pairs={{0,1},{1,2},{2,3},{3,4},{4,5},{5,6},{6,7},{7,8},{8,9},{9,10},{10,1... | collective-permute-start | bytes 196616 | tf_op jit(solution)/shard_map/ppermute | solution.py:364
  91.7 11.9 %collective-permute-done.3 = bf16[8,8,512]{2,1,0:T(8,128)(2,1)S(1)} collective-permute-done((bf16[8,8,512]{2,1,0:T(8,128)(2,1)}, bf16[8,8,512]{2,1,0:T(8,128)(2,1)S(1)}, u32[]{:S(2)}, u32[]{:S(2)}) %collective-permute-start.3) | collective-permute-done | bytes 65568 | tf_op jit(solution)/shard_map/ppermute | solution.py:364
  103.6 0.0 collective-permute-done.5
  103.6 0.0 collective-permute-done.4
  103.6 1.8 %maximum_maximum_fusion = bf16[16,32,512]{2,1,0:T(8,128)(2,1)} fusion(bf16[8,24,512]{2,1,0:T(8,128)(2,1)} %get-tuple-element.20, bf16[8,8,512]{2,1,0:T(8,128)(2,1)S(1)} %collective-permute-done.5, bf16[8,24,512]{2,1,0:T(8,128)(2,1)S(1)} %collective-permute-done.4, bf16[8,8,512]{2,1,0:T(8,128)(2,1)S(1)} %collective-permute-done.3), kind=kLoop, calls=%fused_computation | loop fusion | flops 2097152 | bytes 1048576 | tf_op jit(solution)/shard_map/concatenate | solution.py:407
Async XLA Ops:
  72.3 7.7 %collective-permute-start = (bf16[8,24,512]{2,1,0:T(8,128)(2,1)}, bf16[8,24,512]{2,1,0:T(8,128)(2,1)S(1)}, u32[]{:S(2)}, u32[]{:S(2)}) collective-permute-start(bf16[8,24,512]{2,1,0:T(8,128)(2,1)} %get-tuple-element.14), channel_id=1, source_target_pairs={{0,112},{1,113},{2,114},{3,115},{4,116},{5,117},{6,118},{7,119},{8... | collective-permute-start | bytes 589832 | tf_op jit(solution)/shard_map/ppermute | solution.py:364
  73.8 5.3 %collective-permute-start.1 = (bf16[8,8,512]{2,1,0:T(8,128)(2,1)}, bf16[8,8,512]{2,1,0:T(8,128)(2,1)S(1)}, u32[]{:S(2)}, u32[]{:S(2)}) collective-permute-start(bf16[8,8,512]{2,1,0:T(8,128)(2,1)} %get-tuple-element.15), channel_id=1, source_target_pairs={{0,15},{1,0},{2,1},{3,2},{4,3},{5,4},{6,5},{7,6},{8,7},{9,8},{10,9... | collective-permute-start | bytes 196616 | tf_op jit(solution)/shard_map/ppermute | solution.py:364
  74.3 5.3 %collective-permute-start.2 = (bf16[8,8,512]{2,1,0:T(8,128)(2,1)}, bf16[8,8,512]{2,1,0:T(8,128)(2,1)S(1)}, u32[]{:S(2)}, u32[]{:S(2)}) collective-permute-start(bf16[8,8,512]{2,1,0:T(8,128)(2,1)} %get-tuple-element.16), channel_id=1, source_target_pairs={{0,127},{1,112},{2,113},{3,114},{4,115},{5,116},{6,117},{7,118},{8... | collective-permute-start | bytes 196616 | tf_op jit(solution)/shard_map/ppermute | solution.py:364
  79.1 0.9 copy-start.1
  79.6 0.6 copy-start.2
  80.0 0.7 copy-start
  90.3 13.3 %collective-permute-start.4 = (bf16[8,24,512]{2,1,0:T(8,128)(2,1)}, bf16[8,24,512]{2,1,0:T(8,128)(2,1)S(1)}, u32[]{:S(2)}, u32[]{:S(2)}) collective-permute-start(bf16[8,24,512]{2,1,0:T(8,128)(2,1)} %get-tuple-element.18), channel_id=1, source_target_pairs={{0,16},{1,17},{2,18},{3,19},{4,20},{5,21},{6,22},{7,23},{8,24},{9,... | collective-permute-start | bytes 589832 | tf_op jit(solution)/shard_map/ppermute | solution.py:364
  90.3 13.2 %collective-permute-start.3 = (bf16[8,8,512]{2,1,0:T(8,128)(2,1)}, bf16[8,8,512]{2,1,0:T(8,128)(2,1)S(1)}, u32[]{:S(2)}, u32[]{:S(2)}) collective-permute-start(bf16[8,8,512]{2,1,0:T(8,128)(2,1)} %get-tuple-element.17), channel_id=1, source_target_pairs={{0,17},{1,18},{2,19},{3,20},{4,21},{5,22},{6,23},{7,24},{8,25},{9,... | collective-permute-start | bytes 196616 | tf_op jit(solution)/shard_map/ppermute | solution.py:364
  90.4 13.1 %collective-permute-start.5 = (bf16[8,8,512]{2,1,0:T(8,128)(2,1)}, bf16[8,8,512]{2,1,0:T(8,128)(2,1)S(1)}, u32[]{:S(2)}, u32[]{:S(2)}) collective-permute-start(bf16[8,8,512]{2,1,0:T(8,128)(2,1)} %get-tuple-element.19), channel_id=1, source_target_pairs={{0,1},{1,2},{2,3},{3,4},{4,5},{5,6},{6,7},{7,8},{8,9},{9,10},{10,1... | collective-permute-start | bytes 196616 | tf_op jit(solution)/shard_map/ppermute | solution.py:364

commit v2 on v1

--- a/solution.py
+++ b/solution.py
@@ -22,8 +22,8 @@
 TILE = 512
 EPS = 1e-5
 ENCODE_VMEM = 67043328 - (100 << 10)
-BIN_VMEM = 67043328 - (3000 << 10)
-SHIFT_VMEM = 67043328 - (1100 << 10)
+BIN_VMEM = (64 << 20) - (16000 << 10)
+SHIFT_VMEM = (64 << 20) - (12000 << 10)
 BF = jnp.bfloat16
 F32 = jnp.float32
 VMEM = pl.BlockSpec(memory_space=pltpu.VMEM)
@@ -59,7 +59,7 @@
 
 def encode_kernel(
     place, count, dest, token, rows_hbm, w_in_hbm, w_out_hbm, slab_hbm,
-    rows, w_in, w_out, slab, encoded, slots, in_sems, out_sems,
+    rows, w_in, w_out, slab, encoded, total, slots, in_sems, out_sems,
 ):
     tiles = FF // TILE
     rows_copy = pltpu.make_async_copy(rows_hbm, rows, in_sems.at[2 * tiles])
@@ -72,9 +72,8 @@
             pltpu.make_async_copy(w_out_hbm.at[f, :], w_out.at[f, :], in_sems.at[tiles + t])
         )
     rows_copy.start()
-    for t in range(tiles):
-        w_in_copies[t].start()
-        w_out_copies[t].start()
+    w_in_copies[0].start()
+    w_out_copies[0].start()
 
     live_count = count[0]
     lane_base = (place[0] % 8) * CAP
@@ -105,25 +104,27 @@
     marks = jnp.where(sub == 0, high[:, None, :], jnp.where(sub == 1, low[:, None, :], 0.0))
     slab[:, 4 * CAP : SLAB, :] = marks.astype(BF)
     rows_copy.wait()
-
-    def encode_block(b, _):
-        r = pl.ds(pl.multiple_of(b * BLK, BLK), BLK)
-        x = rows[r, :]
-        total = jnp.zeros((BLK, D), F32)
-        for t in range(tiles):
-
-            @pl.when(b == 0)
-            def _():
-                w_in_copies[t].wait()
-                w_out_copies[t].wait()
-
-            f = slice(t * TILE, (t + 1) * TILE)
-            hidden = gelu(dot(x, w_in[:, f])).astype(BF)
-            total = total + dot(hidden, w_out[f, :])
-        encoded[r, :] = total.astype(BF)
-        return 0
-
-    lax.fori_loop(0, OBS_DEV // BLK, encode_block, 0)
+    for t in range(tiles):
+        w_in_copies[t].wait()
+        w_out_copies[t].wait()
+        if t + 1 < tiles:
+            w_in_copies[t + 1].start()
+            w_out_copies[t + 1].start()
+        f = slice(t * TILE, (t + 1) * TILE)
+
+        def encode_block(b, _):
+            r = pl.ds(pl.multiple_of(b * BLK, BLK), BLK)
+            hidden = gelu(dot(rows[r, :], w_in[:, f])).astype(BF)
+            part = dot(hidden, w_out[f, :])
+            if t > 0:
+                part = total[r, :] + part
+            if t + 1 < tiles:
+                total[r, :] = part
+            else:
+                encoded[r, :] = part.astype(BF)
+            return 0
+
+        lax.fori_loop(0, OBS_DEV // BLK, encode_block, 0)
     step = BLK // CAP
 
     def slab_copy(b):
@@ -157,6 +158,7 @@
             pltpu.VMEM((FF, D), BF),
             pltpu.VMEM((OWNERS, SLAB, LANES), BF),
             pltpu.VMEM((OBS_DEV, D), BF),
+            pltpu.VMEM((OBS_DEV, D), F32),
             pltpu.VMEM((1, OBS_DEV), jnp.int32),
             pltpu.SemaphoreType.DMA((2 * FF // TILE + 1,)),
             pltpu.SemaphoreType.DMA((OWNERS * CAP // BLK,)),
@@ -177,18 +179,17 @@
         f = slice(t * TILE, (t + 1) * TILE)
         pairs.append((w_up.at[layer, :, f], v_up.at[:, f]))
         pairs.append((w_down.at[layer, f, :], v_down.at[f, :]))
-    copies = [pltpu.make_async_copy(a, b, sems.at[i]) for i, (a, b) in enumerate(pairs)]
-    for copy in copies:
-        copy.start()
-    return copies
-
-
-def block_body(x, bias, gain_a, gain_b, weights, copies, qkv, mixed):
+    return [pltpu.make_async_copy(a, b, sems.at[i]) for i, (a, b) in enumerate(pairs)]
+
+
+def block_body(layer, x, bias, gains, weights, copies, qkv, mixed):
     w_qkv, w_proj, w_up, w_down = weights
     count = x.shape[0]
     area = WIN * WIN
-    h = normed(x, gain_a)
+    h = normed(x, gains[layer, 0:1, :])
     copies[0].wait()
+    for copy in copies[1:]:
+        copy.start()
     qkv[...] = dot(h, w_qkv[...]).astype(BF)
     first = iota((area, LANES), 1) < 64
     ones = jnp.ones((area, LANES), BF)
@@ -211,23 +212,22 @@
             mixed[r, c : c + LANES] = jnp.where(first, out[0], out[1]).astype(BF)
     copies[1].wait()
     attended = x + dot(mixed[...], w_proj[...])
-    h = normed(attended, gain_b)
+    h = normed(attended, gains[layer, 1:2, :])
     total = attended
     for t in range(FF // TILE):
-        copies[2 + 2 * t].wait()
-        copies[3 + 2 * t].wait()
+        copies[2 * t + 2].wait()
+        copies[2 * t + 3].wait()
         f = slice(t * TILE, (t + 1) * TILE)
         total = total + dot(gelu(dot(h, w_up[:, f])).astype(BF), w_down[f, :])
     return total.astype(BF)
 
 
 def bin_kernel(
-    arrived, background_hbm, gains, wq, wp, wu, wd, keep, below, right, corner,
-    lined, pick, background, vq, vp, vu, vd, qkv, mixed, state, sems, back_sem,
+    arrived, background, gains, wq, wp, wu, wd, keep, below, right, corner,
+    lined, pick, vq, vp, vu, vd, qkv, mixed, state, sems,
 ):
-    back_copy = pltpu.make_async_copy(background_hbm, background, back_sem.at[0])
-    back_copy.start()
     copies = weight_copies(0, (wq, wp, wu, wd), (vq, vp, vu, vd), sems)
+    copies[0].start()
     for k in range(4):
         lined[:, k * LANES : (k + 1) * LANES] = arrived[:, k * CAP : (k + 1) * CAP, :].reshape(
             OWNERS * CAP, LANES
@@ -246,14 +246,11 @@
         pick[:, g * LANES : (g + 1) * LANES] = hit.astype(BF)
     tally = jnp.sum(tally, 1, keepdims=True)
     sums = dot(pick[...], lined[...]) / jnp.maximum(tally, 1.0)
-    back_copy.wait()
     for w in range(2):
         r = slice(w * BLK, (w + 1) * BLK)
         back = background[:, w * WIN : (w + 1) * WIN, :].astype(F32).reshape(BLK, D)
         state[r, :] = (back + sums[r, :]).astype(BF).astype(F32)
-    done = block_body(
-        state[...], None, gains[0, 0:1, :], gains[0, 1:2, :], (vq, vp, vu, vd), copies, qkv, mixed
-    )
+    done = block_body(0, state[...], None, gains, (vq, vp, vu, vd), copies, qkv, mixed)
     one = done[:BLK].reshape(WIN, WIN, D)
     two = done[BLK:].reshape(WIN, WIN, D)
     corner[...] = one[:HALF, :HALF]
@@ -270,12 +267,12 @@
     pltpu.VMEM((D, FF), BF),
     pltpu.VMEM((FF, D), BF),
 ]
+WEIGHT_SEMS = pltpu.SemaphoreType.DMA((2 + 2 * FF // TILE,))
 BLOCK_SCRATCH = [
     pltpu.VMEM((CELLS, 3 * D), BF),
     pltpu.VMEM((CELLS, D), BF),
     pltpu.VMEM((CELLS, D), F32),
 ]
-WEIGHT_SEMS = pltpu.SemaphoreType.DMA((2 + 2 * FF // TILE,))
 BLOCK_COST = pl.CostEstimate(flops=4 << 30, transcendentals=2 << 20, bytes_accessed=8 << 20)
 PIECES = (
     jax.ShapeDtypeStruct((HALF, CLON - HALF, D), BF),
@@ -289,16 +286,15 @@
     return pl.pallas_call(
         bin_kernel,
         out_shape=PIECES,
-        in_specs=[VMEM, HBM, VMEM] + [HBM] * 4,
+        in_specs=[VMEM] * 3 + [HBM] * 4,
         out_specs=[VMEM] * 4,
         scratch_shapes=[
             pltpu.VMEM((OWNERS * CAP, D), BF),
             pltpu.VMEM((CELLS, OWNERS * CAP), BF),
-            pltpu.VMEM((CLAT, CLON, D), BF),
         ]
         + WEIGHT_SCRATCH
         + BLOCK_SCRATCH
-        + [WEIGHT_SEMS, pltpu.SemaphoreType.DMA((1,))],
+        + [WEIGHT_SEMS],
         compiler_params=pltpu.CompilerParams(vmem_limit_bytes=BIN_VMEM),
         cost_estimate=BLOCK_COST,
         name="bin_block",
@@ -310,6 +306,7 @@
     vq, vp, vu, vd, qkv, mixed, state, bias, sems,
 ):
     copies = weight_copies(1, (wq, wp, wu, wd), (vq, vp, vu, vd), sems)
+    copies[0].start()
     area = WIN * WIN
     split = (iota((area, area), 0) < area // 2) != (iota((area, area), 1) < area // 2)
     bias[...] = jnp.where(split & (last[0] == 1), -1e30, 0.0)
@@ -323,7 +320,7 @@
     state[2 * h : 3 * h, :] = top.reshape(h, D)
     state[3 * h : 4 * h, :] = bottom.reshape(h, D)
     done = block_body(
-        state[...], bias[...], gains[1, 0:1, :], gains[1, 1:2, :], (vq, vp, vu, vd), copies, qkv, mixed
+        1, state[...], bias[...], gains, (vq, vp, vu, vd), copies, qkv, mixed
     )
     one = done[:BLK].reshape(WIN, WIN, D)
     two = done[BLK:].reshape(WIN, WIN, D)

time: 106 us -> 98.8 us (0.932)
  Pallas kernels: 36.7 us -> 32.1 us
    pallas_call x1, Pallas kernels: 12.1 us -> 8.33 us  [bin_block(): pl.pallas_call(bin_kernel, out_shape=PIECES, in_specs=[VMEM] * 3 + [HBM]...]
    pallas_call x1, Pallas kernels: 9.55 us -> 7.71 us  [shift_block(): pl.pallas_call(shift_kernel, out_shape=PIECES, in_specs=[SMEM] + [VMEM] *...]
where the time goes in v2:
time: 98.8 us; the launch traced here: 98.5 us
  blocking collectives  44.4 us (45%)
  Pallas kernels  32.1 us (32%)
  waiting for transfers between devices  16.5 us (17%)
  starting transfers between devices  3.97 us (4%)
    all_to_all x1, blocking collectives, on_device(): lax.all_to_all(slab, ('lat', 'lon'), split_axis=0, concat_axis=0, tiled=T...  44.4 us
    ppermute x6, waiting for transfers between devices, moved(): return lax.ppermute(block, ('lat', 'lon'), route)  16.5 us
    pallas_call x1, Pallas kernels, encode(): pl.pallas_call(encode_kernel, out_shape=jax.ShapeDtypeStruct((OWNERS, SLA...  16 us
    pallas_call x1, Pallas kernels, bin_block(): pl.pallas_call(bin_kernel, out_shape=PIECES, in_specs=[VMEM] * 3 + [HBM]...  8.33 us
    pallas_call x1, Pallas kernels, shift_block(): pl.pallas_call(shift_kernel, out_shape=PIECES, in_specs=[SMEM] + [VMEM] *...  7.71 us
    ppermute x6, starting transfers between devices, moved(): return lax.ppermute(block, ('lat', 'lon'), route)  3.97 us
  transfers between devices with their start and end apart: 6, of which 4 were waited for; matrix products, arithmetic and copies ran while one was open for 0% of the time, Pallas kernels for 0%

profile of v2, /device:TPU:0, one launch (start us, length us, event | category | flops | bytes accessed | tf_op | source)
XLA Modules:
  0.0 98.5 jit_solution(15125966397229634331)
XLA Ops:
  0.7 16.0 %encode.1 = bf16[128,72,128]{2,1,0:T(8,128)(2,1)} custom-call(s32[1]{0:T(128)} %bitcast.1.place, s32[1]{0:T(128)S(6)} %copy.13.count, s32[1,1024]{1,0:T(1,128)} %bitcast.4, s32[1,1024]{1,0:T(1,128)} %bitcast.5, bf16[1024,512]{1,0:T(8,128)(2,1)} %rows_hbm.1, bf16[512,2048]{1,0:T(8,128)(2,1)} %w_in_hbm.1, bf16[2048,512]{1,0:T(8,128)(2,1)} %w_out_hbm.1), custom_call_target="tpu_custom_call" | custom-call | flops 7516192768 | bytes 8388608 | tf_op jit(solution)/shard_map/encode/pallas_call | solution.py:150
  16.7 0.0 copy-start
  16.7 0.0 copy-start.1
  16.7 0.0 copy-start.2
  16.7 44.4 %all_to_all.5.arrived = bf16[128,72,128]{2,1,0:T(8,128)(2,1)S(1)} all-to-all(bf16[128,72,128]{2,1,0:T(8,128)(2,1)} %encode.1), channel_id=1, replica_groups=mesh['lat'=8,'lon'=16] {'lat','lon'}, dimensions={0} | all-to-all | bytes 4718592 | tf_op jit(solution)/shard_map/all_to_all | solution.py:389
  61.1 0.0 copy-done
  61.1 0.0 copy-done.1
  61.1 0.0 copy-done.2
  61.1 8.3 %bin_block.1 = (bf16[8,24,512]{2,1,0:T(8,128)(2,1)S(1)}, bf16[8,24,512]{2,1,0:T(8,128)(2,1)S(1)}, bf16[8,8,512]{2,1,0:T(8,128)(2,1)S(1)}, bf16[8,8,512]{2,1,0:T(8,128)(2,1)S(1)}) custom-call(bf16[128,72,128]{2,1,0:T(8,128)(2,1)S(1)} %all_to_all.5.arrived, bf16[16,32,512]{2,1,0:T(8,128)(2,1)S(1)} %copy-done.1, f32[2,2,512]{2,1,0:T(2,128)S(1)} %copy-done.2, ...), custom_call_target="tpu_custom_call" | custom-call | flops 4294967296 | bytes 8388608 | tf_op jit(solution)/shard_map/bin_block/pallas_call | solution.py:286
  69.4 1.5 %collective-permute-start = (bf16[8,24,512]{2,1,0:T(8,128)(2,1)S(1)}, bf16[8,24,512]{2,1,0:T(8,128)(2,1)S(1)}, u32[]{:S(2)}, u32[]{:S(2)}) collective-permute-start(bf16[8,24,512]{2,1,0:T(8,128)(2,1)S(1)} %get-tuple-element.14), channel_id=1, source_target_pairs={{0,112},{1,113},{2,114},{3,115},{4,116},{5,117},{6,118},{7,119},{8... | collective-permute-start | bytes 589832 | tf_op jit(solution)/shard_map/ppermute | solution.py:361
  70.9 0.6 collective-permute-start.1
  71.5 0.5 collective-permute-start.2
  72.0 3.9 %collective-permute-done.1.right = bf16[8,8,512]{2,1,0:T(8,128)(2,1)S(1)} collective-permute-done((bf16[8,8,512]{2,1,0:T(8,128)(2,1)S(1)}, bf16[8,8,512]{2,1,0:T(8,128)(2,1)S(1)}, u32[]{:S(2)}, u32[]{:S(2)}) %collective-permute-start.1) | collective-permute-done | bytes 65568 | tf_op jit(solution)/shard_map/ppermute | solution.py:361
  75.9 0.6 collective-permute-done.2.corner
  76.6 0.4 collective-permute-done.below
  77.0 7.7 %shift_block.1 = (bf16[8,24,512]{2,1,0:T(8,128)(2,1)S(1)}, bf16[8,24,512]{2,1,0:T(8,128)(2,1)S(1)}, bf16[8,8,512]{2,1,0:T(8,128)(2,1)S(1)}, bf16[8,8,512]{2,1,0:T(8,128)(2,1)S(1)}) custom-call(s32[1]{0:T(128)} %bitcast.last, bf16[8,24,512]{2,1,0:T(8,128)(2,1)S(1)} %get-tuple-element.13.mine, bf16[8,24,512]{2,1,0:T(8,128)(2,1)S(1)} %collective-permute-done.below, ...), custom_call_target="tpu_custom_call" | custom-call | flops 4294967296 | bytes 8388608 | tf_op jit(solution)/shard_map/shift_block/pallas_call | solution.py:336
  84.7 0.1 collective-permute-start.4
  84.8 0.1 collective-permute-start.3
  84.9 1.3 %collective-permute-start.5 = (bf16[8,8,512]{2,1,0:T(8,128)(2,1)S(1)}, bf16[8,8,512]{2,1,0:T(8,128)(2,1)S(1)}, u32[]{:S(2)}, u32[]{:S(2)}) collective-permute-start(bf16[8,8,512]{2,1,0:T(8,128)(2,1)S(1)} %get-tuple-element.19), channel_id=1, source_target_pairs={{0,1},{1,2},{2,3},{3,4},{4,5},{5,6},{6,7},{7,8},{8,9},{9,10},{10,1... | collective-permute-start | bytes 196616 | tf_op jit(solution)/shard_map/ppermute | solution.py:361
  86.1 11.5 %collective-permute-done.3 = bf16[8,8,512]{2,1,0:T(8,128)(2,1)S(1)} collective-permute-done((bf16[8,8,512]{2,1,0:T(8,128)(2,1)S(1)}, bf16[8,8,512]{2,1,0:T(8,128)(2,1)S(1)}, u32[]{:S(2)}, u32[]{:S(2)}) %collective-permute-start.3) | collective-permute-done | bytes 65568 | tf_op jit(solution)/shard_map/ppermute | solution.py:361
  97.7 0.0 collective-permute-done.5
  97.7 0.0 collective-permute-done.4
  97.7 0.9 maximum_maximum_fusion
Async XLA Ops:
  16.7 44.4 %copy-start = (bf16[2,512,512]{2,1,0:T(8,128)(2,1)S(1)}, bf16[2,512,512]{2,1,0:T(8,128)(2,1)}, u32[]{:S(2)}) copy-start(bf16[2,512,512]{2,1,0:T(8,128)(2,1)} %wp.3) | copy-start | bytes 3145732
  16.7 44.4 %copy-start.1 = (bf16[16,32,512]{2,1,0:T(8,128)(2,1)S(1)}, bf16[16,32,512]{2,1,0:T(8,128)(2,1)}, u32[]{:S(2)}) copy-start(bf16[16,32,512]{2,1,0:T(8,128)(2,1)} %background.1) | copy-start | bytes 1572868
  16.7 44.4 %copy-start.2 = (f32[2,2,512]{2,1,0:T(2,128)S(1)}, f32[2,2,512]{2,1,0:T(2,128)}, u32[]{:S(2)}) copy-start(f32[2,2,512]{2,1,0:T(2,128)} %gains.3) | copy-start | bytes 24580
  69.4 7.5 %collective-permute-start = (bf16[8,24,512]{2,1,0:T(8,128)(2,1)S(1)}, bf16[8,24,512]{2,1,0:T(8,128)(2,1)S(1)}, u32[]{:S(2)}, u32[]{:S(2)}) collective-permute-start(bf16[8,24,512]{2,1,0:T(8,128)(2,1)S(1)} %get-tuple-element.14), channel_id=1, source_target_pairs={{0,112},{1,113},{2,114},{3,115},{4,116},{5,117},{6,118},{7,119},{8... | collective-permute-start | bytes 589832 | tf_op jit(solution)/shard_map/ppermute | solution.py:361
  70.9 5.0 %collective-permute-start.1 = (bf16[8,8,512]{2,1,0:T(8,128)(2,1)S(1)}, bf16[8,8,512]{2,1,0:T(8,128)(2,1)S(1)}, u32[]{:S(2)}, u32[]{:S(2)}) collective-permute-start(bf16[8,8,512]{2,1,0:T(8,128)(2,1)S(1)} %get-tuple-element.15), channel_id=1, source_target_pairs={{0,15},{1,0},{2,1},{3,2},{4,3},{5,4},{6,5},{7,6},{8,7},{9,8},{10,9... | collective-permute-start | bytes 196616 | tf_op jit(solution)/shard_map/ppermute | solution.py:361
  71.5 5.1 %collective-permute-start.2 = (bf16[8,8,512]{2,1,0:T(8,128)(2,1)S(1)}, bf16[8,8,512]{2,1,0:T(8,128)(2,1)S(1)}, u32[]{:S(2)}, u32[]{:S(2)}) collective-permute-start(bf16[8,8,512]{2,1,0:T(8,128)(2,1)S(1)} %get-tuple-element.16), channel_id=1, source_target_pairs={{0,127},{1,112},{2,113},{3,114},{4,115},{5,116},{6,117},{7,118},{8... | collective-permute-start | bytes 196616 | tf_op jit(solution)/shard_map/ppermute | solution.py:361
  84.7 13.0 %collective-permute-start.4 = (bf16[8,24,512]{2,1,0:T(8,128)(2,1)S(1)}, bf16[8,24,512]{2,1,0:T(8,128)(2,1)S(1)}, u32[]{:S(2)}, u32[]{:S(2)}) collective-permute-start(bf16[8,24,512]{2,1,0:T(8,128)(2,1)S(1)} %get-tuple-element.18), channel_id=1, source_target_pairs={{0,16},{1,17},{2,18},{3,19},{4,20},{5,21},{6,22},{7,23},{8,24},{9,... | collective-permute-start | bytes 589832 | tf_op jit(solution)/shard_map/ppermute | solution.py:361
  84.8 12.9 %collective-permute-start.3 = (bf16[8,8,512]{2,1,0:T(8,128)(2,1)S(1)}, bf16[8,8,512]{2,1,0:T(8,128)(2,1)S(1)}, u32[]{:S(2)}, u32[]{:S(2)}) collective-permute-start(bf16[8,8,512]{2,1,0:T(8,128)(2,1)S(1)} %get-tuple-element.17), channel_id=1, source_target_pairs={{0,17},{1,18},{2,19},{3,20},{4,21},{5,22},{6,23},{7,24},{8,25},{9,... | collective-permute-start | bytes 196616 | tf_op jit(solution)/shard_map/ppermute | solution.py:361
  84.9 12.8 %collective-permute-start.5 = (bf16[8,8,512]{2,1,0:T(8,128)(2,1)S(1)}, bf16[8,8,512]{2,1,0:T(8,128)(2,1)S(1)}, u32[]{:S(2)}, u32[]{:S(2)}) collective-permute-start(bf16[8,8,512]{2,1,0:T(8,128)(2,1)S(1)} %get-tuple-element.19), channel_id=1, source_target_pairs={{0,1},{1,2},{2,3},{3,4},{4,5},{5,6},{6,7},{7,8},{8,9},{9,10},{10,1... | collective-permute-start | bytes 196616 | tf_op jit(solution)/shard_map/ppermute | solution.py:361

commit v3 on v2

--- a/solution.py
+++ b/solution.py
@@ -20,6 +20,8 @@
 SLAB = 4 * CAP + 8
 BLK = 256
 TILE = 512
+ENC_TILE = 1024
+PUT = 512
 EPS = 1e-5
 ENCODE_VMEM = 67043328 - (100 << 10)
 BIN_VMEM = (64 << 20) - (16000 << 10)
@@ -61,19 +63,18 @@
     place, count, dest, token, rows_hbm, w_in_hbm, w_out_hbm, slab_hbm,
     rows, w_in, w_out, slab, encoded, total, slots, in_sems, out_sems,
 ):
-    tiles = FF // TILE
+    tiles = FF // ENC_TILE
     rows_copy = pltpu.make_async_copy(rows_hbm, rows, in_sems.at[2 * tiles])
     w_in_copies = []
     w_out_copies = []
     for t in range(tiles):
-        f = slice(t * TILE, (t + 1) * TILE)
+        f = slice(t * ENC_TILE, (t + 1) * ENC_TILE)
         w_in_copies.append(pltpu.make_async_copy(w_in_hbm.at[:, f], w_in.at[:, f], in_sems.at[t]))
         w_out_copies.append(
             pltpu.make_async_copy(w_out_hbm.at[f, :], w_out.at[f, :], in_sems.at[tiles + t])
         )
     rows_copy.start()
     w_in_copies[0].start()
-    w_out_copies[0].start()
 
     live_count = count[0]
     lane_base = (place[0] % 8) * CAP
@@ -106,33 +107,31 @@
     rows_copy.wait()
     for t in range(tiles):
         w_in_copies[t].wait()
+        if t == 0:
+            w_out_copies[0].start()
+        if t + 1 < tiles:
+            w_in_copies[t + 1].start()
+        f = slice(t * ENC_TILE, (t + 1) * ENC_TILE)
+
+        hidden = gelu(dot(rows[...], w_in[:, f])).astype(BF)
         w_out_copies[t].wait()
         if t + 1 < tiles:
-            w_in_copies[t + 1].start()
             w_out_copies[t + 1].start()
-        f = slice(t * TILE, (t + 1) * TILE)
-
-        def encode_block(b, _):
-            r = pl.ds(pl.multiple_of(b * BLK, BLK), BLK)
-            hidden = gelu(dot(rows[r, :], w_in[:, f])).astype(BF)
-            part = dot(hidden, w_out[f, :])
-            if t > 0:
-                part = total[r, :] + part
-            if t + 1 < tiles:
-                total[r, :] = part
-            else:
-                encoded[r, :] = part.astype(BF)
-            return 0
-
-        lax.fori_loop(0, OBS_DEV // BLK, encode_block, 0)
-    step = BLK // CAP
+        part = dot(hidden, w_out[f, :])
+        if t > 0:
+            part = total[...] + part
+        if t + 1 < tiles:
+            total[...] = part
+        else:
+            encoded[...] = part.astype(BF)
+    step = PUT // CAP
 
     def slab_copy(b):
         d = pl.ds(b * step, step)
         return pltpu.make_async_copy(slab.at[d], slab_hbm.at[d], out_sems.at[b])
 
     def place_block(b, _):
-        wanted = iota((BLK, OBS_DEV), 0) + b * BLK
+        wanted = iota((PUT, OBS_DEV), 0) + b * PUT
         pick = jnp.where(slots[...] == wanted, 1.0, 0.0).astype(BF)
         moved = dot(pick, encoded[...]).astype(BF).reshape(step, CAP, D)
         d = pl.ds(b * step, step)
@@ -160,8 +159,8 @@
             pltpu.VMEM((OBS_DEV, D), BF),
             pltpu.VMEM((OBS_DEV, D), F32),
             pltpu.VMEM((1, OBS_DEV), jnp.int32),
-            pltpu.SemaphoreType.DMA((2 * FF // TILE + 1,)),
-            pltpu.SemaphoreType.DMA((OWNERS * CAP // BLK,)),
+            pltpu.SemaphoreType.DMA((2 * FF // ENC_TILE + 1,)),
+            pltpu.SemaphoreType.DMA((OWNERS * CAP // PUT,)),
         ],
         compiler_params=pltpu.CompilerParams(vmem_limit_bytes=ENCODE_VMEM),
         cost_estimate=pl.CostEstimate(
@@ -205,7 +204,7 @@
                 mine = first if head == 0 else jnp.logical_not(first)
                 scores = dot_nt(jnp.where(mine, q, BF(0)), k)
                 if bias is not None:
-                    scores = scores + bias
+                    scores = scores + bias[w]
                 probs = jnp.exp(scores - jnp.max(scores, -1, keepdims=True)).astype(BF)
                 both = dot(probs, v)
                 out.append(both[:, :LANES] / both[:, LANES:])
@@ -223,7 +222,8 @@
 
 
 def bin_kernel(
-    arrived, background, gains, wq, wp, wu, wd, keep, below, right, corner,
+    arrived, background, gains, wq, wp, wu, wd,
+    mid, edge, to_up, to_down, to_down_left, to_left,
     lined, pick, vq, vp, vu, vd, qkv, mixed, state, sems,
 ):
     copies = weight_copies(0, (wq, wp, wu, wd), (vq, vp, vu, vd), sems)
@@ -253,12 +253,14 @@
     done = block_body(0, state[...], None, gains, (vq, vp, vu, vd), copies, qkv, mixed)
     one = done[:BLK].reshape(WIN, WIN, D)
     two = done[BLK:].reshape(WIN, WIN, D)
-    corner[...] = one[:HALF, :HALF]
-    right[...] = one[HALF:, :HALF]
-    below[:, :HALF, :] = one[:HALF, HALF:]
-    below[:, HALF:, :] = two[:HALF]
-    keep[:, :HALF, :] = one[HALF:, HALF:]
-    keep[:, HALF:, :] = two[HALF:]
+    mid[:, :HALF, :] = one[HALF:, HALF:]
+    mid[:, HALF:, :] = two[HALF:, :HALF]
+    edge[...] = two[:HALF, HALF:]
+    to_up[:, :HALF, :] = one[:HALF, HALF:]
+    to_up[:, HALF:, :] = two[:HALF, :HALF]
+    to_down[...] = two[HALF:, HALF:]
+    to_down_left[...] = one[HALF:, :HALF]
+    to_left[...] = one[:HALF, :HALF]
 
 
 WEIGHT_SCRATCH = [
@@ -274,12 +276,9 @@
     pltpu.VMEM((CELLS, D), F32),
 ]
 BLOCK_COST = pl.CostEstimate(flops=4 << 30, transcendentals=2 << 20, bytes_accessed=8 << 20)
-PIECES = (
-    jax.ShapeDtypeStruct((HALF, CLON - HALF, D), BF),
-    jax.ShapeDtypeStruct((HALF, CLON - HALF, D), BF),
-    jax.ShapeDtypeStruct((HALF, HALF, D), BF),
-    jax.ShapeDtypeStruct((HALF, HALF, D), BF),
-)
+WIDE = jax.ShapeDtypeStruct((HALF, WIN, D), BF)
+NARROW = jax.ShapeDtypeStruct((HALF, HALF, D), BF)
+PIECES = (WIDE, NARROW, WIDE, NARROW, NARROW, NARROW)
 
 
 def bin_block(arrived, background, gains, *weights):
@@ -287,7 +286,7 @@
         bin_kernel,
         out_shape=PIECES,
         in_specs=[VMEM] * 3 + [HBM] * 4,
-        out_specs=[VMEM] * 4,
+        out_specs=[VMEM] * 6,
         scratch_shapes=[
             pltpu.VMEM((OWNERS * CAP, D), BF),
             pltpu.VMEM((CELLS, OWNERS * CAP), BF),
@@ -302,49 +301,47 @@
 
 
 def shift_kernel(
-    last, mine, below, right, corner, gains, wq, wp, wu, wd, keep, above, left, diagonal,
+    ends, mid, edge, below, above, above_right, right, gains, wq, wp, wu, wd,
+    own_mid, own_edge, to_down, to_up, to_up_right, to_right,
     vq, vp, vu, vd, qkv, mixed, state, bias, sems,
 ):
     copies = weight_copies(1, (wq, wp, wu, wd), (vq, vp, vu, vd), sems)
     copies[0].start()
     area = WIN * WIN
-    split = (iota((area, area), 0) < area // 2) != (iota((area, area), 1) < area // 2)
-    bias[...] = jnp.where(split & (last[0] == 1), -1e30, 0.0)
-    top = mine[...].astype(F32)
-    bottom = below[...].astype(F32)
     h = area // 2
-    state[0:h, :] = top[:, :WIN, :].reshape(h, D)
-    state[h : 2 * h, :] = bottom[:, :WIN, :].reshape(h, D)
-    top = jnp.concatenate([top[:, WIN:, :], right[...].astype(F32)], 1)
-    bottom = jnp.concatenate([bottom[:, WIN:, :], corner[...].astype(F32)], 1)
+    split = (iota((area, area), 0) < h) != (iota((area, area), 1) < h)
+    for w in range(2):
+        bias[w] = jnp.where(split & (ends[0] == w + 1), -1e30, 0.0)
+    state[0:h, :] = mid[...].astype(F32).reshape(h, D)
+    state[h : 2 * h, :] = below[...].astype(F32).reshape(h, D)
+    top = jnp.concatenate([above[...].astype(F32), above_right[...].astype(F32)], 1)
+    bottom = jnp.concatenate([edge[...].astype(F32), right[...].astype(F32)], 1)
     state[2 * h : 3 * h, :] = top.reshape(h, D)
     state[3 * h : 4 * h, :] = bottom.reshape(h, D)
-    done = block_body(
-        1, state[...], bias[...], gains, (vq, vp, vu, vd), copies, qkv, mixed
-    )
+    done = block_body(1, state[...], bias, gains, (vq, vp, vu, vd), copies, qkv, mixed)
     one = done[:BLK].reshape(WIN, WIN, D)
     two = done[BLK:].reshape(WIN, WIN, D)
-    diagonal[...] = two[HALF:, HALF:]
-    left[...] = two[:HALF, HALF:]
-    above[:, :WIN, :] = one[HALF:]
-    above[:, WIN:, :] = two[HALF:, :HALF]
-    keep[:, :WIN, :] = one[:HALF]
-    keep[:, WIN:, :] = two[:HALF, :HALF]
-
-
-def shift_block(last, mine, below, right, corner, gains, *weights):
+    own_mid[...] = one[:HALF]
+    own_edge[...] = two[HALF:, :HALF]
+    to_down[...] = one[HALF:]
+    to_up[...] = two[:HALF, :HALF]
+    to_up_right[...] = two[:HALF, HALF:]
+    to_right[...] = two[HALF:, HALF:]
+
+
+def shift_block(ends, pieces, gains, *weights):
     return pl.pallas_call(
         shift_kernel,
         out_shape=PIECES,
-        in_specs=[SMEM] + [VMEM] * 5 + [HBM] * 4,
-        out_specs=[VMEM] * 4,
+        in_specs=[SMEM] + [VMEM] * 7 + [HBM] * 4,
+        out_specs=[VMEM] * 6,
         scratch_shapes=WEIGHT_SCRATCH
         + BLOCK_SCRATCH
-        + [pltpu.VMEM((WIN * WIN, WIN * WIN), F32), WEIGHT_SEMS],
+        + [pltpu.VMEM((2, WIN * WIN, WIN * WIN), F32), WEIGHT_SEMS],
         compiler_params=pltpu.CompilerParams(vmem_limit_bytes=SHIFT_VMEM),
         cost_estimate=BLOCK_COST,
         name="shift_block",
-    )(last, mine, below, right, corner, gains, *weights)
+    )(ends, *pieces, gains, *weights)
 
 
 def moved(block, lat_step, lon_step):
@@ -388,19 +385,22 @@
     )
     arrived = lax.all_to_all(slab, ("lat", "lon"), split_axis=0, concat_axis=0, tiled=True)
     weights = (w_qkv, w_proj, w_up, w_down)
-    mine, below, right, corner = bin_block(arrived, background, norm_gain, *weights)
-    below = moved(below, -1, 0)
-    right = moved(right, 0, -1)
-    corner = moved(corner, -1, -1)
-    last = (lat == lax.axis_size("lat") - 1).astype(jnp.int32).reshape(1)
-    mine, above, left, corner = shift_block(
-        last, mine, below, right, corner, norm_gain, *weights
+    mid, edge, up, down, down_left, left = bin_block(arrived, background, norm_gain, *weights)
+    below = moved(up, -1, 0)
+    above = moved(down, 1, 0)
+    above_right = moved(down_left, 1, -1)
+    right = moved(left, 0, -1)
+    ends = jnp.where(lat == lax.axis_size("lat") - 1, 1, jnp.where(lat == 0, 2, 0))
+    ends = ends.astype(jnp.int32).reshape(1)
+    mid, edge, down, up, up_right, right = shift_block(
+        ends, (mid, edge, below, above, above_right, right), norm_gain, *weights
     )
-    above = moved(above, 1, 0)
-    left = moved(left, 0, 1)
-    corner = moved(corner, 1, 1)
-    top = jnp.concatenate([corner, above], 1)
-    bottom = jnp.concatenate([left, mine], 1)
+    above = moved(down, 1, 0)
+    below = moved(up, -1, 0)
+    below_left = moved(up_right, -1, 1)
+    left = moved(right, 0, 1)
+    top = jnp.concatenate([left, above, edge], 1)
+    bottom = jnp.concatenate([below_left, mid, below], 1)
     return jnp.concatenate([top, bottom], 0)
 
 

time: 98.8 us -> 95.3 us (0.965)
  starting transfers between devices: 3.97 us -> 9.2 us
  waiting for transfers between devices: 16.5 us -> 11.7 us
  Pallas kernels: 32.1 us -> 28.2 us
    ppermute x6 -> x8, starting transfers between devices: 3.97 us -> 9.2 us  [moved(): return lax.ppermute(block, ('lat', 'lon'), route)]
    ppermute x6 -> x8, waiting for transfers between devices: 16.5 us -> 11.7 us  [moved(): return lax.ppermute(block, ('lat', 'lon'), route)]
    pallas_call x1, Pallas kernels: 16 us -> 12.1 us  [encode(): pl.pallas_call(encode_kernel, out_shape=jax.ShapeDtypeStruct((OWNERS, SLA...]
  transfers between devices with their start and end apart: 6 -> 8, of which waited for: 4 -> 3; matrix products, arithmetic and copies ran while one was open for 0% -> 0% of each run, Pallas kernels for 0% -> 0%
where the time goes in v3:
time: 95.3 us; the launch traced here: 95.1 us
  blocking collectives  44.4 us (47%)
  Pallas kernels  28.2 us (30%)
  waiting for transfers between devices  11.7 us (12%)
  starting transfers between devices  9.2 us (10%)
    all_to_all x1, blocking collectives, on_device(): lax.all_to_all(slab, ('lat', 'lon'), split_axis=0, concat_axis=0, tiled=T...  44.4 us
    pallas_call x1, Pallas kernels, encode(): pl.pallas_call(encode_kernel, out_shape=jax.ShapeDtypeStruct((OWNERS, SLA...  12.1 us
    ppermute x8, waiting for transfers between devices, moved(): return lax.ppermute(block, ('lat', 'lon'), route)  11.7 us
    ppermute x8, starting transfers between devices, moved(): return lax.ppermute(block, ('lat', 'lon'), route)  9.2 us
    pallas_call x1, Pallas kernels, bin_block(): pl.pallas_call(bin_kernel, out_shape=PIECES, in_specs=[VMEM] * 3 + [HBM]...  8.31 us
    pallas_call x1, Pallas kernels, shift_block(): pl.pallas_call(shift_kernel, out_shape=PIECES, in_specs=[SMEM] + [VMEM] *...  7.76 us
  transfers between devices with their start and end apart: 8, of which 3 were waited for; matrix products, arithmetic and copies ran while one was open for 0% of the time, Pallas kernels for 0%

profile of v3, /device:TPU:0, one launch (start us, length us, event | category | flops | bytes accessed | tf_op | source)
XLA Modules:
  0.0 95.1 jit_solution(5532279437902477051)
XLA Ops:
  0.7 12.1 %encode.1 = bf16[128,72,128]{2,1,0:T(8,128)(2,1)} custom-call(s32[1]{0:T(128)} %bitcast.1.place, s32[1]{0:T(128)S(6)} %copy.13.count, s32[1,1024]{1,0:T(1,128)} %bitcast.4, s32[1,1024]{1,0:T(1,128)} %bitcast.5, bf16[1024,512]{1,0:T(8,128)(2,1)} %rows_hbm.1, bf16[512,2048]{1,0:T(8,128)(2,1)} %w_in_hbm.1, bf16[2048,512]{1,0:T(8,128)(2,1)} %w_out_hbm.1), custom_call_target="tpu_custom_call" | custom-call | flops 7516192768 | bytes 8388608 | tf_op jit(solution)/shard_map/encode/pallas_call | solution.py:149
  12.8 0.0 copy-start
  12.8 0.0 copy-start.1
  12.8 0.0 copy-start.2
  12.8 44.4 %all_to_all.5.arrived = bf16[128,72,128]{2,1,0:T(8,128)(2,1)S(1)} all-to-all(bf16[128,72,128]{2,1,0:T(8,128)(2,1)} %encode.1), channel_id=1, replica_groups=mesh['lat'=8,'lon'=16] {'lat','lon'}, dimensions={0} | all-to-all | bytes 4718592 | tf_op jit(solution)/shard_map/all_to_all | solution.py:386
  57.2 8.3 %bin_block.1 = (bf16[8,16,512]{2,1,0:T(8,128)(2,1)S(1)}, bf16[8,8,512]{2,1,0:T(8,128)(2,1)S(1)}, bf16[8,16,512]{2,1,0:T(8,128)(2,1)S(1)}, bf16[8,8,512]{2,1,0:T(...) custom-call(bf16[128,72,128]{2,1,0:T(8,128)(2,1)S(1)} %all_to_all.5.arrived, ...), custom_call_target="tpu_custom_call" | custom-call | flops 4294967296 | bytes 8388608 | tf_op jit(solution)/shard_map/bin_block/pallas_call | solution.py:285
  65.5 1.5 %collective-permute-start = (bf16[8,16,512]{2,1,0:T(8,128)(2,1)S(1)}, bf16[8,16,512]{2,1,0:T(8,128)(2,1)S(1)}, u32[]{:S(2)}, u32[]{:S(2)}) collective-permute-start(bf16[8,16,512]{2,1,0:T(8,128)(2,1)S(1)} %get-tuple-element.19), channel_id=1, source_target_pairs={{0,112},{1,113},{2,114},{3,115},{4,116},{5,117},{6,118},{7,119},{8... | collective-permute-start | bytes 393224 | tf_op jit(solution)/shard_map/ppermute | solution.py:358
  67.0 0.6 collective-permute-start.1
  67.6 0.0 collective-permute-start.2
  67.6 0.5 collective-permute-start.3
  68.1 7.4 %collective-permute-done.1.above = bf16[8,8,512]{2,1,0:T(8,128)(2,1)S(1)} collective-permute-done((bf16[8,8,512]{2,1,0:T(8,128)(2,1)S(1)}, bf16[8,8,512]{2,1,0:T(8,128)(2,1)S(1)}, u32[]{:S(2)}, u32[]{:S(2)}) %collective-permute-start.1) | collective-permute-done | bytes 65568 | tf_op jit(solution)/shard_map/ppermute | solution.py:358
  75.5 0.0 collective-permute-done.2.above_right
  75.6 0.0 collective-permute-done.3.right
  75.6 0.0 collective-permute-done.below
  75.6 7.8 %shift_block.1 = (bf16[8,16,512]{2,1,0:T(8,128)(2,1)S(1)}, bf16[8,8,512]{2,1,0:T(8,128)(2,1)S(1)}, bf16[8,16,512]{2,1,0:T(8,128)(2,1)S(1)}, bf16[8,8,512]{2,1,0:...) custom-call(s32[1]{0:T(128)} %bitcast.ends, ...), custom_call_target="tpu_custom_call" | custom-call | flops 4294967296 | bytes 8388608 | tf_op jit(solution)/shard_map/shift_block/pallas_call | solution.py:333
  83.3 0.1 collective-permute-start.5
  83.4 0.1 collective-permute-start.4
  83.5 6.4 %collective-permute-start.6 = (bf16[8,8,512]{2,1,0:T(8,128)(2,1)S(1)}, bf16[8,8,512]{2,1,0:T(8,128)(2,1)S(1)}, u32[]{:S(2)}, u32[]{:S(2)}) collective-permute-start(bf16[8,8,512]{2,1,0:T(8,128)(2,1)S(1)} %get-tuple-element.26), channel_id=1, source_target_pairs={{0,113},{1,114},{2,115},{3,116},{4,117},{5,118},{6,119},{7,120},{8... | collective-permute-start | bytes 196616 | tf_op jit(solution)/shard_map/ppermute | solution.py:358
  89.9 0.0 collective-permute-start.7
  89.9 0.0 collective-permute-done.4
  89.9 1.9 %collective-permute-done.6 = bf16[8,8,512]{2,1,0:T(8,128)(2,1)S(1)} collective-permute-done((bf16[8,8,512]{2,1,0:T(8,128)(2,1)S(1)}, bf16[8,8,512]{2,1,0:T(8,128)(2,1)S(1)}, u32[]{:S(2)}, u32[]{:S(2)}) %collective-permute-start.6) | collective-permute-done | bytes 65568 | tf_op jit(solution)/shard_map/ppermute | solution.py:358
  91.9 2.4 %collective-permute-done.7 = bf16[8,8,512]{2,1,0:T(8,128)(2,1)S(1)} collective-permute-done((bf16[8,8,512]{2,1,0:T(8,128)(2,1)S(1)}, bf16[8,8,512]{2,1,0:T(8,128)(2,1)S(1)}, u32[]{:S(2)}, u32[]{:S(2)}) %collective-permute-start.7) | collective-permute-done | bytes 65568 | tf_op jit(solution)/shard_map/ppermute | solution.py:358
  94.2 0.0 collective-permute-done.5
  94.2 0.9 maximum_maximum_fusion
  (3 shorter events, 0.0 us)
Async XLA Ops:
  12.8 44.4 %copy-start = (bf16[2,512,512]{2,1,0:T(8,128)(2,1)S(1)}, bf16[2,512,512]{2,1,0:T(8,128)(2,1)}, u32[]{:S(2)}) copy-start(bf16[2,512,512]{2,1,0:T(8,128)(2,1)} %wp.3) | copy-start | bytes 3145732
  12.8 44.4 %copy-start.1 = (bf16[16,32,512]{2,1,0:T(8,128)(2,1)S(1)}, bf16[16,32,512]{2,1,0:T(8,128)(2,1)}, u32[]{:S(2)}) copy-start(bf16[16,32,512]{2,1,0:T(8,128)(2,1)} %background.1) | copy-start | bytes 1572868
  12.8 44.4 %copy-start.2 = (f32[2,2,512]{2,1,0:T(2,128)S(1)}, f32[2,2,512]{2,1,0:T(2,128)}, u32[]{:S(2)}) copy-start(f32[2,2,512]{2,1,0:T(2,128)} %gains.3) | copy-start | bytes 24580
  65.5 10.1 %collective-permute-start = (bf16[8,16,512]{2,1,0:T(8,128)(2,1)S(1)}, bf16[8,16,512]{2,1,0:T(8,128)(2,1)S(1)}, u32[]{:S(2)}, u32[]{:S(2)}) collective-permute-start(bf16[8,16,512]{2,1,0:T(8,128)(2,1)S(1)} %get-tuple-element.19), channel_id=1, source_target_pairs={{0,112},{1,113},{2,114},{3,115},{4,116},{5,117},{6,118},{7,119},{8... | collective-permute-start | bytes 393224 | tf_op jit(solution)/shard_map/ppermute | solution.py:358
  67.0 8.5 %collective-permute-start.1 = (bf16[8,8,512]{2,1,0:T(8,128)(2,1)S(1)}, bf16[8,8,512]{2,1,0:T(8,128)(2,1)S(1)}, u32[]{:S(2)}, u32[]{:S(2)}) collective-permute-start(bf16[8,8,512]{2,1,0:T(8,128)(2,1)S(1)} %get-tuple-element.20), channel_id=1, source_target_pairs={{0,16},{1,17},{2,18},{3,19},{4,20},{5,21},{6,22},{7,23},{8,24},{9,... | collective-permute-start | bytes 196616 | tf_op jit(solution)/shard_map/ppermute | solution.py:358
  67.6 8.0 %collective-permute-start.2 = (bf16[8,8,512]{2,1,0:T(8,128)(2,1)S(1)}, bf16[8,8,512]{2,1,0:T(8,128)(2,1)S(1)}, u32[]{:S(2)}, u32[]{:S(2)}) collective-permute-start(bf16[8,8,512]{2,1,0:T(8,128)(2,1)S(1)} %get-tuple-element.21), channel_id=1, source_target_pairs={{0,31},{1,16},{2,17},{3,18},{4,19},{5,20},{6,21},{7,22},{8,23},{9,... | collective-permute-start | bytes 196616 | tf_op jit(solution)/shard_map/ppermute | solution.py:358
  67.6 8.0 %collective-permute-start.3 = (bf16[8,8,512]{2,1,0:T(8,128)(2,1)S(1)}, bf16[8,8,512]{2,1,0:T(8,128)(2,1)S(1)}, u32[]{:S(2)}, u32[]{:S(2)}) collective-permute-start(bf16[8,8,512]{2,1,0:T(8,128)(2,1)S(1)} %get-tuple-element.22), channel_id=1, source_target_pairs={{0,15},{1,0},{2,1},{3,2},{4,3},{5,4},{6,5},{7,6},{8,7},{9,8},{10,9... | collective-permute-start | bytes 196616 | tf_op jit(solution)/shard_map/ppermute | solution.py:358
  83.3 10.9 %collective-permute-start.5 = (bf16[8,16,512]{2,1,0:T(8,128)(2,1)S(1)}, bf16[8,16,512]{2,1,0:T(8,128)(2,1)S(1)}, u32[]{:S(2)}, u32[]{:S(2)}) collective-permute-start(bf16[8,16,512]{2,1,0:T(8,128)(2,1)S(1)} %get-tuple-element.24), channel_id=1, source_target_pairs={{0,16},{1,17},{2,18},{3,19},{4,20},{5,21},{6,22},{7,23},{8,24},{9,... | collective-permute-start | bytes 393224 | tf_op jit(solution)/shard_map/ppermute | solution.py:358
  83.4 6.5 %collective-permute-start.4 = (bf16[8,8,512]{2,1,0:T(8,128)(2,1)S(1)}, bf16[8,8,512]{2,1,0:T(8,128)(2,1)S(1)}, u32[]{:S(2)}, u32[]{:S(2)}) collective-permute-start(bf16[8,8,512]{2,1,0:T(8,128)(2,1)S(1)} %get-tuple-element.23), channel_id=1, source_target_pairs={{0,1},{1,2},{2,3},{3,4},{4,5},{5,6},{6,7},{7,8},{8,9},{9,10},{10,1... | collective-permute-start | bytes 196616 | tf_op jit(solution)/shard_map/ppermute | solution.py:358
  83.5 8.3 %collective-permute-start.6 = (bf16[8,8,512]{2,1,0:T(8,128)(2,1)S(1)}, bf16[8,8,512]{2,1,0:T(8,128)(2,1)S(1)}, u32[]{:S(2)}, u32[]{:S(2)}) collective-permute-start(bf16[8,8,512]{2,1,0:T(8,128)(2,1)S(1)} %get-tuple-element.26), channel_id=1, source_target_pairs={{0,113},{1,114},{2,115},{3,116},{4,117},{5,118},{6,119},{7,120},{8... | collective-permute-start | bytes 196616 | tf_op jit(solution)/shard_map/ppermute | solution.py:358
  89.9 4.3 %collective-permute-start.7 = (bf16[8,8,512]{2,1,0:T(8,128)(2,1)S(1)}, bf16[8,8,512]{2,1,0:T(8,128)(2,1)S(1)}, u32[]{:S(2)}, u32[]{:S(2)}) collective-permute-start(bf16[8,8,512]{2,1,0:T(8,128)(2,1)S(1)} %get-tuple-element.28), channel_id=1, source_target_pairs={{0,112},{1,113},{2,114},{3,115},{4,116},{5,117},{6,118},{7,119},{8... | collective-permute-start | bytes 196616 | tf_op jit(solution)/shard_map/ppermute | solution.py:358

commit v4 on v2

--- a/solution.py
+++ b/solution.py
@@ -19,11 +19,16 @@
 LANES = 128
 SLAB = 4 * CAP + 8
 BLK = 256
-TILE = 512
+TILE = 1024
+ENC_TILES = (1024, 1024)
+AHEAD = 5
+ENC = 1024
+PUT = 1024
 EPS = 1e-5
 ENCODE_VMEM = 67043328 - (100 << 10)
 BIN_VMEM = (64 << 20) - (16000 << 10)
-SHIFT_VMEM = (64 << 20) - (12000 << 10)
+SHIFT_VMEM = 16 << 20
+FETCH_VMEM = (64 << 20) - (18500 << 10)
 BF = jnp.bfloat16
 F32 = jnp.float32
 VMEM = pl.BlockSpec(memory_space=pltpu.VMEM)
@@ -61,19 +66,20 @@
     place, count, dest, token, rows_hbm, w_in_hbm, w_out_hbm, slab_hbm,
     rows, w_in, w_out, slab, encoded, total, slots, in_sems, out_sems,
 ):
-    tiles = FF // TILE
-    rows_copy = pltpu.make_async_copy(rows_hbm, rows, in_sems.at[2 * tiles])
-    w_in_copies = []
-    w_out_copies = []
-    for t in range(tiles):
-        f = slice(t * TILE, (t + 1) * TILE)
-        w_in_copies.append(pltpu.make_async_copy(w_in_hbm.at[:, f], w_in.at[:, f], in_sems.at[t]))
-        w_out_copies.append(
-            pltpu.make_async_copy(w_out_hbm.at[f, :], w_out.at[f, :], in_sems.at[tiles + t])
-        )
-    rows_copy.start()
-    w_in_copies[0].start()
-    w_out_copies[0].start()
+    copies = [pltpu.make_async_copy(rows_hbm, rows, in_sems.at[0])]
+    spans = []
+    for t, width in enumerate(ENC_TILES):
+        f = slice(sum(ENC_TILES[:t]), sum(ENC_TILES[: t + 1]))
+        spans.append(f)
+        copies.append(pltpu.make_async_copy(w_in_hbm.at[:, f], w_in.at[:, f], in_sems.at[2 * t + 1]))
+        copies.append(pltpu.make_async_copy(w_out_hbm.at[f, :], w_out.at[f, :], in_sems.at[2 * t + 2]))
+    for copy in copies[:AHEAD]:
+        copy.start()
+
+    def arrive(i):
+        copies[i].wait()
+        if i + AHEAD < len(copies):
+            copies[i + AHEAD].start()
 
     live_count = count[0]
     lane_base = (place[0] % 8) * CAP
@@ -103,36 +109,32 @@
     sub = iota((OWNERS, 8, LANES), 1)
     marks = jnp.where(sub == 0, high[:, None, :], jnp.where(sub == 1, low[:, None, :], 0.0))
     slab[:, 4 * CAP : SLAB, :] = marks.astype(BF)
-    rows_copy.wait()
-    for t in range(tiles):
-        w_in_copies[t].wait()
-        w_out_copies[t].wait()
-        if t + 1 < tiles:
-            w_in_copies[t + 1].start()
-            w_out_copies[t + 1].start()
-        f = slice(t * TILE, (t + 1) * TILE)
+    arrive(0)
+    for t, f in enumerate(spans):
+        arrive(2 * t + 1)
+        arrive(2 * t + 2)
 
         def encode_block(b, _):
-            r = pl.ds(pl.multiple_of(b * BLK, BLK), BLK)
+            r = pl.ds(pl.multiple_of(b * ENC, ENC), ENC)
             hidden = gelu(dot(rows[r, :], w_in[:, f])).astype(BF)
             part = dot(hidden, w_out[f, :])
             if t > 0:
                 part = total[r, :] + part
-            if t + 1 < tiles:
+            if t + 1 < len(spans):
                 total[r, :] = part
             else:
                 encoded[r, :] = part.astype(BF)
             return 0
 
-        lax.fori_loop(0, OBS_DEV // BLK, encode_block, 0)
-    step = BLK // CAP
+        lax.fori_loop(0, OBS_DEV // ENC, encode_block, 0)
+    step = PUT // CAP
 
     def slab_copy(b):
         d = pl.ds(b * step, step)
         return pltpu.make_async_copy(slab.at[d], slab_hbm.at[d], out_sems.at[b])
 
     def place_block(b, _):
-        wanted = iota((BLK, OBS_DEV), 0) + b * BLK
+        wanted = iota((PUT, OBS_DEV), 0) + b * PUT
         pick = jnp.where(slots[...] == wanted, 1.0, 0.0).astype(BF)
         moved = dot(pick, encoded[...]).astype(BF).reshape(step, CAP, D)
         d = pl.ds(b * step, step)
@@ -160,8 +162,8 @@
             pltpu.VMEM((OBS_DEV, D), BF),
             pltpu.VMEM((OBS_DEV, D), F32),
             pltpu.VMEM((1, OBS_DEV), jnp.int32),
-            pltpu.SemaphoreType.DMA((2 * FF // TILE + 1,)),
-            pltpu.SemaphoreType.DMA((OWNERS * CAP // BLK,)),
+            pltpu.SemaphoreType.DMA((2 * len(ENC_TILES) + 1,)),
+            pltpu.SemaphoreType.DMA((OWNERS * CAP // PUT,)),
         ],
         compiler_params=pltpu.CompilerParams(vmem_limit_bytes=ENCODE_VMEM),
         cost_estimate=pl.CostEstimate(
@@ -174,7 +176,11 @@
 def weight_copies(layer, hbm, vmem, sems):
     w_qkv, w_proj, w_up, w_down = hbm
     v_qkv, v_proj, v_up, v_down = vmem
-    pairs = [(w_qkv.at[layer], v_qkv), (w_proj.at[layer], v_proj)]
+    pairs = []
+    for part in range(3):
+        c = slice(part * D, (part + 1) * D)
+        pairs.append((w_qkv.at[layer, :, c], v_qkv.at[:, c]))
+    pairs.append((w_proj.at[layer], v_proj))
     for t in range(FF // TILE):
         f = slice(t * TILE, (t + 1) * TILE)
         pairs.append((w_up.at[layer, :, f], v_up.at[:, f]))
@@ -182,15 +188,42 @@
     return [pltpu.make_async_copy(a, b, sems.at[i]) for i, (a, b) in enumerate(pairs)]
 
 
+def fetch_kernel(after, wq, wp, wu, wd, vq, vp, vu, vd, sems):
+    copies = []
+    for i, (a, b) in enumerate(((wq, vq), (wp, vp), (wu, vu), (wd, vd))):
+        copies.append(pltpu.make_async_copy(a.at[1], b, sems.at[i]))
+        copies[-1].start()
+    for copy in copies:
+        copy.wait()
+
+
+def fetch(after, *arrays):
+    size = sum(a.size * a.dtype.itemsize for a in arrays)
+    return pl.pallas_call(
+        fetch_kernel,
+        out_shape=[jax.ShapeDtypeStruct(a.shape[1:], a.dtype) for a in arrays],
+        in_specs=[HBM] * 5,
+        out_specs=[VMEM] * 4,
+        scratch_shapes=[pltpu.SemaphoreType.DMA((4,))],
+        compiler_params=pltpu.CompilerParams(vmem_limit_bytes=FETCH_VMEM),
+        cost_estimate=pl.CostEstimate(flops=0, transcendentals=0, bytes_accessed=2 * size),
+        name="fetch",
+    )(after, *arrays)
+
+
 def block_body(layer, x, bias, gains, weights, copies, qkv, mixed):
     w_qkv, w_proj, w_up, w_down = weights
     count = x.shape[0]
     area = WIN * WIN
     h = normed(x, gains[layer, 0:1, :])
-    copies[0].wait()
-    for copy in copies[1:]:
+    for part in range(3):
+        c = slice(part * D, (part + 1) * D)
+        if copies:
+            copies[part].wait()
+            copies[part + 3].start()
+        qkv[:, c] = dot(h, w_qkv[:, c]).astype(BF)
+    for copy in copies[6:]:
         copy.start()
-    qkv[...] = dot(h, w_qkv[...]).astype(BF)
     first = iota((area, LANES), 1) < 64
     ones = jnp.ones((area, LANES), BF)
     for w in range(count // area):
@@ -210,24 +243,28 @@
                 both = dot(probs, v)
                 out.append(both[:, :LANES] / both[:, LANES:])
             mixed[r, c : c + LANES] = jnp.where(first, out[0], out[1]).astype(BF)
-    copies[1].wait()
+    if copies:
+        copies[3].wait()
     attended = x + dot(mixed[...], w_proj[...])
     h = normed(attended, gains[layer, 1:2, :])
     total = attended
     for t in range(FF // TILE):
-        copies[2 * t + 2].wait()
-        copies[2 * t + 3].wait()
+        if copies:
+            copies[2 * t + 4].wait()
+            copies[2 * t + 5].wait()
         f = slice(t * TILE, (t + 1) * TILE)
         total = total + dot(gelu(dot(h, w_up[:, f])).astype(BF), w_down[f, :])
     return total.astype(BF)
 
 
 def bin_kernel(
-    arrived, background, gains, wq, wp, wu, wd, keep, below, right, corner,
+    arrived, background, gains, wq, wp, wu, wd,
+    keep, below, right, corner,
     lined, pick, vq, vp, vu, vd, qkv, mixed, state, sems,
 ):
     copies = weight_copies(0, (wq, wp, wu, wd), (vq, vp, vu, vd), sems)
-    copies[0].start()
+    for copy in copies[:3]:
+        copy.start()
     for k in range(4):
         lined[:, k * LANES : (k + 1) * LANES] = arrived[:, k * CAP : (k + 1) * CAP, :].reshape(
             OWNERS * CAP, LANES
@@ -267,19 +304,16 @@
     pltpu.VMEM((D, FF), BF),
     pltpu.VMEM((FF, D), BF),
 ]
-WEIGHT_SEMS = pltpu.SemaphoreType.DMA((2 + 2 * FF // TILE,))
+WEIGHT_SEMS = pltpu.SemaphoreType.DMA((4 + 2 * FF // TILE,))
 BLOCK_SCRATCH = [
     pltpu.VMEM((CELLS, 3 * D), BF),
     pltpu.VMEM((CELLS, D), BF),
     pltpu.VMEM((CELLS, D), F32),
 ]
 BLOCK_COST = pl.CostEstimate(flops=4 << 30, transcendentals=2 << 20, bytes_accessed=8 << 20)
-PIECES = (
-    jax.ShapeDtypeStruct((HALF, CLON - HALF, D), BF),
-    jax.ShapeDtypeStruct((HALF, CLON - HALF, D), BF),
-    jax.ShapeDtypeStruct((HALF, HALF, D), BF),
-    jax.ShapeDtypeStruct((HALF, HALF, D), BF),
-)
+WIDE = jax.ShapeDtypeStruct((HALF, CLON - HALF, D), BF)
+NARROW = jax.ShapeDtypeStruct((HALF, HALF, D), BF)
+PIECES = (WIDE, WIDE, NARROW, NARROW)
 
 
 def bin_block(arrived, background, gains, *weights):
@@ -302,26 +336,22 @@
 
 
 def shift_kernel(
-    last, mine, below, right, corner, gains, wq, wp, wu, wd, keep, above, left, diagonal,
-    vq, vp, vu, vd, qkv, mixed, state, bias, sems,
+    last, mine, below, right, corner, gains, wq, wp, wu, wd,
+    keep, above, left, diagonal, qkv, mixed, state, bias,
 ):
-    copies = weight_copies(1, (wq, wp, wu, wd), (vq, vp, vu, vd), sems)
-    copies[0].start()
     area = WIN * WIN
-    split = (iota((area, area), 0) < area // 2) != (iota((area, area), 1) < area // 2)
+    h = area // 2
+    split = (iota((area, area), 0) < h) != (iota((area, area), 1) < h)
     bias[...] = jnp.where(split & (last[0] == 1), -1e30, 0.0)
     top = mine[...].astype(F32)
     bottom = below[...].astype(F32)
-    h = area // 2
     state[0:h, :] = top[:, :WIN, :].reshape(h, D)
     state[h : 2 * h, :] = bottom[:, :WIN, :].reshape(h, D)
     top = jnp.concatenate([top[:, WIN:, :], right[...].astype(F32)], 1)
     bottom = jnp.concatenate([bottom[:, WIN:, :], corner[...].astype(F32)], 1)
     state[2 * h : 3 * h, :] = top.reshape(h, D)
     state[3 * h : 4 * h, :] = bottom.reshape(h, D)
-    done = block_body(
-        1, state[...], bias[...], gains, (vq, vp, vu, vd), copies, qkv, mixed
-    )
+    done = block_body(1, state[...], bias[...], gains, (wq, wp, wu, wd), (), qkv, mixed)
     one = done[:BLK].reshape(WIN, WIN, D)
     two = done[BLK:].reshape(WIN, WIN, D)
     diagonal[...] = two[HALF:, HALF:]
@@ -332,19 +362,17 @@
     keep[:, WIN:, :] = two[:HALF, :HALF]
 
 
-def shift_block(last, mine, below, right, corner, gains, *weights):
+def shift_block(last, pieces, gains, *weights):
     return pl.pallas_call(
         shift_kernel,
         out_shape=PIECES,
-        in_specs=[SMEM] + [VMEM] * 5 + [HBM] * 4,
+        in_specs=[SMEM] + [VMEM] * 9,
         out_specs=[VMEM] * 4,
-        scratch_shapes=WEIGHT_SCRATCH
-        + BLOCK_SCRATCH
-        + [pltpu.VMEM((WIN * WIN, WIN * WIN), F32), WEIGHT_SEMS],
+        scratch_shapes=BLOCK_SCRATCH + [pltpu.VMEM((WIN * WIN, WIN * WIN), F32)],
         compiler_params=pltpu.CompilerParams(vmem_limit_bytes=SHIFT_VMEM),
         cost_estimate=BLOCK_COST,
         name="shift_block",
-    )(last, mine, below, right, corner, gains, *weights)
+    )(last, *pieces, gains, *weights)
 
 
 def moved(block, lat_step, lon_step):
@@ -389,13 +417,12 @@
     arrived = lax.all_to_all(slab, ("lat", "lon"), split_axis=0, concat_axis=0, tiled=True)
     weights = (w_qkv, w_proj, w_up, w_down)
     mine, below, right, corner = bin_block(arrived, background, norm_gain, *weights)
+    late = fetch(mine, *weights)
     below = moved(below, -1, 0)
     right = moved(right, 0, -1)
     corner = moved(corner, -1, -1)
     last = (lat == lax.axis_size("lat") - 1).astype(jnp.int32).reshape(1)
-    mine, above, left, corner = shift_block(
-        last, mine, below, right, corner, norm_gain, *weights
-    )
+    mine, above, left, corner = shift_block(last, (mine, below, right, corner), norm_gain, *late)
     above = moved(above, 1, 0)
     left = moved(left, 0, 1)
     corner = moved(corner, 1, 1)

time: 98.8 us -> 91.9 us (0.930)
  Pallas kernels: 32.1 us -> 28 us
  waiting for transfers between devices: 16.5 us -> 13.8 us
    pallas_call x1, Pallas kernels: 16 us -> 11 us  [encode(): pl.pallas_call(encode_kernel, out_shape=jax.ShapeDtypeStruct((OWNERS, SLA...]
    ppermute x6, waiting for transfers between devices: 16.5 us -> 13.8 us  [moved(): return lax.ppermute(block, ('lat', 'lon'), route)]
    pallas_call x0 -> x1, Pallas kernels: none -> 2.75 us  [fetch(): pl.pallas_call(fetch_kernel, out_shape=[jax.ShapeDtypeStruct(a.shape[1:],...]
    pallas_call x1, Pallas kernels: 7.71 us -> 5.78 us  [shift_block(): pl.pallas_call(shift_kernel, out_shape=PIECES, in_specs=[SMEM] + [VMEM] *...]
  transfers between devices with their start and end apart: 6 -> 6, of which waited for: 4 -> 4; matrix products, arithmetic and copies ran while one was open for 0% -> 0% of each run, Pallas kernels for 0% -> 3%
where the time goes in v4:
time: 91.9 us; the launch traced here: 91.7 us
  blocking collectives  44.4 us (48%)
  Pallas kernels  28 us (30%)
  waiting for transfers between devices  13.8 us (15%)
  starting transfers between devices  4.01 us (4%)
    all_to_all x1, blocking collectives, on_device(): lax.all_to_all(slab, ('lat', 'lon'), split_axis=0, concat_axis=0, tiled=T...  44.4 us
    ppermute x6, waiting for transfers between devices, moved(): return lax.ppermute(block, ('lat', 'lon'), route)  13.8 us
    pallas_call x1, Pallas kernels, encode(): pl.pallas_call(encode_kernel, out_shape=jax.ShapeDtypeStruct((OWNERS, SLA...  11 us
    pallas_call x1, Pallas kernels, bin_block(): pl.pallas_call(bin_kernel, out_shape=PIECES, in_specs=[VMEM] * 3 + [HBM]...  8.44 us
    pallas_call x1, Pallas kernels, shift_block(): pl.pallas_call(shift_kernel, out_shape=PIECES, in_specs=[SMEM] + [VMEM] *...  5.78 us
    ppermute x6, starting transfers between devices, moved(): return lax.ppermute(block, ('lat', 'lon'), route)  4.01 us
    pallas_call x1, Pallas kernels, fetch(): pl.pallas_call(fetch_kernel, out_shape=[jax.ShapeDtypeStruct(a.shape[1:],...  2.75 us
  transfers between devices with their start and end apart: 6, of which 4 were waited for; matrix products, arithmetic and copies ran while one was open for 0% of the time, Pallas kernels for 3%

profile of v4, /device:TPU:0, one launch (start us, length us, event | category | flops | bytes accessed | tf_op | source)
XLA Modules:
  0.0 91.7 jit_solution(13433416065255956921)
XLA Ops:
  0.7 11.0 %encode.1 = bf16[128,72,128]{2,1,0:T(8,128)(2,1)} custom-call(s32[1]{0:T(128)} %bitcast.1.place, s32[1]{0:T(128)S(6)} %copy.13.count, s32[1,1024]{1,0:T(1,128)} %bitcast.4, s32[1,1024]{1,0:T(1,128)} %bitcast.5, bf16[1024,512]{1,0:T(8,128)(2,1)} %rows_hbm.1, bf16[512,2048]{1,0:T(8,128)(2,1)} %w_in_hbm.1, bf16[2048,512]{1,0:T(8,128)(2,1)} %w_out_hbm.1), custom_call_target="tpu_custom_call" | custom-call | flops 7516192768 | bytes 8388608 | tf_op jit(solution)/shard_map/encode/pallas_call | solution.py:152
  11.7 0.0 copy-start
  11.7 0.0 copy-start.1
  11.7 0.0 copy-start.2
  11.7 44.4 %all_to_all.5.arrived = bf16[128,72,128]{2,1,0:T(8,128)(2,1)S(1)} all-to-all(bf16[128,72,128]{2,1,0:T(8,128)(2,1)} %encode.1), channel_id=1, replica_groups=mesh['lat'=8,'lon'=16] {'lat','lon'}, dimensions={0} | all-to-all | bytes 4718592 | tf_op jit(solution)/shard_map/all_to_all | solution.py:417
  56.0 0.0 copy-done
  56.0 0.0 copy-done.1
  56.1 0.0 copy-done.2
  56.1 8.4 %bin_block.1 = (bf16[8,24,512]{2,1,0:T(8,128)(2,1)S(1)}, bf16[8,24,512]{2,1,0:T(8,128)(2,1)S(1)}, bf16[8,8,512]{2,1,0:T(8,128)(2,1)S(1)}, bf16[8,8,512]{2,1,0:T(8,128)(2,1)S(1)}) custom-call(bf16[128,72,128]{2,1,0:T(8,128)(2,1)S(1)} %all_to_all.5.arrived, bf16[16,32,512]{2,1,0:T(8,128)(2,1)S(1)} %copy-done.1, f32[2,2,512]{2,1,0:T(2,128)S(1)} %copy-done.2, ...), custom_call_target="tpu_custom_call" | custom-call | flops 4294967296 | bytes 8388608 | tf_op jit(solution)/shard_map/bin_block/pallas_call | solution.py:320
  64.5 1.5 %collective-permute-start = (bf16[8,24,512]{2,1,0:T(8,128)(2,1)S(1)}, bf16[8,24,512]{2,1,0:T(8,128)(2,1)S(1)}, u32[]{:S(2)}, u32[]{:S(2)}) collective-permute-start(bf16[8,24,512]{2,1,0:T(8,128)(2,1)S(1)} %get-tuple-element.18), channel_id=1, source_target_pairs={{0,112},{1,113},{2,114},{3,115},{4,116},{5,117},{6,118},{7,119},{8... | collective-permute-start | bytes 589832 | tf_op jit(solution)/shard_map/ppermute | solution.py:389
  66.0 0.6 collective-permute-start.1
  66.6 0.5 collective-permute-start.2
  67.1 2.7 %fetch.1 = (bf16[512,1536]{1,0:T(8,128)(2,1)S(1)}, bf16[512,512]{1,0:T(8,128)(2,1)S(1)}, bf16[512,2048]{1,0:T(8,128)(2,1)S(1)}, bf16[2048,512]{1,0:T(8,128)(2,1)S(1)}) custom-call(bf16[8,24,512]{2,1,0:T(8,128)(2,1)S(1)} %get-tuple-element.17.after.mine, bf16[2,512,1536]{2,1,0:T(8,128)(2,1)} %wq.3, bf16[2,512,512]{2,1,0:T(8,128)(2,1)S(1)} %copy-done, ...), custom_call_target="tpu_custom_call" | custom-call | bytes 25165824 | tf_op jit(solution)/shard_map/fetch/pallas_call | solution.py:202
  69.8 1.2 %collective-permute-done.1.right = bf16[8,8,512]{2,1,0:T(8,128)(2,1)S(1)} collective-permute-done((bf16[8,8,512]{2,1,0:T(8,128)(2,1)S(1)}, bf16[8,8,512]{2,1,0:T(8,128)(2,1)S(1)}, u32[]{:S(2)}, u32[]{:S(2)}) %collective-permute-start.1) | collective-permute-done | bytes 65568 | tf_op jit(solution)/shard_map/ppermute | solution.py:389
  71.0 0.6 collective-permute-done.2.corner
  71.7 0.4 collective-permute-done.below
  72.0 5.8 %shift_block.1 = (bf16[8,24,512]{2,1,0:T(8,128)(2,1)S(1)}, bf16[8,24,512]{2,1,0:T(8,128)(2,1)S(1)}, bf16[8,8,512]{2,1,0:T(8,128)(2,1)S(1)}, bf16[8,8,512]{2,1,0:T(8,128)(2,1)S(1)}) custom-call(s32[1]{0:T(128)} %bitcast.last, bf16[8,24,512]{2,1,0:T(8,128)(2,1)S(1)} %get-tuple-element.17.after.mine, bf16[8,24,512]{2,1,0:T(8,128)(2,1)S(1)} %collective-permute-done.below, ...), custom_call_target="tpu_custom_call" | custom-call | flops 4294967296 | bytes 8388608 | tf_op jit(solution)/shard_map/shift_block/pallas_call | solution.py:366
  77.8 0.1 collective-permute-start.4
  77.9 0.1 collective-permute-start.3
  78.0 1.3 %collective-permute-start.5 = (bf16[8,8,512]{2,1,0:T(8,128)(2,1)S(1)}, bf16[8,8,512]{2,1,0:T(8,128)(2,1)S(1)}, u32[]{:S(2)}, u32[]{:S(2)}) collective-permute-start(bf16[8,8,512]{2,1,0:T(8,128)(2,1)S(1)} %get-tuple-element.27), channel_id=1, source_target_pairs={{0,1},{1,2},{2,3},{3,4},{4,5},{5,6},{6,7},{7,8},{8,9},{9,10},{10,1... | collective-permute-start | bytes 196616 | tf_op jit(solution)/shard_map/ppermute | solution.py:389
  79.3 11.6 %collective-permute-done.3 = bf16[8,8,512]{2,1,0:T(8,128)(2,1)S(1)} collective-permute-done((bf16[8,8,512]{2,1,0:T(8,128)(2,1)S(1)}, bf16[8,8,512]{2,1,0:T(8,128)(2,1)S(1)}, u32[]{:S(2)}, u32[]{:S(2)}) %collective-permute-start.3) | collective-permute-done | bytes 65568 | tf_op jit(solution)/shard_map/ppermute | solution.py:389
  90.8 0.0 collective-permute-done.5
  90.8 0.0 collective-permute-done.4
  90.8 0.8 maximum_maximum_fusion
Async XLA Ops:
  11.7 44.4 %copy-start = (bf16[2,512,512]{2,1,0:T(8,128)(2,1)S(1)}, bf16[2,512,512]{2,1,0:T(8,128)(2,1)}, u32[]{:S(2)}) copy-start(bf16[2,512,512]{2,1,0:T(8,128)(2,1)} %wp.3) | copy-start | bytes 3145732
  11.7 44.4 %copy-start.1 = (bf16[16,32,512]{2,1,0:T(8,128)(2,1)S(1)}, bf16[16,32,512]{2,1,0:T(8,128)(2,1)}, u32[]{:S(2)}) copy-start(bf16[16,32,512]{2,1,0:T(8,128)(2,1)} %background.1) | copy-start | bytes 1572868
  11.7 44.4 %copy-start.2 = (f32[2,2,512]{2,1,0:T(2,128)S(1)}, f32[2,2,512]{2,1,0:T(2,128)}, u32[]{:S(2)}) copy-start(f32[2,2,512]{2,1,0:T(2,128)} %gains.3) | copy-start | bytes 24580
  64.5 7.5 %collective-permute-start = (bf16[8,24,512]{2,1,0:T(8,128)(2,1)S(1)}, bf16[8,24,512]{2,1,0:T(8,128)(2,1)S(1)}, u32[]{:S(2)}, u32[]{:S(2)}) collective-permute-start(bf16[8,24,512]{2,1,0:T(8,128)(2,1)S(1)} %get-tuple-element.18), channel_id=1, source_target_pairs={{0,112},{1,113},{2,114},{3,115},{4,116},{5,117},{6,118},{7,119},{8... | collective-permute-start | bytes 589832 | tf_op jit(solution)/shard_map/ppermute | solution.py:389
  66.0 5.0 %collective-permute-start.1 = (bf16[8,8,512]{2,1,0:T(8,128)(2,1)S(1)}, bf16[8,8,512]{2,1,0:T(8,128)(2,1)S(1)}, u32[]{:S(2)}, u32[]{:S(2)}) collective-permute-start(bf16[8,8,512]{2,1,0:T(8,128)(2,1)S(1)} %get-tuple-element.19), channel_id=1, source_target_pairs={{0,15},{1,0},{2,1},{3,2},{4,3},{5,4},{6,5},{7,6},{8,7},{9,8},{10,9... | collective-permute-start | bytes 196616 | tf_op jit(solution)/shard_map/ppermute | solution.py:389
  66.6 5.1 %collective-permute-start.2 = (bf16[8,8,512]{2,1,0:T(8,128)(2,1)S(1)}, bf16[8,8,512]{2,1,0:T(8,128)(2,1)S(1)}, u32[]{:S(2)}, u32[]{:S(2)}) collective-permute-start(bf16[8,8,512]{2,1,0:T(8,128)(2,1)S(1)} %get-tuple-element.20), channel_id=1, source_target_pairs={{0,127},{1,112},{2,113},{3,114},{4,115},{5,116},{6,117},{7,118},{8... | collective-permute-start | bytes 196616 | tf_op jit(solution)/shard_map/ppermute | solution.py:389
  77.8 13.0 %collective-permute-start.4 = (bf16[8,24,512]{2,1,0:T(8,128)(2,1)S(1)}, bf16[8,24,512]{2,1,0:T(8,128)(2,1)S(1)}, u32[]{:S(2)}, u32[]{:S(2)}) collective-permute-start(bf16[8,24,512]{2,1,0:T(8,128)(2,1)S(1)} %get-tuple-element.26), channel_id=1, source_target_pairs={{0,16},{1,17},{2,18},{3,19},{4,20},{5,21},{6,22},{7,23},{8,24},{9,... | collective-permute-start | bytes 589832 | tf_op jit(solution)/shard_map/ppermute | solution.py:389
  77.9 12.9 %collective-permute-start.3 = (bf16[8,8,512]{2,1,0:T(8,128)(2,1)S(1)}, bf16[8,8,512]{2,1,0:T(8,128)(2,1)S(1)}, u32[]{:S(2)}, u32[]{:S(2)}) collective-permute-start(bf16[8,8,512]{2,1,0:T(8,128)(2,1)S(1)} %get-tuple-element.25), channel_id=1, source_target_pairs={{0,17},{1,18},{2,19},{3,20},{4,21},{5,22},{6,23},{7,24},{8,25},{9,... | collective-permute-start | bytes 196616 | tf_op jit(solution)/shard_map/ppermute | solution.py:389
  78.0 12.8 %collective-permute-start.5 = (bf16[8,8,512]{2,1,0:T(8,128)(2,1)S(1)}, bf16[8,8,512]{2,1,0:T(8,128)(2,1)S(1)}, u32[]{:S(2)}, u32[]{:S(2)}) collective-permute-start(bf16[8,8,512]{2,1,0:T(8,128)(2,1)S(1)} %get-tuple-element.27), channel_id=1, source_target_pairs={{0,1},{1,2},{2,3},{3,4},{4,5},{5,6},{6,7},{7,8},{8,9},{9,10},{10,1... | collective-permute-start | bytes 196616 | tf_op jit(solution)/shard_map/ppermute | solution.py:389

commit v5 on v4

--- a/solution.py
+++ b/solution.py
@@ -220,10 +220,7 @@
         c = slice(part * D, (part + 1) * D)
         if copies:
             copies[part].wait()
-            copies[part + 3].start()
         qkv[:, c] = dot(h, w_qkv[:, c]).astype(BF)
-    for copy in copies[6:]:
-        copy.start()
     first = iota((area, LANES), 1) < 64
     ones = jnp.ones((area, LANES), BF)
     for w in range(count // area):
@@ -259,11 +256,11 @@
 
 def bin_kernel(
     arrived, background, gains, wq, wp, wu, wd,
-    keep, below, right, corner,
+    keep, above, right, corner,
     lined, pick, vq, vp, vu, vd, qkv, mixed, state, sems,
 ):
     copies = weight_copies(0, (wq, wp, wu, wd), (vq, vp, vu, vd), sems)
-    for copy in copies[:3]:
+    for copy in copies:
         copy.start()
     for k in range(4):
         lined[:, k * LANES : (k + 1) * LANES] = arrived[:, k * CAP : (k + 1) * CAP, :].reshape(
@@ -290,12 +287,12 @@
     done = block_body(0, state[...], None, gains, (vq, vp, vu, vd), copies, qkv, mixed)
     one = done[:BLK].reshape(WIN, WIN, D)
     two = done[BLK:].reshape(WIN, WIN, D)
-    corner[...] = one[:HALF, :HALF]
-    right[...] = one[HALF:, :HALF]
-    below[:, :HALF, :] = one[:HALF, HALF:]
-    below[:, HALF:, :] = two[:HALF]
-    keep[:, :HALF, :] = one[HALF:, HALF:]
-    keep[:, HALF:, :] = two[HALF:]
+    corner[...] = one[HALF:, :HALF]
+    right[...] = one[:HALF, :HALF]
+    above[:, :HALF, :] = one[HALF:, HALF:]
+    above[:, HALF:, :] = two[HALF:]
+    keep[:, :HALF, :] = one[:HALF, HALF:]
+    keep[:, HALF:, :] = two[:HALF]
 
 
 WEIGHT_SCRATCH = [
@@ -336,33 +333,33 @@
 
 
 def shift_kernel(
-    last, mine, below, right, corner, gains, wq, wp, wu, wd,
-    keep, above, left, diagonal, qkv, mixed, state, bias,
+    first, mine, above, right, corner, gains, wq, wp, wu, wd,
+    keep, back, left, diagonal, qkv, mixed, state, bias,
 ):
     area = WIN * WIN
     h = area // 2
     split = (iota((area, area), 0) < h) != (iota((area, area), 1) < h)
-    bias[...] = jnp.where(split & (last[0] == 1), -1e30, 0.0)
-    top = mine[...].astype(F32)
-    bottom = below[...].astype(F32)
+    bias[...] = jnp.where(split & (first[0] == 1), -1e30, 0.0)
+    top = above[...].astype(F32)
+    bottom = mine[...].astype(F32)
     state[0:h, :] = top[:, :WIN, :].reshape(h, D)
     state[h : 2 * h, :] = bottom[:, :WIN, :].reshape(h, D)
-    top = jnp.concatenate([top[:, WIN:, :], right[...].astype(F32)], 1)
-    bottom = jnp.concatenate([bottom[:, WIN:, :], corner[...].astype(F32)], 1)
+    top = jnp.concatenate([top[:, WIN:, :], corner[...].astype(F32)], 1)
+    bottom = jnp.concatenate([bottom[:, WIN:, :], right[...].astype(F32)], 1)
     state[2 * h : 3 * h, :] = top.reshape(h, D)
     state[3 * h : 4 * h, :] = bottom.reshape(h, D)
     done = block_body(1, state[...], bias[...], gains, (wq, wp, wu, wd), (), qkv, mixed)
     one = done[:BLK].reshape(WIN, WIN, D)
     two = done[BLK:].reshape(WIN, WIN, D)
-    diagonal[...] = two[HALF:, HALF:]
-    left[...] = two[:HALF, HALF:]
-    above[:, :WIN, :] = one[HALF:]
-    above[:, WIN:, :] = two[HALF:, :HALF]
-    keep[:, :WIN, :] = one[:HALF]
-    keep[:, WIN:, :] = two[:HALF, :HALF]
-
-
-def shift_block(last, pieces, gains, *weights):
+    diagonal[...] = two[:HALF, HALF:]
+    left[...] = two[HALF:, HALF:]
+    back[:, :WIN, :] = one[:HALF]
+    back[:, WIN:, :] = two[:HALF, :HALF]
+    keep[:, :WIN, :] = one[HALF:]
+    keep[:, WIN:, :] = two[HALF:, :HALF]
+
+
+def shift_block(first, pieces, gains, *weights):
     return pl.pallas_call(
         shift_kernel,
         out_shape=PIECES,
@@ -372,7 +369,7 @@
         compiler_params=pltpu.CompilerParams(vmem_limit_bytes=SHIFT_VMEM),
         cost_estimate=BLOCK_COST,
         name="shift_block",
-    )(last, *pieces, gains, *weights)
+    )(first, *pieces, gains, *weights)
 
 
 def moved(block, lat_step, lon_step):
@@ -416,18 +413,18 @@
     )
     arrived = lax.all_to_all(slab, ("lat", "lon"), split_axis=0, concat_axis=0, tiled=True)
     weights = (w_qkv, w_proj, w_up, w_down)
-    mine, below, right, corner = bin_block(arrived, background, norm_gain, *weights)
+    mine, above, right, corner = bin_block(arrived, background, norm_gain, *weights)
     late = fetch(mine, *weights)
-    below = moved(below, -1, 0)
+    above = moved(above, 1, 0)
     right = moved(right, 0, -1)
-    corner = moved(corner, -1, -1)
-    last = (lat == lax.axis_size("lat") - 1).astype(jnp.int32).reshape(1)
-    mine, above, left, corner = shift_block(last, (mine, below, right, corner), norm_gain, *late)
-    above = moved(above, 1, 0)
+    corner = moved(corner, 1, -1)
+    first = (lat == 0).astype(jnp.int32).reshape(1)
+    mine, back, left, corner = shift_block(first, (mine, above, right, corner), norm_gain, *late)
+    below = moved(back, -1, 0)
     left = moved(left, 0, 1)
-    corner = moved(corner, 1, 1)
-    top = jnp.concatenate([corner, above], 1)
-    bottom = jnp.concatenate([left, mine], 1)
+    corner = moved(corner, -1, 1)
+    top = jnp.concatenate([left, mine], 1)
+    bottom = jnp.concatenate([corner, below], 1)
     return jnp.concatenate([top, bottom], 0)
 
 

time: 91.9 us -> 91.2 us (level)
  starting transfers between devices: 4.01 us -> 2.05 us
  waiting for transfers between devices: 13.8 us -> 14.9 us
    ppermute x6, starting transfers between devices: 4.01 us -> 2.05 us  [moved(): return lax.ppermute(block, ('lat', 'lon'), route)]
    ppermute x6, waiting for transfers between devices: 13.8 us -> 14.9 us  [moved(): return lax.ppermute(block, ('lat', 'lon'), route)]
  transfers between devices with their start and end apart: 6 -> 6, of which waited for: 4 -> 3; matrix products, arithmetic and copies ran while one was open for 0% -> 0% of each run, Pallas kernels for 3% -> 3%
where the time goes in v5:
time: 91.2 us; the launch traced here: 90.5 us
  blocking collectives  44.4 us (49%)
  Pallas kernels  27.6 us (30%)
  waiting for transfers between devices  14.9 us (16%)
  starting transfers between devices  2.05 us (2%)
    all_to_all x1, blocking collectives, on_device(): lax.all_to_all(slab, ('lat', 'lon'), split_axis=0, concat_axis=0, tiled=T...  44.4 us
    ppermute x6, waiting for transfers between devices, moved(): return lax.ppermute(block, ('lat', 'lon'), route)  14.9 us
    pallas_call x1, Pallas kernels, encode(): pl.pallas_call(encode_kernel, out_shape=jax.ShapeDtypeStruct((OWNERS, SLA...  11 us
    pallas_call x1, Pallas kernels, bin_block(): pl.pallas_call(bin_kernel, out_shape=PIECES, in_specs=[VMEM] * 3 + [HBM]...  8.13 us
    pallas_call x1, Pallas kernels, shift_block(): pl.pallas_call(shift_kernel, out_shape=PIECES, in_specs=[SMEM] + [VMEM] *...  5.77 us
    pallas_call x1, Pallas kernels, fetch(): pl.pallas_call(fetch_kernel, out_shape=[jax.ShapeDtypeStruct(a.shape[1:],...  2.75 us
    ppermute x6, starting transfers between devices, moved(): return lax.ppermute(block, ('lat', 'lon'), route)  2.05 us
  transfers between devices with their start and end apart: 6, of which 3 were waited for; matrix products, arithmetic and copies ran while one was open for 0% of the time, Pallas kernels for 3%

profile of v5, /device:TPU:0, one launch (start us, length us, event | category | flops | bytes accessed | tf_op | source)
XLA Modules:
  0.0 90.5 jit_solution(15735261764976494611)
XLA Ops:
  0.7 11.0 %encode.1 = bf16[128,72,128]{2,1,0:T(8,128)(2,1)} custom-call(s32[1]{0:T(128)} %bitcast.1.place, s32[1]{0:T(128)S(6)} %copy.13.count, s32[1,1024]{1,0:T(1,128)} %bitcast.4, s32[1,1024]{1,0:T(1,128)} %bitcast.5, bf16[1024,512]{1,0:T(8,128)(2,1)} %rows_hbm.1, bf16[512,2048]{1,0:T(8,128)(2,1)} %w_in_hbm.1, bf16[2048,512]{1,0:T(8,128)(2,1)} %w_out_hbm.1), custom_call_target="tpu_custom_call" | custom-call | flops 7516192768 | bytes 8388608 | tf_op jit(solution)/shard_map/encode/pallas_call | solution.py:152
  11.7 0.0 copy-start
  11.7 0.0 copy-start.1
  11.7 0.0 copy-start.2
  11.7 44.4 %all_to_all.5.arrived = bf16[128,72,128]{2,1,0:T(8,128)(2,1)S(1)} all-to-all(bf16[128,72,128]{2,1,0:T(8,128)(2,1)} %encode.1), channel_id=1, replica_groups=mesh['lat'=8,'lon'=16] {'lat','lon'}, dimensions={0} | all-to-all | bytes 4718592 | tf_op jit(solution)/shard_map/all_to_all | solution.py:414
  56.0 0.0 copy-done
  56.0 0.0 copy-done.1
  56.1 0.0 copy-done.2
  56.1 8.1 %bin_block.1 = (bf16[8,24,512]{2,1,0:T(8,128)(2,1)S(1)}, bf16[8,24,512]{2,1,0:T(8,128)(2,1)S(1)}, bf16[8,8,512]{2,1,0:T(8,128)(2,1)S(1)}, bf16[8,8,512]{2,1,0:T(8,128)(2,1)S(1)}) custom-call(bf16[128,72,128]{2,1,0:T(8,128)(2,1)S(1)} %all_to_all.5.arrived, bf16[16,32,512]{2,1,0:T(8,128)(2,1)S(1)} %copy-done.1, f32[2,2,512]{2,1,0:T(2,128)S(1)} %copy-done.2, ...), custom_call_target="tpu_custom_call" | custom-call | flops 4294967296 | bytes 8388608 | tf_op jit(solution)/shard_map/bin_block/pallas_call | solution.py:317
  64.2 0.1 collective-permute-start
  64.3 0.3 collective-permute-start.1
  64.6 0.1 collective-permute-start.2
  64.7 2.7 %fetch.1 = (bf16[512,1536]{1,0:T(8,128)(2,1)S(1)}, bf16[512,512]{1,0:T(8,128)(2,1)S(1)}, bf16[512,2048]{1,0:T(8,128)(2,1)S(1)}, bf16[2048,512]{1,0:T(8,128)(2,1)S(1)}) custom-call(bf16[8,24,512]{2,1,0:T(8,128)(2,1)S(1)} %get-tuple-element.17.after.mine, bf16[2,512,1536]{2,1,0:T(8,128)(2,1)} %wq.3, bf16[2,512,512]{2,1,0:T(8,128)(2,1)S(1)} %copy-done, ...), custom_call_target="tpu_custom_call" | custom-call | bytes 25165824 | tf_op jit(solution)/shard_map/fetch/pallas_call | solution.py:202
  67.5 0.0 collective-permute-done.1.right
  67.5 6.2 %collective-permute-done.2.corner = bf16[8,8,512]{2,1,0:T(8,128)(2,1)S(1)} collective-permute-done((bf16[8,8,512]{2,1,0:T(8,128)(2,1)S(1)}, bf16[8,8,512]{2,1,0:T(8,128)(2,1)S(1)}, u32[]{:S(2)}, u32[]{:S(2)}) %collective-permute-start.2) | collective-permute-done | bytes 65568 | tf_op jit(solution)/shard_map/ppermute | solution.py:386
  73.7 1.0 %collective-permute-done.above = bf16[8,24,512]{2,1,0:T(8,128)(2,1)S(1)} collective-permute-done((bf16[8,24,512]{2,1,0:T(8,128)(2,1)S(1)}, bf16[8,24,512]{2,1,0:T(8,128)(2,1)S(1)}, u32[]{:S(2)}, u32[]{:S(2)}) %collective-permute-start) | collective-permute-done | bytes 196640 | tf_op jit(solution)/shard_map/ppermute | solution.py:386
  74.7 5.8 %shift_block.1 = (bf16[8,24,512]{2,1,0:T(8,128)(2,1)S(1)}, bf16[8,24,512]{2,1,0:T(8,128)(2,1)S(1)}, bf16[8,8,512]{2,1,0:T(8,128)(2,1)S(1)}, bf16[8,8,512]{2,1,0:T(8,128)(2,1)S(1)}) custom-call(s32[1]{0:T(128)} %bitcast.first, bf16[8,24,512]{2,1,0:T(8,128)(2,1)S(1)} %get-tuple-element.17.after.mine, bf16[8,24,512]{2,1,0:T(8,128)(2,1)S(1)} %collective-permute-done.above, ...), custom_call_target="tpu_custom_call" | custom-call | flops 4294967296 | bytes 8388608 | tf_op jit(solution)/shard_map/shift_block/pallas_call | solution.py:363
  80.5 0.9 collective-permute-start.5
  81.4 0.6 collective-permute-start.3
  82.0 0.1 collective-permute-start.4
  82.0 7.6 %collective-permute-done.3 = bf16[8,8,512]{2,1,0:T(8,128)(2,1)S(1)} collective-permute-done((bf16[8,8,512]{2,1,0:T(8,128)(2,1)S(1)}, bf16[8,8,512]{2,1,0:T(8,128)(2,1)S(1)}, u32[]{:S(2)}, u32[]{:S(2)}) %collective-permute-start.3) | collective-permute-done | bytes 65568 | tf_op jit(solution)/shard_map/ppermute | solution.py:386
  89.7 0.0 collective-permute-done.4
  89.7 0.0 collective-permute-done.5
  89.7 0.8 maximum_maximum_fusion
Async XLA Ops:
  11.7 44.4 %copy-start = (bf16[2,512,512]{2,1,0:T(8,128)(2,1)S(1)}, bf16[2,512,512]{2,1,0:T(8,128)(2,1)}, u32[]{:S(2)}) copy-start(bf16[2,512,512]{2,1,0:T(8,128)(2,1)} %wp.3) | copy-start | bytes 3145732
  11.7 44.4 %copy-start.1 = (bf16[16,32,512]{2,1,0:T(8,128)(2,1)S(1)}, bf16[16,32,512]{2,1,0:T(8,128)(2,1)}, u32[]{:S(2)}) copy-start(bf16[16,32,512]{2,1,0:T(8,128)(2,1)} %background.1) | copy-start | bytes 1572868
  11.7 44.4 %copy-start.2 = (f32[2,2,512]{2,1,0:T(2,128)S(1)}, f32[2,2,512]{2,1,0:T(2,128)}, u32[]{:S(2)}) copy-start(f32[2,2,512]{2,1,0:T(2,128)} %gains.3) | copy-start | bytes 24580
  64.2 10.5 %collective-permute-start = (bf16[8,24,512]{2,1,0:T(8,128)(2,1)S(1)}, bf16[8,24,512]{2,1,0:T(8,128)(2,1)S(1)}, u32[]{:S(2)}, u32[]{:S(2)}) collective-permute-start(bf16[8,24,512]{2,1,0:T(8,128)(2,1)S(1)} %get-tuple-element.18), channel_id=1, source_target_pairs={{0,16},{1,17},{2,18},{3,19},{4,20},{5,21},{6,22},{7,23},{8,24},{9,... | collective-permute-start | bytes 589832 | tf_op jit(solution)/shard_map/ppermute | solution.py:386
  64.3 3.2 %collective-permute-start.1 = (bf16[8,8,512]{2,1,0:T(8,128)(2,1)S(1)}, bf16[8,8,512]{2,1,0:T(8,128)(2,1)S(1)}, u32[]{:S(2)}, u32[]{:S(2)}) collective-permute-start(bf16[8,8,512]{2,1,0:T(8,128)(2,1)S(1)} %get-tuple-element.19), channel_id=1, source_target_pairs={{0,15},{1,0},{2,1},{3,2},{4,3},{5,4},{6,5},{7,6},{8,7},{9,8},{10,9... | collective-permute-start | bytes 196616 | tf_op jit(solution)/shard_map/ppermute | solution.py:386
  64.6 9.1 %collective-permute-start.2 = (bf16[8,8,512]{2,1,0:T(8,128)(2,1)S(1)}, bf16[8,8,512]{2,1,0:T(8,128)(2,1)S(1)}, u32[]{:S(2)}, u32[]{:S(2)}) collective-permute-start(bf16[8,8,512]{2,1,0:T(8,128)(2,1)S(1)} %get-tuple-element.20), channel_id=1, source_target_pairs={{0,31},{1,16},{2,17},{3,18},{4,19},{5,20},{6,21},{7,22},{8,23},{9,... | collective-permute-start | bytes 196616 | tf_op jit(solution)/shard_map/ppermute | solution.py:386
  80.5 9.2 %collective-permute-start.5 = (bf16[8,24,512]{2,1,0:T(8,128)(2,1)S(1)}, bf16[8,24,512]{2,1,0:T(8,128)(2,1)S(1)}, u32[]{:S(2)}, u32[]{:S(2)}) collective-permute-start(bf16[8,24,512]{2,1,0:T(8,128)(2,1)S(1)} %get-tuple-element.28), channel_id=1, source_target_pairs={{0,112},{1,113},{2,114},{3,115},{4,116},{5,117},{6,118},{7,119},{8... | collective-permute-start | bytes 589832 | tf_op jit(solution)/shard_map/ppermute | solution.py:386
  81.4 8.3 %collective-permute-start.3 = (bf16[8,8,512]{2,1,0:T(8,128)(2,1)S(1)}, bf16[8,8,512]{2,1,0:T(8,128)(2,1)S(1)}, u32[]{:S(2)}, u32[]{:S(2)}) collective-permute-start(bf16[8,8,512]{2,1,0:T(8,128)(2,1)S(1)} %get-tuple-element.25), channel_id=1, source_target_pairs={{0,1},{1,2},{2,3},{3,4},{4,5},{5,6},{6,7},{7,8},{8,9},{9,10},{10,1... | collective-permute-start | bytes 196616 | tf_op jit(solution)/shard_map/ppermute | solution.py:386
  82.0 7.7 %collective-permute-start.4 = (bf16[8,8,512]{2,1,0:T(8,128)(2,1)S(1)}, bf16[8,8,512]{2,1,0:T(8,128)(2,1)S(1)}, u32[]{:S(2)}, u32[]{:S(2)}) collective-permute-start(bf16[8,8,512]{2,1,0:T(8,128)(2,1)S(1)} %get-tuple-element.27), channel_id=1, source_target_pairs={{0,113},{1,114},{2,115},{3,116},{4,117},{5,118},{6,119},{7,120},{8... | collective-permute-start | bytes 196616 | tf_op jit(solution)/shard_map/ppermute | solution.py:386

commit v6 on v5

--- a/solution.py
+++ b/solution.py
@@ -15,6 +15,8 @@
 CELLS = CLAT * CLON
 OBS_DEV = 1024
 OWNERS = 128
+N_LAT = 8
+N_LON = 16
 CAP = 16
 LANES = 128
 SLAB = 4 * CAP + 8
@@ -28,6 +30,7 @@
 ENCODE_VMEM = 67043328 - (100 << 10)
 BIN_VMEM = (64 << 20) - (16000 << 10)
 SHIFT_VMEM = 16 << 20
+LATE_VMEM = 8 << 20
 FETCH_VMEM = (64 << 20) - (18500 << 10)
 BF = jnp.bfloat16
 F32 = jnp.float32
@@ -92,7 +95,8 @@
     low = jnp.zeros((OWNERS, LANES), F32)
     for b in range(OBS_DEV // BLK):
         cols = slice(b * BLK, (b + 1) * BLK)
-        target = dest[:, cols]
+        owner = dest[:, cols]
+        target = owner % N_LON * N_LAT + owner // N_LON
         live = (iota((1, BLK), 1) + b * BLK) < live_count
         hits = jnp.where((owner_col == target) & live, 1.0, 0.0)
         hits_bf = hits.astype(BF)
@@ -211,38 +215,40 @@
     )(after, *arrays)
 
 
-def block_body(layer, x, bias, gains, weights, copies, qkv, mixed):
-    w_qkv, w_proj, w_up, w_down = weights
-    count = x.shape[0]
-    area = WIN * WIN
+def project(layer, x, gains, w_qkv, copies, qkv):
     h = normed(x, gains[layer, 0:1, :])
     for part in range(3):
         c = slice(part * D, (part + 1) * D)
         if copies:
             copies[part].wait()
         qkv[:, c] = dot(h, w_qkv[:, c]).astype(BF)
-    first = iota((area, LANES), 1) < 64
-    ones = jnp.ones((area, LANES), BF)
-    for w in range(count // area):
-        r = slice(w * area, (w + 1) * area)
-        for pair in range(HEADS // 2):
-            c = pair * LANES
-            q = qkv[r, c : c + LANES] * BF(0.125)
-            k = qkv[r, D + c : D + c + LANES]
-            v = jnp.concatenate([qkv[r, 2 * D + c : 2 * D + c + LANES], ones], 1)
-            out = []
-            for head in range(2):
-                mine = first if head == 0 else jnp.logical_not(first)
-                scores = dot_nt(jnp.where(mine, q, BF(0)), k)
-                if bias is not None:
-                    scores = scores + bias
-                probs = jnp.exp(scores - jnp.max(scores, -1, keepdims=True)).astype(BF)
-                both = dot(probs, v)
-                out.append(both[:, :LANES] / both[:, LANES:])
-            mixed[r, c : c + LANES] = jnp.where(first, out[0], out[1]).astype(BF)
+
+
+def attend(queries, keys, values, bias, mixed):
+    count = queries.shape[0]
+    first = iota((count, LANES), 1) < 64
+    ones = jnp.ones((WIN * WIN, LANES), BF)
+    for pair in range(HEADS // 2):
+        c = slice(pair * LANES, (pair + 1) * LANES)
+        q = queries[:, c] * BF(0.125)
+        k = keys[:, c]
+        v = jnp.concatenate([values[:, c], ones], 1)
+        out = []
+        for head in range(2):
+            mine = first if head == 0 else jnp.logical_not(first)
+            scores = dot_nt(jnp.where(mine, q, BF(0)), k)
+            if bias is not None:
+                scores = scores + bias
+            probs = jnp.exp(scores - jnp.max(scores, -1, keepdims=True)).astype(BF)
+            both = dot(probs, v)
+            out.append(both[:, :LANES] / both[:, LANES:])
+        mixed[:, c] = jnp.where(first, out[0], out[1]).astype(BF)
+
+
+def finish(layer, x, mixed, gains, w_proj, w_up, w_down, copies):
     if copies:
         copies[3].wait()
-    attended = x + dot(mixed[...], w_proj[...])
+    attended = x + dot(mixed, w_proj[...])
     h = normed(attended, gains[layer, 1:2, :])
     total = attended
     for t in range(FF // TILE):
@@ -284,7 +290,12 @@
         r = slice(w * BLK, (w + 1) * BLK)
         back = background[:, w * WIN : (w + 1) * WIN, :].astype(F32).reshape(BLK, D)
         state[r, :] = (back + sums[r, :]).astype(BF).astype(F32)
-    done = block_body(0, state[...], None, gains, (vq, vp, vu, vd), copies, qkv, mixed)
+    project(0, state[...], gains, vq, copies, qkv)
+    for w in range(2):
+        r = pl.ds(w * BLK, BLK)
+        parts = [qkv.at[r, pl.ds(part * D, D)] for part in range(3)]
+        attend(*parts, None, mixed.at[r])
+    done = finish(0, state[...], mixed[...], gains, vp, vu, vd, copies)
     one = done[:BLK].reshape(WIN, WIN, D)
     two = done[BLK:].reshape(WIN, WIN, D)
     corner[...] = one[HALF:, :HALF]
@@ -332,14 +343,18 @@
     )(arrived, background, gains, *weights)
 
 
+def region_bias(first):
+    area = WIN * WIN
+    split = (iota((area, area), 0) < BLK // 2) != (iota((area, area), 1) < BLK // 2)
+    return jnp.where(split & (first == 1), -1e30, 0.0)
+
+
 def shift_kernel(
     first, mine, above, right, corner, gains, wq, wp, wu, wd,
-    keep, back, left, diagonal, qkv, mixed, state, bias,
+    edge, back, left, diagonal, late_q, late_kv, late_x, qkv, mixed, state, bias,
 ):
-    area = WIN * WIN
-    h = area // 2
-    split = (iota((area, area), 0) < h) != (iota((area, area), 1) < h)
-    bias[...] = jnp.where(split & (first[0] == 1), -1e30, 0.0)
+    h = BLK // 2
+    bias[...] = region_bias(first[0])
     top = above[...].astype(F32)
     bottom = mine[...].astype(F32)
     state[0:h, :] = top[:, :WIN, :].reshape(h, D)
@@ -348,28 +363,73 @@
     bottom = jnp.concatenate([bottom[:, WIN:, :], right[...].astype(F32)], 1)
     state[2 * h : 3 * h, :] = top.reshape(h, D)
     state[3 * h : 4 * h, :] = bottom.reshape(h, D)
-    done = block_body(1, state[...], bias[...], gains, (wq, wp, wu, wd), (), qkv, mixed)
-    one = done[:BLK].reshape(WIN, WIN, D)
-    two = done[BLK:].reshape(WIN, WIN, D)
+    project(1, state[...], gains, wq, (), qkv)
+    parts = [qkv.at[pl.ds(0, BLK), pl.ds(part * D, D)] for part in range(3)]
+    attend(parts[0].at[pl.ds(0, h)], parts[1], parts[2], bias[0:h, :], mixed.at[pl.ds(0, h)])
+    parts = [qkv.at[pl.ds(BLK, BLK), pl.ds(part * D, D)] for part in range(3)]
+    attend(*parts, bias[...], mixed.at[pl.ds(h, BLK)])
+    late_q[...] = qkv[h:BLK, :D]
+    late_kv[...] = qkv[0:BLK, D:]
+    late_x[...] = state[h:BLK, :].astype(BF)
+    x = jnp.concatenate([state[0:h, :], state[BLK:, :]], 0)
+    done = finish(1, x, mixed[...], gains, wp, wu, wd, ())
+    one = done[:h].reshape(HALF, WIN, D)
+    two = done[h:].reshape(WIN, WIN, D)
     diagonal[...] = two[:HALF, HALF:]
     left[...] = two[HALF:, HALF:]
-    back[:, :WIN, :] = one[:HALF]
+    back[:, :WIN, :] = one
     back[:, WIN:, :] = two[:HALF, :HALF]
-    keep[:, :WIN, :] = one[HALF:]
-    keep[:, WIN:, :] = two[HALF:, :HALF]
+    edge[...] = two[HALF:, :HALF]
 
 
 def shift_block(first, pieces, gains, *weights):
+    h = BLK // 2
     return pl.pallas_call(
         shift_kernel,
-        out_shape=PIECES,
+        out_shape=(
+            NARROW,
+            WIDE,
+            NARROW,
+            NARROW,
+            jax.ShapeDtypeStruct((h, D), BF),
+            jax.ShapeDtypeStruct((BLK, 2 * D), BF),
+            jax.ShapeDtypeStruct((h, D), BF),
+        ),
         in_specs=[SMEM] + [VMEM] * 9,
-        out_specs=[VMEM] * 4,
-        scratch_shapes=BLOCK_SCRATCH + [pltpu.VMEM((WIN * WIN, WIN * WIN), F32)],
+        out_specs=[VMEM] * 7,
+        scratch_shapes=[
+            pltpu.VMEM((CELLS, 3 * D), BF),
+            pltpu.VMEM((CELLS - h, D), BF),
+            pltpu.VMEM((CELLS, D), F32),
+            pltpu.VMEM((BLK, BLK), F32),
+        ],
         compiler_params=pltpu.CompilerParams(vmem_limit_bytes=SHIFT_VMEM),
         cost_estimate=BLOCK_COST,
         name="shift_block",
     )(first, *pieces, gains, *weights)
+
+
+def late_kernel(first, q, kv, x, gains, wp, wu, wd, out, mixed):
+    h = BLK // 2
+    bias = region_bias(first[0])[h:, :]
+    attend(q, kv.at[:, pl.ds(0, D)], kv.at[:, pl.ds(D, D)], bias, mixed)
+    done = finish(1, x[...].astype(F32), mixed[...], gains, wp, wu, wd, ())
+    out[...] = done.reshape(HALF, WIN, D)
+
+
+def late_block(first, q, kv, x, gains, *weights):
+    return pl.pallas_call(
+        late_kernel,
+        out_shape=jax.ShapeDtypeStruct((HALF, WIN, D), BF),
+        in_specs=[SMEM] + [VMEM] * 7,
+        out_specs=VMEM,
+        scratch_shapes=[pltpu.VMEM((BLK // 2, D), BF)],
+        compiler_params=pltpu.CompilerParams(vmem_limit_bytes=LATE_VMEM),
+        cost_estimate=pl.CostEstimate(
+            flops=1 << 30, transcendentals=1 << 19, bytes_accessed=6 << 20
+        ),
+        name="late_block",
+    )(first, q, kv, x, gains, *weights)
 
 
 def moved(block, lat_step, lon_step):
@@ -401,7 +461,7 @@
     norm_gain,
 ):
     lat = lax.axis_index("lat")
-    place = (lat * lax.axis_size("lon") + lax.axis_index("lon")).astype(jnp.int32).reshape(1)
+    place = (lax.axis_index("lon") * N_LAT + lat).astype(jnp.int32).reshape(1)
     slab = encode(
         place,
         obs_count,
@@ -411,7 +471,7 @@
         w_obs_in,
         w_obs_out,
     )
-    arrived = lax.all_to_all(slab, ("lat", "lon"), split_axis=0, concat_axis=0, tiled=True)
+    arrived = lax.all_to_all(slab, ("lon", "lat"), split_axis=0, concat_axis=0, tiled=True)
     weights = (w_qkv, w_proj, w_up, w_down)
     mine, above, right, corner = bin_block(arrived, background, norm_gain, *weights)
     late = fetch(mine, *weights)
@@ -419,11 +479,14 @@
     right = moved(right, 0, -1)
     corner = moved(corner, 1, -1)
     first = (lat == 0).astype(jnp.int32).reshape(1)
-    mine, back, left, corner = shift_block(first, (mine, above, right, corner), norm_gain, *late)
+    edge, back, left, corner, q, kv, x = shift_block(
+        first, (mine, above, right, corner), norm_gain, *late
+    )
     below = moved(back, -1, 0)
     left = moved(left, 0, 1)
     corner = moved(corner, -1, 1)
-    top = jnp.concatenate([left, mine], 1)
+    mid = late_block(first, q, kv, x, norm_gain, *late[1:])
+    top = jnp.concatenate([left, mid, edge], 1)
     bottom = jnp.concatenate([corner, below], 1)
     return jnp.concatenate([top, bottom], 0)
 

time: 91.2 us -> 89.8 us (0.985)
  waiting for transfers between devices: 14.9 us -> 12 us
  Pallas kernels: 27.6 us -> 28.7 us
    ppermute x6, waiting for transfers between devices: 14.9 us -> 12 us  [moved(): return lax.ppermute(block, ('lat', 'lon'), route)]
    pallas_call x1 -> x2, Pallas kernels: 5.77 us -> 6.69 us  [the longest x1 4.87 us: shift_block(): pl.pallas_call(shift_kernel, out_shape=(NARROW, WIDE, NARROW, NARROW, jax...]
  transfers between devices with their start and end apart: 6 -> 6, of which waited for: 3 -> 3; matrix products, arithmetic and copies ran while one was open for 0% -> 0% of each run, Pallas kernels for 3% -> 5%
where the time goes in v6:
time: 89.8 us; the launch traced here: 89.2 us
  blocking collectives  44.1 us (49%)
  Pallas kernels  28.7 us (32%)
  waiting for transfers between devices  12 us (13%)
  starting transfers between devices  2.76 us (3%)
    all_to_all x1, blocking collectives, on_device(): lax.all_to_all(slab, ('lon', 'lat'), split_axis=0, concat_axis=0, tiled=T...  44.1 us
    ppermute x6, waiting for transfers between devices, moved(): return lax.ppermute(block, ('lat', 'lon'), route)  12 us
    pallas_call x1, Pallas kernels, encode(): pl.pallas_call(encode_kernel, out_shape=jax.ShapeDtypeStruct((OWNERS, SLA...  11 us
    pallas_call x1, Pallas kernels, bin_block(): pl.pallas_call(bin_kernel, out_shape=PIECES, in_specs=[VMEM] * 3 + [HBM]...  8.23 us
    pallas_call x1, Pallas kernels, shift_block(): pl.pallas_call(shift_kernel, out_shape=(NARROW, WIDE, NARROW, NARROW, jax...  4.87 us
    ppermute x6, starting transfers between devices, moved(): return lax.ppermute(block, ('lat', 'lon'), route)  2.76 us
    pallas_call x1, Pallas kernels, fetch(): pl.pallas_call(fetch_kernel, out_shape=[jax.ShapeDtypeStruct(a.shape[1:],...  2.75 us
    pallas_call x1, Pallas kernels, late_block(): pl.pallas_call(late_kernel, out_shape=jax.ShapeDtypeStruct((HALF, WIN, D)...  1.83 us
  transfers between devices with their start and end apart: 6, of which 3 were waited for; matrix products, arithmetic and copies ran while one was open for 0% of the time, Pallas kernels for 5%

profile of v6, /device:TPU:0, one launch (start us, length us, event | category | flops | bytes accessed | tf_op | source)
XLA Modules:
  0.0 89.2 jit_solution(10537495411207884638)
XLA Ops:
  0.7 11.0 %encode.1 = bf16[128,72,128]{2,1,0:T(8,128)(2,1)} custom-call(s32[1]{0:T(128)} %bitcast.1.place, s32[1]{0:T(128)S(6)} %copy.13.count, s32[1,1024]{1,0:T(1,128)} %bitcast.4, s32[1,1024]{1,0:T(1,128)} %bitcast.5, bf16[1024,512]{1,0:T(8,128)(2,1)} %rows_hbm.1, bf16[512,2048]{1,0:T(8,128)(2,1)} %w_in_hbm.1, bf16[2048,512]{1,0:T(8,128)(2,1)} %w_out_hbm.1), custom_call_target="tpu_custom_call" | custom-call | flops 7516192768 | bytes 8388608 | tf_op jit(solution)/shard_map/encode/pallas_call | solution.py:156
  11.7 0.0 copy-start
  11.7 0.0 copy-start.1
  11.7 0.0 copy-start.2
  11.7 44.1 %all_to_all.5.arrived = bf16[128,72,128]{2,1,0:T(8,128)(2,1)S(1)} all-to-all(bf16[128,72,128]{2,1,0:T(8,128)(2,1)} %encode.1), channel_id=1, replica_groups=mesh['lat'=8,'lon'=16] {'lon','lat'}, dimensions={0} | all-to-all | bytes 4718592 | tf_op jit(solution)/shard_map/all_to_all | solution.py:474
  55.8 0.0 copy-done
  55.8 0.0 copy-done.1
  55.8 8.2 %bin_block.1 = (bf16[8,24,512]{2,1,0:T(8,128)(2,1)S(1)}, bf16[8,24,512]{2,1,0:T(8,128)(2,1)S(1)}, bf16[8,8,512]{2,1,0:T(8,128)(2,1)S(1)}, bf16[8,8,512]{2,1,0:T(8,128)(2,1)S(1)}) custom-call(bf16[128,72,128]{2,1,0:T(8,128)(2,1)S(1)} %all_to_all.5.arrived, bf16[16,32,512]{2,1,0:T(8,128)(2,1)S(1)} %copy-done.2, f32[2,2,512]{2,1,0:T(2,128)S(1)} %copy-done.1, ...), custom_call_target="tpu_custom_call" | custom-call | flops 4294967296 | bytes 8388608 | tf_op jit(solution)/shard_map/bin_block/pallas_call | solution.py:328
  64.1 0.9 %collective-permute-start = (bf16[8,24,512]{2,1,0:T(8,128)(2,1)S(1)}, bf16[8,24,512]{2,1,0:T(8,128)(2,1)S(1)}, u32[]{:S(2)}, u32[]{:S(2)}) collective-permute-start(bf16[8,24,512]{2,1,0:T(8,128)(2,1)S(1)} %get-tuple-element.21), channel_id=1, source_target_pairs={{0,16},{1,17},{2,18},{3,19},{4,20},{5,21},{6,22},{7,23},{8,24},{9,... | collective-permute-start | bytes 589832 | tf_op jit(solution)/shard_map/ppermute | solution.py:446
  65.0 0.0 collective-permute-start.1
  65.0 0.1 collective-permute-start.2
  65.1 2.7 %fetch.1 = (bf16[512,1536]{1,0:T(8,128)(2,1)S(1)}, bf16[512,512]{1,0:T(8,128)(2,1)S(1)}, bf16[512,2048]{1,0:T(8,128)(2,1)S(1)}, bf16[2048,512]{1,0:T(8,128)(2,1)S(1)}) custom-call(bf16[8,24,512]{2,1,0:T(8,128)(2,1)S(1)} %get-tuple-element.20.after.mine, bf16[2,512,1536]{2,1,0:T(8,128)(2,1)} %wq.3, bf16[2,512,512]{2,1,0:T(8,128)(2,1)S(1)} %copy-done, ...), custom_call_target="tpu_custom_call" | custom-call | bytes 25165824 | tf_op jit(solution)/shard_map/fetch/pallas_call | solution.py:206
  67.8 0.0 collective-permute-done.1.right
  67.9 5.2 %collective-permute-done.2.corner = bf16[8,8,512]{2,1,0:T(8,128)(2,1)S(1)} collective-permute-done((bf16[8,8,512]{2,1,0:T(8,128)(2,1)S(1)}, bf16[8,8,512]{2,1,0:T(8,128)(2,1)S(1)}, u32[]{:S(2)}, u32[]{:S(2)}) %collective-permute-start.2) | collective-permute-done | bytes 65568 | tf_op jit(solution)/shard_map/ppermute | solution.py:446
  73.1 1.1 %collective-permute-done.above = bf16[8,24,512]{2,1,0:T(8,128)(2,1)S(1)} collective-permute-done((bf16[8,24,512]{2,1,0:T(8,128)(2,1)S(1)}, bf16[8,24,512]{2,1,0:T(8,128)(2,1)S(1)}, u32[]{:S(2)}, u32[]{:S(2)}) %collective-permute-start) | collective-permute-done | bytes 196640 | tf_op jit(solution)/shard_map/ppermute | solution.py:446
  74.2 4.9 %shift_block.1 = (bf16[8,8,512]{2,1,0:T(8,128)(2,1)S(1)}, bf16[8,24,512]{2,1,0:T(8,128)(2,1)S(1)}, bf16[8,8,512]{2,1,0:T(8,128)(2,1)S(1)}, bf16[8,8,512]{2,1,0:T...) custom-call(s32[1]{0:T(128)} %bitcast.first, ...), custom_call_target="tpu_custom_call" | custom-call | flops 4294967296 | bytes 8388608 | tf_op jit(solution)/shard_map/shift_block/pallas_call | solution.py:387
  79.1 0.3 collective-permute-start.5
  79.4 0.3 collective-permute-start.3
  79.7 1.1 %collective-permute-start.4 = (bf16[8,8,512]{2,1,0:T(8,128)(2,1)S(1)}, bf16[8,8,512]{2,1,0:T(8,128)(2,1)S(1)}, u32[]{:S(2)}, u32[]{:S(2)}) collective-permute-start(bf16[8,8,512]{2,1,0:T(8,128)(2,1)S(1)} %get-tuple-element.33), channel_id=1, source_target_pairs={{0,113},{1,114},{2,115},{3,116},{4,117},{5,118},{6,119},{7,120},{8... | collective-permute-start | bytes 196616 | tf_op jit(solution)/shard_map/ppermute | solution.py:446
  80.8 1.8 %late_block.1 = bf16[8,16,512]{2,1,0:T(8,128)(2,1)S(1)} custom-call(s32[1]{0:T(128)} %bitcast.first, bf16[128,512]{1,0:T(8,128)(2,1)S(1)} %get-tuple-element.29.q, bf16[256,1024]{1,0:T(8,128)(2,1)S(1)} %get-tuple-element.30.kv, bf16[128,512]{1,0:T(8,128)(2,1)S(1)} %get-tuple-element.31.x, f32[2,2,512]{2,1,0:T(2,128)S(1)} %copy-done.1, ...), custom_call_target="tpu_custom_call" | custom-call | flops 1073741824 | bytes 6291456 | tf_op jit(solution)/shard_map/late_block/pallas_call | solution.py:421
  82.7 5.6 %collective-permute-done.3 = bf16[8,8,512]{2,1,0:T(8,128)(2,1)S(1)} collective-permute-done((bf16[8,8,512]{2,1,0:T(8,128)(2,1)S(1)}, bf16[8,8,512]{2,1,0:T(8,128)(2,1)S(1)}, u32[]{:S(2)}, u32[]{:S(2)}) %collective-permute-start.3) | collective-permute-done | bytes 65568 | tf_op jit(solution)/shard_map/ppermute | solution.py:446
  88.3 0.0 collective-permute-done.4
  88.3 0.0 collective-permute-done.5
  88.3 0.8 maximum_maximum_fusion
  (1 shorter events, 0.0 us)
Async XLA Ops:
  11.7 44.2 %copy-start = (bf16[2,512,512]{2,1,0:T(8,128)(2,1)S(1)}, bf16[2,512,512]{2,1,0:T(8,128)(2,1)}, u32[]{:S(2)}) copy-start(bf16[2,512,512]{2,1,0:T(8,128)(2,1)} %wp.3) | copy-start | bytes 3145732
  11.7 44.2 %copy-start.1 = (f32[2,2,512]{2,1,0:T(2,128)S(1)}, f32[2,2,512]{2,1,0:T(2,128)}, u32[]{:S(2)}) copy-start(f32[2,2,512]{2,1,0:T(2,128)} %gains.5) | copy-start | bytes 24580
  11.7 44.2 %copy-start.2 = (bf16[16,32,512]{2,1,0:T(8,128)(2,1)S(1)}, bf16[16,32,512]{2,1,0:T(8,128)(2,1)}, u32[]{:S(2)}) copy-start(bf16[16,32,512]{2,1,0:T(8,128)(2,1)} %background.1) | copy-start | bytes 1572868
  64.1 10.2 %collective-permute-start = (bf16[8,24,512]{2,1,0:T(8,128)(2,1)S(1)}, bf16[8,24,512]{2,1,0:T(8,128)(2,1)S(1)}, u32[]{:S(2)}, u32[]{:S(2)}) collective-permute-start(bf16[8,24,512]{2,1,0:T(8,128)(2,1)S(1)} %get-tuple-element.21), channel_id=1, source_target_pairs={{0,16},{1,17},{2,18},{3,19},{4,20},{5,21},{6,22},{7,23},{8,24},{9,... | collective-permute-start | bytes 589832 | tf_op jit(solution)/shard_map/ppermute | solution.py:446
  65.0 2.9 %collective-permute-start.1 = (bf16[8,8,512]{2,1,0:T(8,128)(2,1)S(1)}, bf16[8,8,512]{2,1,0:T(8,128)(2,1)S(1)}, u32[]{:S(2)}, u32[]{:S(2)}) collective-permute-start(bf16[8,8,512]{2,1,0:T(8,128)(2,1)S(1)} %get-tuple-element.22), channel_id=1, source_target_pairs={{0,15},{1,0},{2,1},{3,2},{4,3},{5,4},{6,5},{7,6},{8,7},{9,8},{10,9... | collective-permute-start | bytes 196616 | tf_op jit(solution)/shard_map/ppermute | solution.py:446
  65.0 8.1 %collective-permute-start.2 = (bf16[8,8,512]{2,1,0:T(8,128)(2,1)S(1)}, bf16[8,8,512]{2,1,0:T(8,128)(2,1)S(1)}, u32[]{:S(2)}, u32[]{:S(2)}) collective-permute-start(bf16[8,8,512]{2,1,0:T(8,128)(2,1)S(1)} %get-tuple-element.23), channel_id=1, source_target_pairs={{0,31},{1,16},{2,17},{3,18},{4,19},{5,20},{6,21},{7,22},{8,23},{9,... | collective-permute-start | bytes 196616 | tf_op jit(solution)/shard_map/ppermute | solution.py:446
  79.1 9.2 %collective-permute-start.5 = (bf16[8,24,512]{2,1,0:T(8,128)(2,1)S(1)}, bf16[8,24,512]{2,1,0:T(8,128)(2,1)S(1)}, u32[]{:S(2)}, u32[]{:S(2)}) collective-permute-start(bf16[8,24,512]{2,1,0:T(8,128)(2,1)S(1)} %get-tuple-element.34), channel_id=1, source_target_pairs={{0,112},{1,113},{2,114},{3,115},{4,116},{5,117},{6,118},{7,119},{8... | collective-permute-start | bytes 589832 | tf_op jit(solution)/shard_map/ppermute | solution.py:446
  79.4 8.9 %collective-permute-start.3 = (bf16[8,8,512]{2,1,0:T(8,128)(2,1)S(1)}, bf16[8,8,512]{2,1,0:T(8,128)(2,1)S(1)}, u32[]{:S(2)}, u32[]{:S(2)}) collective-permute-start(bf16[8,8,512]{2,1,0:T(8,128)(2,1)S(1)} %get-tuple-element.28), channel_id=1, source_target_pairs={{0,1},{1,2},{2,3},{3,4},{4,5},{5,6},{6,7},{7,8},{8,9},{9,10},{10,1... | collective-permute-start | bytes 196616 | tf_op jit(solution)/shard_map/ppermute | solution.py:446
  79.7 8.6 %collective-permute-start.4 = (bf16[8,8,512]{2,1,0:T(8,128)(2,1)S(1)}, bf16[8,8,512]{2,1,0:T(8,128)(2,1)S(1)}, u32[]{:S(2)}, u32[]{:S(2)}) collective-permute-start(bf16[8,8,512]{2,1,0:T(8,128)(2,1)S(1)} %get-tuple-element.33), channel_id=1, source_target_pairs={{0,113},{1,114},{2,115},{3,116},{4,117},{5,118},{6,119},{7,120},{8... | collective-permute-start | bytes 196616 | tf_op jit(solution)/shard_map/ppermute | solution.py:446

commit v7 on v6

--- a/solution.py
+++ b/solution.py
@@ -483,9 +483,10 @@
         first, (mine, above, right, corner), norm_gain, *late
     )
     below = moved(back, -1, 0)
+    mid = late_block(first, q, kv, x, norm_gain, *late[1:])
+    left, corner, mid = lax.optimization_barrier((left, corner, mid))
     left = moved(left, 0, 1)
     corner = moved(corner, -1, 1)
-    mid = late_block(first, q, kv, x, norm_gain, *late[1:])
     top = jnp.concatenate([left, mid, edge], 1)
     bottom = jnp.concatenate([corner, below], 1)
     return jnp.concatenate([top, bottom], 0)

time: 89.8 us -> 90.1 us (level)
  transfers between devices with their start and end apart: 6 -> 6, of which waited for: 3 -> 4; matrix products, arithmetic and copies ran while one was open for 0% -> 0% of each run, Pallas kernels for 5% -> 5%
where the time goes in v7:
time: 90.1 us; the launch traced here: 89.9 us
  blocking collectives  44.1 us (49%)
  Pallas kernels  28.7 us (32%)
  waiting for transfers between devices  12.7 us (14%)
  starting transfers between devices  2.83 us (3%)
    all_to_all x1, blocking collectives, on_device(): lax.all_to_all(slab, ('lon', 'lat'), split_axis=0, concat_axis=0, tiled=T...  44.1 us
    ppermute x6, waiting for transfers between devices, moved(): return lax.ppermute(block, ('lat', 'lon'), route)  12.7 us
    pallas_call x1, Pallas kernels, encode(): pl.pallas_call(encode_kernel, out_shape=jax.ShapeDtypeStruct((OWNERS, SLA...  11 us
    pallas_call x1, Pallas kernels, bin_block(): pl.pallas_call(bin_kernel, out_shape=PIECES, in_specs=[VMEM] * 3 + [HBM]...  8.23 us
    pallas_call x1, Pallas kernels, shift_block(): pl.pallas_call(shift_kernel, out_shape=(NARROW, WIDE, NARROW, NARROW, jax...  4.87 us
    ppermute x6, starting transfers between devices, moved(): return lax.ppermute(block, ('lat', 'lon'), route)  2.83 us
    pallas_call x1, Pallas kernels, fetch(): pl.pallas_call(fetch_kernel, out_shape=[jax.ShapeDtypeStruct(a.shape[1:],...  2.75 us
    pallas_call x1, Pallas kernels, late_block(): pl.pallas_call(late_kernel, out_shape=jax.ShapeDtypeStruct((HALF, WIN, D)...  1.83 us
  transfers between devices with their start and end apart: 6, of which 4 were waited for; matrix products, arithmetic and copies ran while one was open for 0% of the time, Pallas kernels for 5%

profile of v7, /device:TPU:0, one launch (start us, length us, event | category | flops | bytes accessed | tf_op | source)
XLA Modules:
  0.0 89.9 jit_solution(715519720075713511)
XLA Ops:
  0.7 11.0 %encode.1 = bf16[128,72,128]{2,1,0:T(8,128)(2,1)} custom-call(s32[1]{0:T(128)} %bitcast.1.place, s32[1]{0:T(128)S(6)} %copy.13.count, s32[1,1024]{1,0:T(1,128)} %bitcast.4, s32[1,1024]{1,0:T(1,128)} %bitcast.5, bf16[1024,512]{1,0:T(8,128)(2,1)} %rows_hbm.1, bf16[512,2048]{1,0:T(8,128)(2,1)} %w_in_hbm.1, bf16[2048,512]{1,0:T(8,128)(2,1)} %w_out_hbm.1), custom_call_target="tpu_custom_call" | custom-call | flops 7516192768 | bytes 8388608 | tf_op jit(solution)/shard_map/encode/pallas_call | solution.py:156
  11.7 0.0 copy-start
  11.7 0.0 copy-start.1
  11.7 0.0 copy-start.2
  11.7 44.1 %all_to_all.5.arrived = bf16[128,72,128]{2,1,0:T(8,128)(2,1)S(1)} all-to-all(bf16[128,72,128]{2,1,0:T(8,128)(2,1)} %encode.1), channel_id=1, replica_groups=mesh['lat'=8,'lon'=16] {'lon','lat'}, dimensions={0} | all-to-all | bytes 4718592 | tf_op jit(solution)/shard_map/all_to_all | solution.py:474
  55.8 0.0 copy-done
  55.8 0.0 copy-done.1
  55.8 8.2 %bin_block.1 = (bf16[8,24,512]{2,1,0:T(8,128)(2,1)S(1)}, bf16[8,24,512]{2,1,0:T(8,128)(2,1)S(1)}, bf16[8,8,512]{2,1,0:T(8,128)(2,1)S(1)}, bf16[8,8,512]{2,1,0:T(8,128)(2,1)S(1)}) custom-call(bf16[128,72,128]{2,1,0:T(8,128)(2,1)S(1)} %all_to_all.5.arrived, bf16[16,32,512]{2,1,0:T(8,128)(2,1)S(1)} %copy-done.2, f32[2,2,512]{2,1,0:T(2,128)S(1)} %copy-done.1, ...), custom_call_target="tpu_custom_call" | custom-call | flops 4294967296 | bytes 8388608 | tf_op jit(solution)/shard_map/bin_block/pallas_call | solution.py:328
  64.1 0.9 %collective-permute-start = (bf16[8,24,512]{2,1,0:T(8,128)(2,1)S(1)}, bf16[8,24,512]{2,1,0:T(8,128)(2,1)S(1)}, u32[]{:S(2)}, u32[]{:S(2)}) collective-permute-start(bf16[8,24,512]{2,1,0:T(8,128)(2,1)S(1)} %get-tuple-element.24), channel_id=1, source_target_pairs={{0,16},{1,17},{2,18},{3,19},{4,20},{5,21},{6,22},{7,23},{8,24},{9,... | collective-permute-start | bytes 589832 | tf_op jit(solution)/shard_map/ppermute | solution.py:446
  65.0 0.0 collective-permute-start.1
  65.0 0.1 collective-permute-start.2
  65.1 2.7 %fetch.1 = (bf16[512,1536]{1,0:T(8,128)(2,1)S(1)}, bf16[512,512]{1,0:T(8,128)(2,1)S(1)}, bf16[512,2048]{1,0:T(8,128)(2,1)S(1)}, bf16[2048,512]{1,0:T(8,128)(2,1)S(1)}) custom-call(bf16[8,24,512]{2,1,0:T(8,128)(2,1)S(1)} %get-tuple-element.23.after.mine, bf16[2,512,1536]{2,1,0:T(8,128)(2,1)} %wq.3, bf16[2,512,512]{2,1,0:T(8,128)(2,1)S(1)} %copy-done, ...), custom_call_target="tpu_custom_call" | custom-call | bytes 25165824 | tf_op jit(solution)/shard_map/fetch/pallas_call | solution.py:206
  67.8 0.0 collective-permute-done.1.right
  67.9 5.2 %collective-permute-done.2.corner = bf16[8,8,512]{2,1,0:T(8,128)(2,1)S(1)} collective-permute-done((bf16[8,8,512]{2,1,0:T(8,128)(2,1)S(1)}, bf16[8,8,512]{2,1,0:T(8,128)(2,1)S(1)}, u32[]{:S(2)}, u32[]{:S(2)}) %collective-permute-start.2) | collective-permute-done | bytes 65568 | tf_op jit(solution)/shard_map/ppermute | solution.py:446
  73.1 1.1 %collective-permute-done.above = bf16[8,24,512]{2,1,0:T(8,128)(2,1)S(1)} collective-permute-done((bf16[8,24,512]{2,1,0:T(8,128)(2,1)S(1)}, bf16[8,24,512]{2,1,0:T(8,128)(2,1)S(1)}, u32[]{:S(2)}, u32[]{:S(2)}) %collective-permute-start) | collective-permute-done | bytes 196640 | tf_op jit(solution)/shard_map/ppermute | solution.py:446
  74.2 4.9 %shift_block.1 = (bf16[8,8,512]{2,1,0:T(8,128)(2,1)S(1)}, bf16[8,24,512]{2,1,0:T(8,128)(2,1)S(1)}, bf16[8,8,512]{2,1,0:T(8,128)(2,1)S(1)}, bf16[8,8,512]{2,1,0:T...) custom-call(s32[1]{0:T(128)} %bitcast.first, ...), custom_call_target="tpu_custom_call" | custom-call | flops 4294967296 | bytes 8388608 | tf_op jit(solution)/shard_map/shift_block/pallas_call | solution.py:387
  79.1 0.3 collective-permute-start.5
  79.4 1.8 %late_block.1 = bf16[8,16,512]{2,1,0:T(8,128)(2,1)S(1)} custom-call(s32[1]{0:T(128)} %bitcast.first, bf16[128,512]{1,0:T(8,128)(2,1)S(1)} %get-tuple-element.33.q, bf16[256,1024]{1,0:T(8,128)(2,1)S(1)} %get-tuple-element.34.kv, bf16[128,512]{1,0:T(8,128)(2,1)S(1)} %get-tuple-element.35.x, f32[2,2,512]{2,1,0:T(2,128)S(1)} %copy-done.1, ...), custom_call_target="tpu_custom_call" | custom-call | flops 1073741824 | bytes 6291456 | tf_op jit(solution)/shard_map/late_block/pallas_call | solution.py:421
  81.2 0.4 collective-permute-start.3
  81.6 1.2 %collective-permute-start.4 = (bf16[8,8,512]{2,1,0:T(8,128)(2,1)S(1)}, bf16[8,8,512]{2,1,0:T(8,128)(2,1)S(1)}, u32[]{:S(2)}, u32[]{:S(2)}) collective-permute-start(bf16[8,8,512]{2,1,0:T(8,128)(2,1)S(1)} %get-tuple-element.39), channel_id=1, source_target_pairs={{0,113},{1,114},{2,115},{3,116},{4,117},{5,118},{6,119},{7,120},{8... | collective-permute-start | bytes 196616 | tf_op jit(solution)/shard_map/ppermute | solution.py:446
  82.7 5.0 %collective-permute-done.3 = bf16[8,8,512]{2,1,0:T(8,128)(2,1)S(1)} collective-permute-done((bf16[8,8,512]{2,1,0:T(8,128)(2,1)S(1)}, bf16[8,8,512]{2,1,0:T(8,128)(2,1)S(1)}, u32[]{:S(2)}, u32[]{:S(2)}) %collective-permute-start.3) | collective-permute-done | bytes 65568 | tf_op jit(solution)/shard_map/ppermute | solution.py:446
  87.7 1.3 %collective-permute-done.4 = bf16[8,8,512]{2,1,0:T(8,128)(2,1)S(1)} collective-permute-done((bf16[8,8,512]{2,1,0:T(8,128)(2,1)S(1)}, bf16[8,8,512]{2,1,0:T(8,128)(2,1)S(1)}, u32[]{:S(2)}, u32[]{:S(2)}) %collective-permute-start.4) | collective-permute-done | bytes 65568 | tf_op jit(solution)/shard_map/ppermute | solution.py:446
  89.0 0.0 collective-permute-done.5
  89.0 0.8 maximum_maximum_fusion
  (1 shorter events, 0.0 us)
Async XLA Ops:
  11.7 44.2 %copy-start = (bf16[2,512,512]{2,1,0:T(8,128)(2,1)S(1)}, bf16[2,512,512]{2,1,0:T(8,128)(2,1)}, u32[]{:S(2)}) copy-start(bf16[2,512,512]{2,1,0:T(8,128)(2,1)} %wp.3) | copy-start | bytes 3145732
  11.7 44.2 %copy-start.1 = (f32[2,2,512]{2,1,0:T(2,128)S(1)}, f32[2,2,512]{2,1,0:T(2,128)}, u32[]{:S(2)}) copy-start(f32[2,2,512]{2,1,0:T(2,128)} %gains.5) | copy-start | bytes 24580
  11.7 44.2 %copy-start.2 = (bf16[16,32,512]{2,1,0:T(8,128)(2,1)S(1)}, bf16[16,32,512]{2,1,0:T(8,128)(2,1)}, u32[]{:S(2)}) copy-start(bf16[16,32,512]{2,1,0:T(8,128)(2,1)} %background.1) | copy-start | bytes 1572868
  64.1 10.2 %collective-permute-start = (bf16[8,24,512]{2,1,0:T(8,128)(2,1)S(1)}, bf16[8,24,512]{2,1,0:T(8,128)(2,1)S(1)}, u32[]{:S(2)}, u32[]{:S(2)}) collective-permute-start(bf16[8,24,512]{2,1,0:T(8,128)(2,1)S(1)} %get-tuple-element.24), channel_id=1, source_target_pairs={{0,16},{1,17},{2,18},{3,19},{4,20},{5,21},{6,22},{7,23},{8,24},{9,... | collective-permute-start | bytes 589832 | tf_op jit(solution)/shard_map/ppermute | solution.py:446
  65.0 2.9 %collective-permute-start.1 = (bf16[8,8,512]{2,1,0:T(8,128)(2,1)S(1)}, bf16[8,8,512]{2,1,0:T(8,128)(2,1)S(1)}, u32[]{:S(2)}, u32[]{:S(2)}) collective-permute-start(bf16[8,8,512]{2,1,0:T(8,128)(2,1)S(1)} %get-tuple-element.25), channel_id=1, source_target_pairs={{0,15},{1,0},{2,1},{3,2},{4,3},{5,4},{6,5},{7,6},{8,7},{9,8},{10,9... | collective-permute-start | bytes 196616 | tf_op jit(solution)/shard_map/ppermute | solution.py:446
  65.0 8.1 %collective-permute-start.2 = (bf16[8,8,512]{2,1,0:T(8,128)(2,1)S(1)}, bf16[8,8,512]{2,1,0:T(8,128)(2,1)S(1)}, u32[]{:S(2)}, u32[]{:S(2)}) collective-permute-start(bf16[8,8,512]{2,1,0:T(8,128)(2,1)S(1)} %get-tuple-element.26), channel_id=1, source_target_pairs={{0,31},{1,16},{2,17},{3,18},{4,19},{5,20},{6,21},{7,22},{8,23},{9,... | collective-permute-start | bytes 196616 | tf_op jit(solution)/shard_map/ppermute | solution.py:446
  79.1 9.9 %collective-permute-start.5 = (bf16[8,24,512]{2,1,0:T(8,128)(2,1)S(1)}, bf16[8,24,512]{2,1,0:T(8,128)(2,1)S(1)}, u32[]{:S(2)}, u32[]{:S(2)}) collective-permute-start(bf16[8,24,512]{2,1,0:T(8,128)(2,1)S(1)} %get-tuple-element.40), channel_id=1, source_target_pairs={{0,112},{1,113},{2,114},{3,115},{4,116},{5,117},{6,118},{7,119},{8... | collective-permute-start | bytes 589832 | tf_op jit(solution)/shard_map/ppermute | solution.py:446
  81.2 6.5 %collective-permute-start.3 = (bf16[8,8,512]{2,1,0:T(8,128)(2,1)S(1)}, bf16[8,8,512]{2,1,0:T(8,128)(2,1)S(1)}, u32[]{:S(2)}, u32[]{:S(2)}) collective-permute-start(bf16[8,8,512]{2,1,0:T(8,128)(2,1)S(1)} %get-tuple-element.36), channel_id=1, source_target_pairs={{0,1},{1,2},{2,3},{3,4},{4,5},{5,6},{6,7},{7,8},{8,9},{9,10},{10,1... | collective-permute-start | bytes 196616 | tf_op jit(solution)/shard_map/ppermute | solution.py:446
  81.6 7.5 %collective-permute-start.4 = (bf16[8,8,512]{2,1,0:T(8,128)(2,1)S(1)}, bf16[8,8,512]{2,1,0:T(8,128)(2,1)S(1)}, u32[]{:S(2)}, u32[]{:S(2)}) collective-permute-start(bf16[8,8,512]{2,1,0:T(8,128)(2,1)S(1)} %get-tuple-element.39), channel_id=1, source_target_pairs={{0,113},{1,114},{2,115},{3,116},{4,117},{5,118},{6,119},{7,120},{8... | collective-permute-start | bytes 196616 | tf_op jit(solution)/shard_map/ppermute | solution.py:446

commit v8 on v7

--- a/solution.py
+++ b/solution.py
@@ -23,7 +23,8 @@
 BLK = 256
 TILE = 1024
 ENC_TILES = (1024, 1024)
-AHEAD = 5
+AHEAD = 3
+ROUTE = 512
 ENC = 1024
 PUT = 1024
 EPS = 1e-5
@@ -66,8 +67,8 @@
 
 
 def encode_kernel(
-    place, count, dest, token, rows_hbm, w_in_hbm, w_out_hbm, slab_hbm,
-    rows, w_in, w_out, slab, encoded, total, slots, in_sems, out_sems,
+    place, count, dest_hbm, token_hbm, rows_hbm, w_in_hbm, w_out_hbm, slab_hbm,
+    dest, token, rows, w_in, w_out, slab, encoded, total, slots, in_sems, out_sems, index_sems,
 ):
     copies = [pltpu.make_async_copy(rows_hbm, rows, in_sems.at[0])]
     spans = []
@@ -76,7 +77,11 @@
         spans.append(f)
         copies.append(pltpu.make_async_copy(w_in_hbm.at[:, f], w_in.at[:, f], in_sems.at[2 * t + 1]))
         copies.append(pltpu.make_async_copy(w_out_hbm.at[f, :], w_out.at[f, :], in_sems.at[2 * t + 2]))
-    for copy in copies[:AHEAD]:
+    index_copies = [
+        pltpu.make_async_copy(dest_hbm, dest, index_sems.at[0]),
+        pltpu.make_async_copy(token_hbm, token, index_sems.at[1]),
+    ]
+    for copy in index_copies + copies[:AHEAD]:
         copy.start()
 
     def arrive(i):
@@ -86,18 +91,20 @@
 
     live_count = count[0]
     lane_base = (place[0] % 8) * CAP
-    before = iota((BLK, BLK), 0) < iota((BLK, BLK), 1)
+    before = iota((ROUTE, ROUTE), 0) < iota((ROUTE, ROUTE), 1)
     upper = jnp.where(before, 1.0, 0.0).astype(BF)
-    owner_col = iota((OWNERS, BLK), 0)
-    lane_col = iota((LANES, BLK), 0)
+    owner_col = iota((OWNERS, ROUTE), 0)
+    lane_col = iota((LANES, ROUTE), 0)
+    for copy in index_copies:
+        copy.wait()
     carry = jnp.zeros((OWNERS, 1), F32)
     high = jnp.zeros((OWNERS, LANES), F32)
     low = jnp.zeros((OWNERS, LANES), F32)
-    for b in range(OBS_DEV // BLK):
-        cols = slice(b * BLK, (b + 1) * BLK)
+    for b in range(OBS_DEV // ROUTE):
+        cols = slice(b * ROUTE, (b + 1) * ROUTE)
         owner = dest[:, cols]
         target = owner % N_LON * N_LAT + owner // N_LON
-        live = (iota((1, BLK), 1) + b * BLK) < live_count
+        live = (iota((1, ROUTE), 1) + b * ROUTE) < live_count
         hits = jnp.where((owner_col == target) & live, 1.0, 0.0)
         hits_bf = hits.astype(BF)
         earlier = dot(hits_bf, upper) + carry
@@ -156,9 +163,11 @@
     return pl.pallas_call(
         encode_kernel,
         out_shape=jax.ShapeDtypeStruct((OWNERS, SLAB, LANES), BF),
-        in_specs=[SMEM, SMEM, VMEM, VMEM, HBM, HBM, HBM],
+        in_specs=[SMEM, SMEM, HBM, HBM, HBM, HBM, HBM],
         out_specs=HBM,
         scratch_shapes=[
+            pltpu.VMEM((1, OBS_DEV), jnp.int32),
+            pltpu.VMEM((1, OBS_DEV), jnp.int32),
             pltpu.VMEM((OBS_DEV, D), BF),
             pltpu.VMEM((D, FF), BF),
             pltpu.VMEM((FF, D), BF),
@@ -168,6 +177,7 @@
             pltpu.VMEM((1, OBS_DEV), jnp.int32),
             pltpu.SemaphoreType.DMA((2 * len(ENC_TILES) + 1,)),
             pltpu.SemaphoreType.DMA((OWNERS * CAP // PUT,)),
+            pltpu.SemaphoreType.DMA((2,)),
         ],
         compiler_params=pltpu.CompilerParams(vmem_limit_bytes=ENCODE_VMEM),
         cost_estimate=pl.CostEstimate(
@@ -432,6 +442,36 @@
     )(first, q, kv, x, gains, *weights)
 
 
+def place_kernel(left, mid, edge, corner, below, out, sems):
+    low = CLON - HALF
+    spots = (
+        (left, slice(0, HALF), slice(0, HALF)),
+        (mid, slice(0, HALF), slice(HALF, low)),
+        (edge, slice(0, HALF), slice(low, CLON)),
+        (corner, slice(HALF, CLAT), slice(0, HALF)),
+        (below, slice(HALF, CLAT), slice(HALF, CLON)),
+    )
+    copies = []
+    for i, (piece, rows, cols) in enumerate(spots):
+        copies.append(pltpu.make_async_copy(piece, out.at[rows, cols, :], sems.at[i]))
+        copies[-1].start()
+    for copy in copies:
+        copy.wait()
+
+
+def assemble(*pieces):
+    return pl.pallas_call(
+        place_kernel,
+        out_shape=jax.ShapeDtypeStruct((CLAT, CLON, D), BF),
+        in_specs=[VMEM] * 5,
+        out_specs=HBM,
+        scratch_shapes=[pltpu.SemaphoreType.DMA((5,))],
+        compiler_params=pltpu.CompilerParams(vmem_limit_bytes=LATE_VMEM),
+        cost_estimate=pl.CostEstimate(flops=0, transcendentals=0, bytes_accessed=1 << 20),
+        name="assemble",
+    )(*pieces)
+
+
 def moved(block, lat_step, lon_step):
     lat_count = lax.axis_size("lat")
     lon_count = lax.axis_size("lon")
@@ -487,9 +527,7 @@
     left, corner, mid = lax.optimization_barrier((left, corner, mid))
     left = moved(left, 0, 1)
     corner = moved(corner, -1, 1)
-    top = jnp.concatenate([left, mid, edge], 1)
-    bottom = jnp.concatenate([corner, below], 1)
-    return jnp.concatenate([top, bottom], 0)
+    return assemble(left, mid, edge, corner, below)
 
 
 def solution(mesh):

time: 90.1 us -> 89.7 us (level)
  no operation moved by 1% of the time
where the time goes in v8:
time: 89.7 us; the launch traced here: 89.6 us
  blocking collectives  44.1 us (49%)
  Pallas kernels  29 us (32%)
  waiting for transfers between devices  12.7 us (14%)
  starting transfers between devices  2.84 us (3%)
    all_to_all x1, blocking collectives, on_device(): lax.all_to_all(slab, ('lon', 'lat'), split_axis=0, concat_axis=0, tiled=T...  44.1 us
    ppermute x6, waiting for transfers between devices, moved(): return lax.ppermute(block, ('lat', 'lon'), route)  12.7 us
    pallas_call x1, Pallas kernels, encode(): pl.pallas_call(encode_kernel, out_shape=jax.ShapeDtypeStruct((OWNERS, SLA...  10.6 us
    pallas_call x1, Pallas kernels, bin_block(): pl.pallas_call(bin_kernel, out_shape=PIECES, in_specs=[VMEM] * 3 + [HBM]...  8.22 us
    pallas_call x1, Pallas kernels, shift_block(): pl.pallas_call(shift_kernel, out_shape=(NARROW, WIDE, NARROW, NARROW, jax...  4.87 us
    ppermute x6, starting transfers between devices, moved(): return lax.ppermute(block, ('lat', 'lon'), route)  2.84 us
    pallas_call x1, Pallas kernels, fetch(): pl.pallas_call(fetch_kernel, out_shape=[jax.ShapeDtypeStruct(a.shape[1:],...  2.75 us
    pallas_call x1, Pallas kernels, late_block(): pl.pallas_call(late_kernel, out_shape=jax.ShapeDtypeStruct((HALF, WIN, D)...  1.83 us
  transfers between devices with their start and end apart: 6, of which 4 were waited for; matrix products, arithmetic and copies ran while one was open for 0% of the time, Pallas kernels for 5%

profile of v8, /device:TPU:0, one launch (start us, length us, event | category | flops | bytes accessed | tf_op | source)
XLA Modules:
  0.0 89.6 jit_solution(12541305407950407558)
XLA Ops:
  0.7 10.6 %encode.1 = bf16[128,72,128]{2,1,0:T(8,128)(2,1)} custom-call(s32[1]{0:T(128)} %bitcast.1.place, s32[1]{0:T(128)S(6)} %copy.13.count, s32[1,1024]{1,0:T(1,128)} %bitcast.4, s32[1,1024]{1,0:T(1,128)} %bitcast.5, bf16[1024,512]{1,0:T(8,128)(2,1)} %rows_hbm.1, bf16[512,2048]{1,0:T(8,128)(2,1)} %w_in_hbm.1, bf16[2048,512]{1,0:T(8,128)(2,1)} %w_out_hbm.1), custom_call_target="tpu_custom_call" | custom-call | flops 7516192768 | bytes 8388608 | tf_op jit(solution)/shard_map/encode/pallas_call | solution.py:163
  11.2 0.0 copy-start
  11.2 0.0 copy-start.1
  11.2 0.0 copy-start.2
  11.2 44.1 %all_to_all.5.arrived = bf16[128,72,128]{2,1,0:T(8,128)(2,1)S(1)} all-to-all(bf16[128,72,128]{2,1,0:T(8,128)(2,1)} %encode.1), channel_id=1, replica_groups=mesh['lat'=8,'lon'=16] {'lon','lat'}, dimensions={0} | all-to-all | bytes 4718592 | tf_op jit(solution)/shard_map/all_to_all | solution.py:514
  55.4 0.0 copy-done
  55.4 0.0 copy-done.2
  55.4 8.2 %bin_block.1 = (bf16[8,24,512]{2,1,0:T(8,128)(2,1)S(1)}, bf16[8,24,512]{2,1,0:T(8,128)(2,1)S(1)}, bf16[8,8,512]{2,1,0:T(8,128)(2,1)S(1)}, bf16[8,8,512]{2,1,0:T(8,128)(2,1)S(1)}) custom-call(bf16[128,72,128]{2,1,0:T(8,128)(2,1)S(1)} %all_to_all.5.arrived, bf16[16,32,512]{2,1,0:T(8,128)(2,1)S(1)} %copy-done.2, f32[2,2,512]{2,1,0:T(2,128)S(1)} %copy-done.1, ...), custom_call_target="tpu_custom_call" | custom-call | flops 4294967296 | bytes 8388608 | tf_op jit(solution)/shard_map/bin_block/pallas_call | solution.py:338
  63.6 0.9 %collective-permute-start = (bf16[8,24,512]{2,1,0:T(8,128)(2,1)S(1)}, bf16[8,24,512]{2,1,0:T(8,128)(2,1)S(1)}, u32[]{:S(2)}, u32[]{:S(2)}) collective-permute-start(bf16[8,24,512]{2,1,0:T(8,128)(2,1)S(1)} %get-tuple-element.24), channel_id=1, source_target_pairs={{0,16},{1,17},{2,18},{3,19},{4,20},{5,21},{6,22},{7,23},{8,24},{9,... | collective-permute-start | bytes 589832 | tf_op jit(solution)/shard_map/ppermute | solution.py:486
  64.5 0.0 collective-permute-start.1
  64.5 0.1 collective-permute-start.2
  64.7 2.7 %fetch.1 = (bf16[512,1536]{1,0:T(8,128)(2,1)S(1)}, bf16[512,512]{1,0:T(8,128)(2,1)S(1)}, bf16[512,2048]{1,0:T(8,128)(2,1)S(1)}, bf16[2048,512]{1,0:T(8,128)(2,1)S(1)}) custom-call(bf16[8,24,512]{2,1,0:T(8,128)(2,1)S(1)} %get-tuple-element.23.after.mine, bf16[2,512,1536]{2,1,0:T(8,128)(2,1)} %wq.3, bf16[2,512,512]{2,1,0:T(8,128)(2,1)S(1)} %copy-done, ...), custom_call_target="tpu_custom_call" | custom-call | bytes 25165824 | tf_op jit(solution)/shard_map/fetch/pallas_call | solution.py:216
  67.4 0.0 collective-permute-done.1.right
  67.4 5.2 %collective-permute-done.2.corner = bf16[8,8,512]{2,1,0:T(8,128)(2,1)S(1)} collective-permute-done((bf16[8,8,512]{2,1,0:T(8,128)(2,1)S(1)}, bf16[8,8,512]{2,1,0:T(8,128)(2,1)S(1)}, u32[]{:S(2)}, u32[]{:S(2)}) %collective-permute-start.2) | collective-permute-done | bytes 65568 | tf_op jit(solution)/shard_map/ppermute | solution.py:486
  72.6 1.1 %collective-permute-done.above = bf16[8,24,512]{2,1,0:T(8,128)(2,1)S(1)} collective-permute-done((bf16[8,24,512]{2,1,0:T(8,128)(2,1)S(1)}, bf16[8,24,512]{2,1,0:T(8,128)(2,1)S(1)}, u32[]{:S(2)}, u32[]{:S(2)}) %collective-permute-start) | collective-permute-done | bytes 196640 | tf_op jit(solution)/shard_map/ppermute | solution.py:486
  73.8 4.9 %shift_block.1 = (bf16[8,8,512]{2,1,0:T(8,128)(2,1)S(1)}, bf16[8,24,512]{2,1,0:T(8,128)(2,1)S(1)}, bf16[8,8,512]{2,1,0:T(8,128)(2,1)S(1)}, bf16[8,8,512]{2,1,0:T...) custom-call(s32[1]{0:T(128)} %bitcast.first, ...), custom_call_target="tpu_custom_call" | custom-call | flops 4294967296 | bytes 8388608 | tf_op jit(solution)/shard_map/shift_block/pallas_call | solution.py:397
  78.7 0.3 collective-permute-start.5
  78.9 1.8 %late_block.1.mid = bf16[8,16,512]{2,1,0:T(8,128)(2,1)S(1)} custom-call(s32[1]{0:T(128)} %bitcast.first, bf16[128,512]{1,0:T(8,128)(2,1)S(1)} %get-tuple-element.33.q, bf16[256,1024]{1,0:T(8,128)(2,1)S(1)} %get-tuple-element.34.kv, bf16[128,512]{1,0:T(8,128)(2,1)S(1)} %get-tuple-element.35.x, f32[2,2,512]{2,1,0:T(2,128)S(1)} %copy-done.1, ...), custom_call_target="tpu_custom_call" | custom-call | flops 1073741824 | bytes 6291456 | tf_op jit(solution)/shard_map/late_block/pallas_call | solution.py:431
  80.8 0.4 collective-permute-start.3
  81.1 1.2 %collective-permute-start.4 = (bf16[8,8,512]{2,1,0:T(8,128)(2,1)S(1)}, bf16[8,8,512]{2,1,0:T(8,128)(2,1)S(1)}, u32[]{:S(2)}, u32[]{:S(2)}) collective-permute-start(bf16[8,8,512]{2,1,0:T(8,128)(2,1)S(1)} %get-tuple-element.39), channel_id=1, source_target_pairs={{0,113},{1,114},{2,115},{3,116},{4,117},{5,118},{6,119},{7,120},{8... | collective-permute-start | bytes 196616 | tf_op jit(solution)/shard_map/ppermute | solution.py:486
  82.3 5.0 %collective-permute-done.3.left = bf16[8,8,512]{2,1,0:T(8,128)(2,1)S(1)} collective-permute-done((bf16[8,8,512]{2,1,0:T(8,128)(2,1)S(1)}, bf16[8,8,512]{2,1,0:T(8,128)(2,1)S(1)}, u32[]{:S(2)}, u32[]{:S(2)}) %collective-permute-start.3) | collective-permute-done | bytes 65568 | tf_op jit(solution)/shard_map/ppermute | solution.py:486
  87.3 1.3 %collective-permute-done.4.corner = bf16[8,8,512]{2,1,0:T(8,128)(2,1)S(1)} collective-permute-done((bf16[8,8,512]{2,1,0:T(8,128)(2,1)S(1)}, bf16[8,8,512]{2,1,0:T(8,128)(2,1)S(1)}, u32[]{:S(2)}, u32[]{:S(2)}) %collective-permute-start.4) | collective-permute-done | bytes 65568 | tf_op jit(solution)/shard_map/ppermute | solution.py:486
  88.6 0.0 collective-permute-done.5.below
  88.6 0.8 assemble.1
  (1 shorter events, 0.0 us)
Async XLA Ops:
  11.2 44.2 %copy-start = (bf16[2,512,512]{2,1,0:T(8,128)(2,1)S(1)}, bf16[2,512,512]{2,1,0:T(8,128)(2,1)}, u32[]{:S(2)}) copy-start(bf16[2,512,512]{2,1,0:T(8,128)(2,1)} %wp.3) | copy-start | bytes 3145732
  11.2 44.2 %copy-start.1 = (f32[2,2,512]{2,1,0:T(2,128)S(1)}, f32[2,2,512]{2,1,0:T(2,128)}, u32[]{:S(2)}) copy-start(f32[2,2,512]{2,1,0:T(2,128)} %gains.5) | copy-start | bytes 24580
  11.2 44.2 %copy-start.2 = (bf16[16,32,512]{2,1,0:T(8,128)(2,1)S(1)}, bf16[16,32,512]{2,1,0:T(8,128)(2,1)}, u32[]{:S(2)}) copy-start(bf16[16,32,512]{2,1,0:T(8,128)(2,1)} %background.1) | copy-start | bytes 1572868
  63.6 10.2 %collective-permute-start = (bf16[8,24,512]{2,1,0:T(8,128)(2,1)S(1)}, bf16[8,24,512]{2,1,0:T(8,128)(2,1)S(1)}, u32[]{:S(2)}, u32[]{:S(2)}) collective-permute-start(bf16[8,24,512]{2,1,0:T(8,128)(2,1)S(1)} %get-tuple-element.24), channel_id=1, source_target_pairs={{0,16},{1,17},{2,18},{3,19},{4,20},{5,21},{6,22},{7,23},{8,24},{9,... | collective-permute-start | bytes 589832 | tf_op jit(solution)/shard_map/ppermute | solution.py:486
  64.5 2.9 %collective-permute-start.1 = (bf16[8,8,512]{2,1,0:T(8,128)(2,1)S(1)}, bf16[8,8,512]{2,1,0:T(8,128)(2,1)S(1)}, u32[]{:S(2)}, u32[]{:S(2)}) collective-permute-start(bf16[8,8,512]{2,1,0:T(8,128)(2,1)S(1)} %get-tuple-element.25), channel_id=1, source_target_pairs={{0,15},{1,0},{2,1},{3,2},{4,3},{5,4},{6,5},{7,6},{8,7},{9,8},{10,9... | collective-permute-start | bytes 196616 | tf_op jit(solution)/shard_map/ppermute | solution.py:486
  64.5 8.1 %collective-permute-start.2 = (bf16[8,8,512]{2,1,0:T(8,128)(2,1)S(1)}, bf16[8,8,512]{2,1,0:T(8,128)(2,1)S(1)}, u32[]{:S(2)}, u32[]{:S(2)}) collective-permute-start(bf16[8,8,512]{2,1,0:T(8,128)(2,1)S(1)} %get-tuple-element.26), channel_id=1, source_target_pairs={{0,31},{1,16},{2,17},{3,18},{4,19},{5,20},{6,21},{7,22},{8,23},{9,... | collective-permute-start | bytes 196616 | tf_op jit(solution)/shard_map/ppermute | solution.py:486
  78.7 9.9 %collective-permute-start.5 = (bf16[8,24,512]{2,1,0:T(8,128)(2,1)S(1)}, bf16[8,24,512]{2,1,0:T(8,128)(2,1)S(1)}, u32[]{:S(2)}, u32[]{:S(2)}) collective-permute-start(bf16[8,24,512]{2,1,0:T(8,128)(2,1)S(1)} %get-tuple-element.40), channel_id=1, source_target_pairs={{0,112},{1,113},{2,114},{3,115},{4,116},{5,117},{6,118},{7,119},{8... | collective-permute-start | bytes 589832 | tf_op jit(solution)/shard_map/ppermute | solution.py:486
  80.8 6.5 %collective-permute-start.3 = (bf16[8,8,512]{2,1,0:T(8,128)(2,1)S(1)}, bf16[8,8,512]{2,1,0:T(8,128)(2,1)S(1)}, u32[]{:S(2)}, u32[]{:S(2)}) collective-permute-start(bf16[8,8,512]{2,1,0:T(8,128)(2,1)S(1)} %get-tuple-element.36), channel_id=1, source_target_pairs={{0,1},{1,2},{2,3},{3,4},{4,5},{5,6},{6,7},{7,8},{8,9},{9,10},{10,1... | collective-permute-start | bytes 196616 | tf_op jit(solution)/shard_map/ppermute | solution.py:486
  81.1 7.5 %collective-permute-start.4 = (bf16[8,8,512]{2,1,0:T(8,128)(2,1)S(1)}, bf16[8,8,512]{2,1,0:T(8,128)(2,1)S(1)}, u32[]{:S(2)}, u32[]{:S(2)}) collective-permute-start(bf16[8,8,512]{2,1,0:T(8,128)(2,1)S(1)} %get-tuple-element.39), channel_id=1, source_target_pairs={{0,113},{1,114},{2,115},{3,116},{4,117},{5,118},{6,119},{7,120},{8... | collective-permute-start | bytes 196616 | tf_op jit(solution)/shard_map/ppermute | solution.py:486

commit v9 on v8

--- a/solution.py
+++ b/solution.py
@@ -21,7 +21,7 @@
 LANES = 128
 SLAB = 4 * CAP + 8
 BLK = 256
-TILE = 1024
+TILE = 2048
 ENC_TILES = (1024, 1024)
 AHEAD = 3
 ROUTE = 512

time: 89.7 us -> 89.6 us (level)
  no operation moved by 1% of the time
where the time goes in v9:
time: 89.6 us; the launch traced here: 89.4 us
  blocking collectives  44.1 us (49%)
  Pallas kernels  28.8 us (32%)
  waiting for transfers between devices  12.7 us (14%)
  starting transfers between devices  2.85 us (3%)
    all_to_all x1, blocking collectives, on_device(): lax.all_to_all(slab, ('lon', 'lat'), split_axis=0, concat_axis=0, tiled=T...  44.1 us
    ppermute x6, waiting for transfers between devices, moved(): return lax.ppermute(block, ('lat', 'lon'), route)  12.7 us
    pallas_call x1, Pallas kernels, encode(): pl.pallas_call(encode_kernel, out_shape=jax.ShapeDtypeStruct((OWNERS, SLA...  10.6 us
    pallas_call x1, Pallas kernels, bin_block(): pl.pallas_call(bin_kernel, out_shape=PIECES, in_specs=[VMEM] * 3 + [HBM]...  8.09 us
    pallas_call x1, Pallas kernels, shift_block(): pl.pallas_call(shift_kernel, out_shape=(NARROW, WIDE, NARROW, NARROW, jax...  4.86 us
    ppermute x6, starting transfers between devices, moved(): return lax.ppermute(block, ('lat', 'lon'), route)  2.85 us
    pallas_call x1, Pallas kernels, fetch(): pl.pallas_call(fetch_kernel, out_shape=[jax.ShapeDtypeStruct(a.shape[1:],...  2.75 us
  transfers between devices with their start and end apart: 6, of which 4 were waited for; matrix products, arithmetic and copies ran while one was open for 0% of the time, Pallas kernels for 5%

profile of v9, /device:TPU:0, one launch (start us, length us, event | category | flops | bytes accessed | tf_op | source)
XLA Modules:
  0.0 89.4 jit_solution(13769637519168787411)
XLA Ops:
  0.7 10.6 %encode.1 = bf16[128,72,128]{2,1,0:T(8,128)(2,1)} custom-call(s32[1]{0:T(128)} %bitcast.1.place, s32[1]{0:T(128)S(6)} %copy.13.count, s32[1,1024]{1,0:T(1,128)} %bitcast.4, s32[1,1024]{1,0:T(1,128)} %bitcast.5, bf16[1024,512]{1,0:T(8,128)(2,1)} %rows_hbm.1, bf16[512,2048]{1,0:T(8,128)(2,1)} %w_in_hbm.1, bf16[2048,512]{1,0:T(8,128)(2,1)} %w_out_hbm.1), custom_call_target="tpu_custom_call" | custom-call | flops 7516192768 | bytes 8388608 | tf_op jit(solution)/shard_map/encode/pallas_call | solution.py:163
  11.2 0.0 copy-start
  11.2 0.0 copy-start.1
  11.2 0.0 copy-start.2
  11.2 44.1 %all_to_all.5.arrived = bf16[128,72,128]{2,1,0:T(8,128)(2,1)S(1)} all-to-all(bf16[128,72,128]{2,1,0:T(8,128)(2,1)} %encode.1), channel_id=1, replica_groups=mesh['lat'=8,'lon'=16] {'lon','lat'}, dimensions={0} | all-to-all | bytes 4718592 | tf_op jit(solution)/shard_map/all_to_all | solution.py:514
  55.4 0.0 copy-done
  55.4 0.0 copy-done.1
  55.4 8.1 %bin_block.1 = (bf16[8,24,512]{2,1,0:T(8,128)(2,1)S(1)}, bf16[8,24,512]{2,1,0:T(8,128)(2,1)S(1)}, bf16[8,8,512]{2,1,0:T(8,128)(2,1)S(1)}, bf16[8,8,512]{2,1,0:T(8,128)(2,1)S(1)}) custom-call(bf16[128,72,128]{2,1,0:T(8,128)(2,1)S(1)} %all_to_all.5.arrived, bf16[16,32,512]{2,1,0:T(8,128)(2,1)S(1)} %copy-done.2, f32[2,2,512]{2,1,0:T(2,128)S(1)} %copy-done.1, ...), custom_call_target="tpu_custom_call" | custom-call | flops 4294967296 | bytes 8388608 | tf_op jit(solution)/shard_map/bin_block/pallas_call | solution.py:338
  63.5 0.9 %collective-permute-start = (bf16[8,24,512]{2,1,0:T(8,128)(2,1)S(1)}, bf16[8,24,512]{2,1,0:T(8,128)(2,1)S(1)}, u32[]{:S(2)}, u32[]{:S(2)}) collective-permute-start(bf16[8,24,512]{2,1,0:T(8,128)(2,1)S(1)} %get-tuple-element.24), channel_id=1, source_target_pairs={{0,16},{1,17},{2,18},{3,19},{4,20},{5,21},{6,22},{7,23},{8,24},{9,... | collective-permute-start | bytes 589832 | tf_op jit(solution)/shard_map/ppermute | solution.py:486
  64.4 0.0 collective-permute-start.1
  64.4 0.1 collective-permute-start.2
  64.5 2.7 %fetch.1 = (bf16[512,1536]{1,0:T(8,128)(2,1)S(1)}, bf16[512,512]{1,0:T(8,128)(2,1)S(1)}, bf16[512,2048]{1,0:T(8,128)(2,1)S(1)}, bf16[2048,512]{1,0:T(8,128)(2,1)S(1)}) custom-call(bf16[8,24,512]{2,1,0:T(8,128)(2,1)S(1)} %get-tuple-element.23.after.mine, bf16[2,512,1536]{2,1,0:T(8,128)(2,1)} %wq.3, bf16[2,512,512]{2,1,0:T(8,128)(2,1)S(1)} %copy-done, ...), custom_call_target="tpu_custom_call" | custom-call | bytes 25165824 | tf_op jit(solution)/shard_map/fetch/pallas_call | solution.py:216
  67.3 0.0 collective-permute-done.1.right
  67.3 5.2 %collective-permute-done.2.corner = bf16[8,8,512]{2,1,0:T(8,128)(2,1)S(1)} collective-permute-done((bf16[8,8,512]{2,1,0:T(8,128)(2,1)S(1)}, bf16[8,8,512]{2,1,0:T(8,128)(2,1)S(1)}, u32[]{:S(2)}, u32[]{:S(2)}) %collective-permute-start.2) | collective-permute-done | bytes 65568 | tf_op jit(solution)/shard_map/ppermute | solution.py:486
  72.5 1.1 %collective-permute-done.above = bf16[8,24,512]{2,1,0:T(8,128)(2,1)S(1)} collective-permute-done((bf16[8,24,512]{2,1,0:T(8,128)(2,1)S(1)}, bf16[8,24,512]{2,1,0:T(8,128)(2,1)S(1)}, u32[]{:S(2)}, u32[]{:S(2)}) %collective-permute-start) | collective-permute-done | bytes 196640 | tf_op jit(solution)/shard_map/ppermute | solution.py:486
  73.6 4.9 %shift_block.1 = (bf16[8,8,512]{2,1,0:T(8,128)(2,1)S(1)}, bf16[8,24,512]{2,1,0:T(8,128)(2,1)S(1)}, bf16[8,8,512]{2,1,0:T(8,128)(2,1)S(1)}, bf16[8,8,512]{2,1,0:T...) custom-call(s32[1]{0:T(128)} %bitcast.first, ...), custom_call_target="tpu_custom_call" | custom-call | flops 4294967296 | bytes 8388608 | tf_op jit(solution)/shard_map/shift_block/pallas_call | solution.py:397
  78.5 0.3 collective-permute-start.5
  78.8 1.8 %late_block.1.mid = bf16[8,16,512]{2,1,0:T(8,128)(2,1)S(1)} custom-call(s32[1]{0:T(128)} %bitcast.first, bf16[128,512]{1,0:T(8,128)(2,1)S(1)} %get-tuple-element.33.q, bf16[256,1024]{1,0:T(8,128)(2,1)S(1)} %get-tuple-element.34.kv, bf16[128,512]{1,0:T(8,128)(2,1)S(1)} %get-tuple-element.35.x, f32[2,2,512]{2,1,0:T(2,128)S(1)} %copy-done.1, ...), custom_call_target="tpu_custom_call" | custom-call | flops 1073741824 | bytes 6291456 | tf_op jit(solution)/shard_map/late_block/pallas_call | solution.py:431
  80.6 0.4 collective-permute-start.3
  80.9 1.2 %collective-permute-start.4 = (bf16[8,8,512]{2,1,0:T(8,128)(2,1)S(1)}, bf16[8,8,512]{2,1,0:T(8,128)(2,1)S(1)}, u32[]{:S(2)}, u32[]{:S(2)}) collective-permute-start(bf16[8,8,512]{2,1,0:T(8,128)(2,1)S(1)} %get-tuple-element.39), channel_id=1, source_target_pairs={{0,113},{1,114},{2,115},{3,116},{4,117},{5,118},{6,119},{7,120},{8... | collective-permute-start | bytes 196616 | tf_op jit(solution)/shard_map/ppermute | solution.py:486
  82.1 5.1 %collective-permute-done.3.left = bf16[8,8,512]{2,1,0:T(8,128)(2,1)S(1)} collective-permute-done((bf16[8,8,512]{2,1,0:T(8,128)(2,1)S(1)}, bf16[8,8,512]{2,1,0:T(8,128)(2,1)S(1)}, u32[]{:S(2)}, u32[]{:S(2)}) %collective-permute-start.3) | collective-permute-done | bytes 65568 | tf_op jit(solution)/shard_map/ppermute | solution.py:486
  87.2 1.2 %collective-permute-done.4.corner = bf16[8,8,512]{2,1,0:T(8,128)(2,1)S(1)} collective-permute-done((bf16[8,8,512]{2,1,0:T(8,128)(2,1)S(1)}, bf16[8,8,512]{2,1,0:T(8,128)(2,1)S(1)}, u32[]{:S(2)}, u32[]{:S(2)}) %collective-permute-start.4) | collective-permute-done | bytes 65568 | tf_op jit(solution)/shard_map/ppermute | solution.py:486
  88.4 0.0 collective-permute-done.5.below
  88.4 0.8 assemble.1
  (1 shorter events, 0.0 us)
Async XLA Ops:
  11.2 44.2 %copy-start = (bf16[2,512,512]{2,1,0:T(8,128)(2,1)S(1)}, bf16[2,512,512]{2,1,0:T(8,128)(2,1)}, u32[]{:S(2)}) copy-start(bf16[2,512,512]{2,1,0:T(8,128)(2,1)} %wp.3) | copy-start | bytes 3145732
  11.2 44.2 %copy-start.1 = (f32[2,2,512]{2,1,0:T(2,128)S(1)}, f32[2,2,512]{2,1,0:T(2,128)}, u32[]{:S(2)}) copy-start(f32[2,2,512]{2,1,0:T(2,128)} %gains.5) | copy-start | bytes 24580
  11.2 44.2 %copy-start.2 = (bf16[16,32,512]{2,1,0:T(8,128)(2,1)S(1)}, bf16[16,32,512]{2,1,0:T(8,128)(2,1)}, u32[]{:S(2)}) copy-start(bf16[16,32,512]{2,1,0:T(8,128)(2,1)} %background.1) | copy-start | bytes 1572868
  63.5 10.2 %collective-permute-start = (bf16[8,24,512]{2,1,0:T(8,128)(2,1)S(1)}, bf16[8,24,512]{2,1,0:T(8,128)(2,1)S(1)}, u32[]{:S(2)}, u32[]{:S(2)}) collective-permute-start(bf16[8,24,512]{2,1,0:T(8,128)(2,1)S(1)} %get-tuple-element.24), channel_id=1, source_target_pairs={{0,16},{1,17},{2,18},{3,19},{4,20},{5,21},{6,22},{7,23},{8,24},{9,... | collective-permute-start | bytes 589832 | tf_op jit(solution)/shard_map/ppermute | solution.py:486
  64.4 2.9 %collective-permute-start.1 = (bf16[8,8,512]{2,1,0:T(8,128)(2,1)S(1)}, bf16[8,8,512]{2,1,0:T(8,128)(2,1)S(1)}, u32[]{:S(2)}, u32[]{:S(2)}) collective-permute-start(bf16[8,8,512]{2,1,0:T(8,128)(2,1)S(1)} %get-tuple-element.25), channel_id=1, source_target_pairs={{0,15},{1,0},{2,1},{3,2},{4,3},{5,4},{6,5},{7,6},{8,7},{9,8},{10,9... | collective-permute-start | bytes 196616 | tf_op jit(solution)/shard_map/ppermute | solution.py:486
  64.4 8.1 %collective-permute-start.2 = (bf16[8,8,512]{2,1,0:T(8,128)(2,1)S(1)}, bf16[8,8,512]{2,1,0:T(8,128)(2,1)S(1)}, u32[]{:S(2)}, u32[]{:S(2)}) collective-permute-start(bf16[8,8,512]{2,1,0:T(8,128)(2,1)S(1)} %get-tuple-element.26), channel_id=1, source_target_pairs={{0,31},{1,16},{2,17},{3,18},{4,19},{5,20},{6,21},{7,22},{8,23},{9,... | collective-permute-start | bytes 196616 | tf_op jit(solution)/shard_map/ppermute | solution.py:486
  78.5 9.9 %collective-permute-start.5 = (bf16[8,24,512]{2,1,0:T(8,128)(2,1)S(1)}, bf16[8,24,512]{2,1,0:T(8,128)(2,1)S(1)}, u32[]{:S(2)}, u32[]{:S(2)}) collective-permute-start(bf16[8,24,512]{2,1,0:T(8,128)(2,1)S(1)} %get-tuple-element.40), channel_id=1, source_target_pairs={{0,112},{1,113},{2,114},{3,115},{4,116},{5,117},{6,118},{7,119},{8... | collective-permute-start | bytes 589832 | tf_op jit(solution)/shard_map/ppermute | solution.py:486
  80.6 6.6 %collective-permute-start.3 = (bf16[8,8,512]{2,1,0:T(8,128)(2,1)S(1)}, bf16[8,8,512]{2,1,0:T(8,128)(2,1)S(1)}, u32[]{:S(2)}, u32[]{:S(2)}) collective-permute-start(bf16[8,8,512]{2,1,0:T(8,128)(2,1)S(1)} %get-tuple-element.36), channel_id=1, source_target_pairs={{0,1},{1,2},{2,3},{3,4},{4,5},{5,6},{6,7},{7,8},{8,9},{9,10},{10,1... | collective-permute-start | bytes 196616 | tf_op jit(solution)/shard_map/ppermute | solution.py:486
  80.9 7.5 %collective-permute-start.4 = (bf16[8,8,512]{2,1,0:T(8,128)(2,1)S(1)}, bf16[8,8,512]{2,1,0:T(8,128)(2,1)S(1)}, u32[]{:S(2)}, u32[]{:S(2)}) collective-permute-start(bf16[8,8,512]{2,1,0:T(8,128)(2,1)S(1)} %get-tuple-element.39), channel_id=1, source_target_pairs={{0,113},{1,114},{2,115},{3,116},{4,117},{5,118},{6,119},{7,120},{8... | collective-permute-start | bytes 196616 | tf_op jit(solution)/shard_map/ppermute | solution.py:486
